TPU v7x, 256 devices: a whole 4x4x8 slice. The times are simulated.
256 devices in a mesh: row: 64 (over z, x, core), col: 4 (over y).
Axes of the slice: x: 4, y: 4, z: 8, core: 2. Of those that a mesh axis runs over, the one named last changes fastest.
Arguments:
- eigen_vectors: float32 [65536, 2048], P('row', 'col'), may hold values from -6 to 6
- panel_first: float32 [65536, 512], P('row', 'col'), may hold values from -0.0234375 to 0.0234375
- panel_second: float32 [65536, 512], P('row', 'col'), may hold values from -0.0234375 to 0.0234375
- factor_first: float32 [512, 512], replicated, as said below
- factor_second: float32 [512, 512], replicated, as said below
Outputs:
- transformed: float32 [65536, 2048], P('row', 'col')
Inputs may be any that keep to these rules, and one draw needn't show every extreme that they name: factor_first is upper triangular. factor_second is upper triangular.
All inputs are finite; a program needn't handle non-finite values.
Results may differ from a plain program's by a relative error of at most 0.0001.
Values sent between devices are 32-bit elements; how exact they have to be, the bound alone decides.
A program may use at most 64 MiB of HBM per device.

v0:
```python
import jax
import jax.numpy as jnp
from jax import lax
from jax.sharding import PartitionSpec as P


def local_dot(left, right):
    return jnp.dot(left, right, precision=lax.Precision.HIGHEST, preferred_element_type=jnp.float32)


def on_device(eigen_vectors, panel_first, panel_second, factor_first, factor_second):
    vectors_first, vectors_second = (
        lax.all_gather(panel_first, "col", axis=1, tiled=True),
        lax.all_gather(panel_second, "col", axis=1, tiled=True),
    )
    updated = eigen_vectors
    for vectors, factor in ((vectors_second, factor_second), (vectors_first, factor_first)):
        projected = lax.psum(local_dot(vectors.T, updated), "row")
        updated = updated - local_dot(vectors, local_dot(factor, projected))
    return updated


def solution(mesh):
    return jax.shard_map(
        on_device,
        mesh=mesh,
        in_specs=(P("row", "col"), P("row", "col"), P("row", "col"), P(), P()),
        out_specs=P("row", "col"),
        check_vma=False,
    )
```

profile of v0, /device:TPU:1, one launch (start us, length us, event | category | flops | bytes accessed | tf_op | source)
XLA Modules:
  0.0 489.2 jit_solution(13519576373823585658)
XLA Ops:
  6.5 0.0 copy-start
  6.5 0.0 all-gather.3.cloned.1.call-start
  6.5 0.7 all-gather.3.cloned.1.call-update
  7.3 0.0 all-reduce.3.cloned.1.call-start
  7.3 41.9 %all-gather.3.cloned.1.call-done = f32[1024,512]{1,0:T(8,128)} async-done(((f32[1024,128]{1,0:T(8,128)}), f32[1024,512]{1,0:T(8,128)}) %all-gather.3.cloned.1.call-update) | async-done | bytes 2097168 | tf_op jit(solution)/shard_map/all_gather | solution.py:14
  49.2 0.0 copy-start.3
  49.2 6.9 %fusion = f32[512,512]{1,0:T(8,128)} fusion(f32[1024,512]{1,0:T(8,128)} %all-gather.3.cloned.1.call-done, f32[1024,512]{1,0:T(8,128)} %param.5), kind=kOutput, calls=%fused_computation.3 | convolution fusion | flops 3221225472 | bytes 5242880 | tf_op jit(solution)/shard_map/dot_general | solution.py:8
  56.1 0.0 all-reduce.3.cloned.1.call-update
  56.1 0.0 all-gather.5.cloned.1.call-start
  56.1 0.7 all-gather.5.cloned.1.call-update
  56.8 0.0 all-reduce.5.cloned.1.call-start
  56.9 0.0 copy-done.3
  56.9 1.8 copy.6
  58.7 183.2 %all-reduce.3.cloned.1.call-done = f32[512,512]{1,0:T(8,128)} async-done(((f32[512,512]{1,0:T(8,128)}), f32[512,512]{1,0:T(8,128)}) %all-reduce.3.cloned.1.call-update) | async-done | bytes 1048592 | tf_op jit(solution)/shard_map/psum | solution.py:18
  241.9 0.0 copy-done
  241.9 0.0 copy-start.1
  241.9 4.8 fusion.1
  246.7 0.0 copy-done.1
  246.7 5.2 %bitcast_subtract_fusion.1 = f32[1024,512]{0,1:T(8,128)S(1)} fusion(f32[1024,512]{0,1:T(8,128)} %copy.6, f32[512,512]{1,0:T(8,128)S(1)} %fusion.1, f32[1024,512]{1,0:T(8,128)S(1)} %copy-done.1), kind=kOutput, calls=%fused_computation.1 | convolution fusion | flops 3221749760 | bytes 7340032 | tf_op jit(solution)/shard_map/dot_general | solution.py:8
  251.9 27.3 %all-gather.5.cloned.1.call-done = f32[1024,512]{1,0:T(8,128)} async-done(((f32[1024,128]{1,0:T(8,128)}), f32[1024,512]{1,0:T(8,128)}) %all-gather.5.cloned.1.call-update) | async-done | bytes 2097168 | tf_op jit(solution)/shard_map/all_gather | solution.py:13
  279.2 6.1 %convolution_bitcast_fusion = f32[512,512]{0,1:T(8,128)} fusion(f32[1024,512]{0,1:T(8,128)S(1)} %bitcast_subtract_fusion.1, f32[1024,512]{1,0:T(8,128)} %all-gather.5.cloned.1.call-done), kind=kOutput, calls=%fused_computation.2 | convolution fusion | flops 3221225472 | bytes 5242880 | tf_op jit(solution)/shard_map/dot_general | solution.py:8
  285.3 0.0 all-reduce.5.cloned.1.call-update
  285.3 185.8 %all-reduce.5.cloned.1.call-done = f32[512,512]{0,1:T(8,128)} async-done(((f32[512,512]{0,1:T(8,128)}), f32[512,512]{0,1:T(8,128)}) %all-reduce.5.cloned.1.call-update) | async-done | bytes 1048592 | tf_op jit(solution)/shard_map/psum | solution.py:18
  471.1 0.0 copy-start.2
  471.1 3.5 fusion.2
  474.7 0.0 copy-done.2
  474.7 5.1 %bitcast_subtract_fusion = f32[1024,512]{0,1:T(8,128)} fusion(f32[1024,512]{0,1:T(8,128)S(1)} %bitcast_subtract_fusion.1, f32[512,512]{1,0:T(8,128)S(1)} %fusion.2, f32[1024,512]{1,0:T(8,128)S(1)} %copy-done.2), kind=kOutput, calls=%fused_computation | convolution fusion | flops 3221749760 | bytes 7340032 | tf_op jit(solution)/shard_map/dot_general | solution.py:8
  479.8 2.9 copy.7
Async XLA Ops:
  6.5 235.3 %copy-start = (f32[512,512]{1,0:T(8,128)S(1)}, f32[512,512]{1,0:T(8,128)}, u32[]{:S(2)}) copy-start(f32[512,512]{1,0:T(8,128)} %param.9) | copy-start | bytes 3145732
  6.5 42.7 %all-gather.3.cloned.1.call-start = ((), (), s32[]{:S(2)}) async-start(), calls=%async_computation | async-start | bytes 2621440 | tf_op jit(solution)/shard_map/all_gather | solution.py:14
  7.3 234.6 %all-reduce.3.cloned.1.call-start = ((), (), s32[]{:S(2)}) async-start(), calls=%async_computation.1 | async-start | bytes 2097152 | tf_op jit(solution)/shard_map/psum | solution.py:18
  49.2 7.7 %copy-start.3 = (f32[1024,512]{1,0:T(8,128)S(1)}, f32[1024,512]{1,0:T(8,128)}, u32[]{:S(2)}) copy-start(f32[1024,512]{1,0:T(8,128)} %param.5) | copy-start | bytes 6291460
  56.1 223.1 %all-gather.5.cloned.1.call-start = ((), (), s32[]{:S(2)}) async-start(), calls=%async_computation.2 | async-start | bytes 2621440 | tf_op jit(solution)/shard_map/all_gather | solution.py:13
  56.8 414.3 %all-reduce.5.cloned.1.call-start = ((), (), s32[]{:S(2)}) async-start(), calls=%async_computation.3 | async-start | bytes 2097152 | tf_op jit(solution)/shard_map/psum | solution.py:18
  241.9 4.9 copy-start.1
  471.1 3.6 copy-start.2
Sparse Core Ops, SparseCore 0:
  9.2 39.9 all-gather.2
  56.2 185.6 all-reduce.2
  243.8 35.3 all-gather.4
  285.4 185.6 all-reduce.4
where the time goes:
time: 490 us; the launch traced here: 489 us
  waiting for transfers between devices  440 us (90%)
  matrix products  31.6 us (6%)
  between operations  13.2 us (3%)
    psum x2, waiting for transfers between devices, on_device(): projected = lax.psum(local_dot(vectors.T, updated), 'row')  369 us
    all_gather x1, waiting for transfers between devices, on_device(): lax.all_gather(panel_second, 'col', axis=1, tiled=True)  41.9 us
    dot_general x6, matrix products, local_dot(): jnp.dot(left, right, precision=lax.Precision.HIGHEST, preferred_element_t...  31.6 us
    all_gather x1, waiting for transfers between devices, on_device(): lax.all_gather(panel_first, 'col', axis=1, tiled=True)  27.3 us
  transfers between devices with their start and end apart: 4, of which 4 were waited for; matrix products, arithmetic and copies ran while one was open for 2% of the time, Pallas kernels for 0%

commit v1 on v0

v1 whole, which is shorter than its diff:
```python
import functools

import jax
import jax.numpy as jnp
from jax import lax
from jax.experimental import pallas as pl
from jax.experimental.pallas import tpu as pltpu
from jax.sharding import PartitionSpec as P


def local_dot(left, right):
    return jnp.dot(left, right, precision=lax.Precision.HIGHEST, preferred_element_type=jnp.float32)


def _allreduce_kernel(n, x_ref, o_ref, recv, rs_send, rs_recv, ag_send, ag_recv):
    me = lax.axis_index("row")
    col = lax.axis_index("col")
    h = x_ref.shape[0] // n
    mesh_id = pl.DeviceIdType.MESH

    def chunk(ref, j):
        return ref.at[pl.ds(pl.multiple_of(j * h, h), h), :]

    def rs_copy(s):
        tgt = lax.rem(me + s, n)
        return pltpu.make_async_remote_copy(
            src_ref=chunk(x_ref, tgt),
            dst_ref=recv.at[s],
            send_sem=rs_send.at[s],
            recv_sem=rs_recv.at[s],
            device_id=(tgt, col),
            device_id_type=mesh_id,
        )

    def ag_copy(s):
        tgt = lax.rem(me + s, n)
        return pltpu.make_async_remote_copy(
            src_ref=chunk(o_ref, me),
            dst_ref=chunk(o_ref, me),
            send_sem=ag_send.at[s],
            recv_sem=ag_recv.at[s],
            device_id=(tgt, col),
            device_id_type=mesh_id,
        )

    @pl.loop(1, n)
    def _(s):
        rs_copy(s).start()

    @pl.loop(1, n)
    def _(s):
        rs_copy(s).wait()

    def add(s, acc):
        return acc + recv[s]

    total = lax.fori_loop(1, n, add, x_ref[pl.ds(pl.multiple_of(me * h, h), h), :])
    o_ref[pl.ds(pl.multiple_of(me * h, h), h), :] = total

    @pl.loop(1, n)
    def _(s):
        ag_copy(s).start()

    @pl.loop(1, n)
    def _(s):
        ag_copy(s).wait()


def row_allreduce(x, n):
    rows, cols = x.shape
    h = rows // n
    return pl.pallas_call(
        functools.partial(_allreduce_kernel, n),
        out_shape=jax.ShapeDtypeStruct((rows, cols), x.dtype),
        in_specs=[pl.BlockSpec(memory_space=pltpu.VMEM)],
        out_specs=pl.BlockSpec(memory_space=pltpu.VMEM),
        scratch_shapes=[
            pltpu.VMEM((n, h, cols), x.dtype),
            pltpu.SemaphoreType.DMA((n,)),
            pltpu.SemaphoreType.DMA((n,)),
            pltpu.SemaphoreType.DMA((n,)),
            pltpu.SemaphoreType.DMA((n,)),
        ],
        compiler_params=pltpu.CompilerParams(has_side_effects=True),
        cost_estimate=pl.CostEstimate(
            flops=rows * cols, transcendentals=0, bytes_accessed=4 * rows * cols * 4
        ),
    )(x)


def on_device(n_row, eigen_vectors, panel_first, panel_second, factor_first, factor_second):
    vectors_first, vectors_second = (
        lax.all_gather(panel_first, "col", axis=1, tiled=True),
        lax.all_gather(panel_second, "col", axis=1, tiled=True),
    )
    updated = eigen_vectors
    for vectors, factor in ((vectors_second, factor_second), (vectors_first, factor_first)):
        projected = row_allreduce(local_dot(vectors.T, updated), n_row)
        updated = updated - local_dot(vectors, local_dot(factor, projected))
    return updated


def solution(mesh):
    return jax.shard_map(
        functools.partial(on_device, mesh.shape["row"]),
        mesh=mesh,
        in_specs=(P("row", "col"), P("row", "col"), P("row", "col"), P(), P()),
        out_specs=P("row", "col"),
        check_vma=False,
    )
```

time: 490 us -> 234 us (0.48)
  waiting for transfers between devices: 440 us -> 42.6 us
  Pallas kernels: 0 us -> 137 us
    psum x2 -> x0, waiting for transfers between devices: 369 us -> none  [on_device(): projected = lax.psum(local_dot(vectors.T, updated), 'row')]
    pallas_call x0 -> x2, Pallas kernels: none -> 137 us  [row_allreduce(): pl.pallas_call(functools.partial(_allreduce_kernel, n), out_shape=jax.Sha...]
    all_gather x1, waiting for transfers between devices: 27.3 us -> 0.02 us  [on_device(): lax.all_gather(panel_first, 'col', axis=1, tiled=True)]
  transfers between devices with their start and end apart: 4 -> 2, of which waited for: 4 -> 1; matrix products, arithmetic and copies ran while one was open for 2% -> 8% of each run, Pallas kernels for 0% -> 29%
where the time goes in v1:
time: 234 us; the launch traced here: 231 us
  Pallas kernels  137 us (59%)
  waiting for transfers between devices  42.6 us (18%)
  matrix products  32.8 us (14%)
  between operations  13.5 us (6%)
  local copies, waits for them, and re-layouts  4.7 us (2%)
    pallas_call x2, Pallas kernels, row_allreduce(): pl.pallas_call(functools.partial(_allreduce_kernel, n), out_shape=jax.Sha...  137 us
    all_gather x1, waiting for transfers between devices, on_device(): lax.all_gather(panel_second, 'col', axis=1, tiled=True)  41.2 us
    dot_general x6, matrix products, local_dot(): jnp.dot(left, right, precision=lax.Precision.HIGHEST, preferred_element_t...  32.8 us
  transfers between devices with their start and end apart: 2, of which 1 were waited for; matrix products, arithmetic and copies ran while one was open for 8% of the time, Pallas kernels for 29%

profile of v1, /device:TPU:1, one launch (start us, length us, event | category | flops | bytes accessed | tf_op | source)
XLA Modules:
  0.0 230.9 jit_solution(9108416816239452970)
XLA Ops:
  6.5 0.0 copy-start
  6.5 0.0 all-gather.3.cloned.1.call-start
  6.5 0.7 all-gather.3.cloned.1.call-update
  7.3 0.0 all-gather.5.cloned.1.call-start
  7.3 0.7 all-gather.5.cloned.1.call-update
  8.0 0.0 copy-start.3
  8.0 41.2 %all-gather.3.cloned.1.call-done = f32[1024,512]{1,0:T(8,128)} async-done(((f32[1024,128]{1,0:T(8,128)}), f32[1024,512]{1,0:T(8,128)}) %all-gather.3.cloned.1.call-update) | async-done | bytes 2097168 | tf_op jit(solution)/shard_map/all_gather | solution.py:94
  49.2 6.7 %fusion.x_ref = f32[512,512]{1,0:T(8,128)} fusion(f32[1024,512]{1,0:T(8,128)} %all-gather.3.cloned.1.call-done, f32[1024,512]{1,0:T(8,128)} %param.5), kind=kOutput, calls=%fused_computation.3 | convolution fusion | flops 3221225472 | bytes 5242880 | tf_op jit(solution)/shard_map/dot_general | solution.py:12
  55.9 0.0 copy-done.3
  55.9 1.8 copy.6
  57.7 67.9 %shard_map.55 = f32[512,512]{1,0:T(8,128)} custom-call(f32[512,512]{1,0:T(8,128)} %fusion.x_ref), custom_call_target="tpu_custom_call" | custom-call | flops 262144 | bytes 4194304 | tf_op jit(solution)/shard_map/pallas_call | solution.py:72
  125.6 0.0 copy-done
  125.6 0.0 copy-start.2
  125.6 4.8 %fusion.1 = f32[512,512]{1,0:T(8,128)S(1)} fusion(f32[512,512]{1,0:T(8,128)} %shard_map.55, f32[512,512]{1,0:T(8,128)S(1)} %copy-done), kind=kOutput, calls=%fused_computation.4 | convolution fusion | flops 1610612736 | bytes 3145728 | tf_op jit(solution)/shard_map/dot_general | solution.py:12
  130.4 0.0 copy-done.2
  130.4 5.2 %bitcast_subtract_fusion.1 = f32[1024,512]{0,1:T(8,128)S(1)} fusion(f32[1024,512]{0,1:T(8,128)} %copy.6, f32[512,512]{1,0:T(8,128)S(1)} %fusion.1, f32[1024,512]{1,0:T(8,128)S(1)} %copy-done.2), kind=kOutput, calls=%fused_computation.1 | convolution fusion | flops 3221749760 | bytes 7340032 | tf_op jit(solution)/shard_map/dot_general | solution.py:12
  135.6 0.0 all-gather.5.cloned.1.call-done
  135.6 6.1 %convolution_bitcast_fusion.x_ref = f32[512,512]{1,0:T(8,128)} fusion(f32[1024,512]{0,1:T(8,128)S(1)} %bitcast_subtract_fusion.1, f32[1024,512]{1,0:T(8,128)} %all-gather.5.cloned.1.call-done), kind=kOutput, calls=%fused_computation.2 | convolution fusion | flops 3221225472 | bytes 5242880 | tf_op jit(solution)/shard_map/dot_general | solution.py:12
  141.7 69.4 %shard_map.56 = f32[512,512]{1,0:T(8,128)} custom-call(f32[512,512]{1,0:T(8,128)} %convolution_bitcast_fusion.x_ref), custom_call_target="tpu_custom_call" | custom-call | flops 262144 | bytes 4194304 | tf_op jit(solution)/shard_map/pallas_call | solution.py:72
  211.1 0.0 copy-start.1
  211.1 5.2 %fusion.2 = f32[512,512]{1,0:T(8,128)S(1)} fusion(f32[512,512]{1,0:T(8,128)} %shard_map.56, f32[512,512]{1,0:T(8,128)} %param.8), kind=kOutput, calls=%fused_computation.5 | convolution fusion | flops 1610612736 | bytes 3145728 | tf_op jit(solution)/shard_map/dot_general | solution.py:12
  216.3 0.0 copy-done.1
  216.3 4.9 %bitcast_subtract_fusion = f32[1024,512]{0,1:T(8,128)} fusion(f32[1024,512]{0,1:T(8,128)S(1)} %bitcast_subtract_fusion.1, f32[512,512]{1,0:T(8,128)S(1)} %fusion.2, f32[1024,512]{1,0:T(8,128)S(1)} %copy-done.1), kind=kOutput, calls=%fused_computation | convolution fusion | flops 3221749760 | bytes 7340032 | tf_op jit(solution)/shard_map/dot_general | solution.py:12
  221.2 2.9 %copy.7 = f32[1024,512]{1,0:T(8,128)} copy(f32[1024,512]{0,1:T(8,128)} %bitcast_subtract_fusion) | data formatting | bytes 4194304 | tf_op jit(solution)/shard_map/sub | solution.py:99
Async XLA Ops:
  6.5 119.0 %copy-start = (f32[512,512]{1,0:T(8,128)S(1)}, f32[512,512]{1,0:T(8,128)}, u32[]{:S(2)}) copy-start(f32[512,512]{1,0:T(8,128)} %param.9) | copy-start | bytes 3145732
  6.5 42.7 %all-gather.3.cloned.1.call-start = ((), (), s32[]{:S(2)}) async-start(), calls=%async_computation | async-start | bytes 2621440 | tf_op jit(solution)/shard_map/all_gather | solution.py:94
  7.3 128.4 %all-gather.5.cloned.1.call-start = ((), (), s32[]{:S(2)}) async-start(), calls=%async_computation.1 | async-start | bytes 2621440 | tf_op jit(solution)/shard_map/all_gather | solution.py:93
  8.0 47.9 %copy-start.3 = (f32[1024,512]{1,0:T(8,128)S(1)}, f32[1024,512]{1,0:T(8,128)}, u32[]{:S(2)}) copy-start(f32[1024,512]{1,0:T(8,128)} %param.5) | copy-start | bytes 6291460
  125.6 4.9 %copy-start.2 = (f32[1024,512]{1,0:T(8,128)S(1)}, f32[1024,512]{1,0:T(8,128)}, u32[]{:S(2)}) copy-start(f32[1024,512]{1,0:T(8,128)} %all-gather.3.cloned.1.call-done) | copy-start | bytes 6291460
  211.1 5.2 %copy-start.1 = (f32[1024,512]{1,0:T(8,128)S(1)}, f32[1024,512]{1,0:T(8,128)}, u32[]{:S(2)}) copy-start(f32[1024,512]{1,0:T(8,128)} %all-gather.5.cloned.1.call-done) | copy-start | bytes 6291460
Sparse Core Ops, SparseCore 0:
  9.2 39.9 all-gather.2
  51.0 38.0 all-gather.4

commit v2 on v0

v2 whole, which is shorter than its diff:
```python
import functools

import jax
import jax.numpy as jnp
from jax import lax
from jax.experimental import pallas as pl
from jax.experimental.pallas import tpu as pltpu
from jax.sharding import PartitionSpec as P


def local_dot(left, right):
    return jnp.dot(left, right, precision=lax.Precision.HIGHEST, preferred_element_type=jnp.float32)


def _allreduce_kernel(groups, x_ref, o_ref, buf1, buf2, recv1, recv2, recv3, send_sems, recv_sems):
    me = lax.axis_index("row")
    col = lax.axis_index("col")
    g1, g2, g3 = groups
    s1, s2, s3 = 1, g1, g1 * g2
    i1 = lax.rem(me, g1)
    i2 = lax.rem(me // s2, g2)
    i3 = me // s3
    rows = x_ref.shape[0]
    p1 = rows // g1
    p2 = p1 // g2
    p3 = p2 // g3
    mesh_id = pl.DeviceIdType.MESH

    def rows_of(ref, start, size):
        return ref.at[pl.ds(pl.multiple_of(start, size), size), :]

    def exchange(stage, g, stride, mine, src_of, dst_of):
        def copy(s):
            j = lax.rem(mine + s, g)
            return pltpu.make_async_remote_copy(
                src_ref=src_of(j),
                dst_ref=dst_of(j, s),
                send_sem=send_sems.at[stage, s],
                recv_sem=recv_sems.at[stage, s],
                device_id=(me + (j - mine) * stride, col),
                device_id_type=mesh_id,
            )

        @pl.loop(1, g)
        def _(s):
            copy(s).start()

        @pl.loop(1, g)
        def _(s):
            copy(s).wait()

    def reduce_stage(stage, g, stride, mine, src, piece, recv):
        exchange(stage, g, stride, mine, lambda j: rows_of(src, j * piece, piece), lambda j, s: recv.at[s])
        return lax.fori_loop(1, g, lambda s, acc: acc + recv[s], src[pl.ds(pl.multiple_of(mine * piece, piece), piece), :])

    buf1[...] = reduce_stage(0, g1, s1, i1, x_ref, p1, recv1)
    buf2[...] = reduce_stage(1, g2, s2, i2, buf1, p2, recv2)
    base3 = i1 * p1 + i2 * p2
    o_ref[pl.ds(pl.multiple_of(base3 + i3 * p3, p3), p3), :] = reduce_stage(2, g3, s3, i3, buf2, p3, recv3)

    def gather_stage(stage, g, stride, mine, base, block):
        own = rows_of(o_ref, base + mine * block, block)
        exchange(stage, g, stride, mine, lambda j: own, lambda j, s: own)

    gather_stage(3, g3, s3, i3, base3, p3)
    gather_stage(4, g2, s2, i2, i1 * p1, p2)
    gather_stage(5, g1, s1, i1, 0, p1)


def row_allreduce(x, n):
    rows, cols = x.shape
    groups = (2, 4, n // 8)
    g1, g2, g3 = groups
    p1 = rows // g1
    p2 = p1 // g2
    p3 = p2 // g3
    return pl.pallas_call(
        functools.partial(_allreduce_kernel, groups),
        out_shape=jax.ShapeDtypeStruct((rows, cols), x.dtype),
        in_specs=[pl.BlockSpec(memory_space=pltpu.VMEM)],
        out_specs=pl.BlockSpec(memory_space=pltpu.VMEM),
        scratch_shapes=[
            pltpu.VMEM((p1, cols), x.dtype),
            pltpu.VMEM((p2, cols), x.dtype),
            pltpu.VMEM((g1, p1, cols), x.dtype),
            pltpu.VMEM((g2, p2, cols), x.dtype),
            pltpu.VMEM((g3, p3, cols), x.dtype),
            pltpu.SemaphoreType.DMA((6, max(groups))),
            pltpu.SemaphoreType.DMA((6, max(groups))),
        ],
        compiler_params=pltpu.CompilerParams(has_side_effects=True),
        cost_estimate=pl.CostEstimate(
            flops=rows * cols, transcendentals=0, bytes_accessed=4 * rows * cols * 4
        ),
    )(x)


def on_device(n_row, eigen_vectors, panel_first, panel_second, factor_first, factor_second):
    vectors_first, vectors_second = (
        lax.all_gather(panel_first, "col", axis=1, tiled=True),
        lax.all_gather(panel_second, "col", axis=1, tiled=True),
    )
    updated = eigen_vectors
    for vectors, factor in ((vectors_second, factor_second), (vectors_first, factor_first)):
        projected = row_allreduce(local_dot(vectors.T, updated), n_row)
        updated = updated - local_dot(vectors, local_dot(factor, projected))
    return updated


def solution(mesh):
    return jax.shard_map(
        functools.partial(on_device, mesh.shape["row"]),
        mesh=mesh,
        in_specs=(P("row", "col"), P("row", "col"), P("row", "col"), P(), P()),
        out_specs=P("row", "col"),
        check_vma=False,
    )
```

time: 490 us -> 186 us (0.38)
  waiting for transfers between devices: 440 us -> 42.6 us
  Pallas kernels: 0 us -> 92.5 us
    psum x2 -> x0, waiting for transfers between devices: 369 us -> none  [on_device(): projected = lax.psum(local_dot(vectors.T, updated), 'row')]
    pallas_call x0 -> x2, Pallas kernels: none -> 92.5 us  [row_allreduce(): pl.pallas_call(functools.partial(_allreduce_kernel, groups), out_shape=ja...]
    all_gather x1, waiting for transfers between devices: 27.3 us -> 0.02 us  [on_device(): lax.all_gather(panel_first, 'col', axis=1, tiled=True)]
  transfers between devices with their start and end apart: 4 -> 2, of which waited for: 4 -> 1; matrix products, arithmetic and copies ran while one was open for 2% -> 10% of each run, Pallas kernels for 0% -> 26%
where the time goes in v2:
time: 186 us
  Pallas kernels  92.5 us (50%)
  waiting for transfers between devices  42.6 us (23%)
  matrix products  32.8 us (18%)
  between operations  13.5 us (7%)
  local copies, waits for them, and re-layouts  4.7 us (3%)
    pallas_call x2, Pallas kernels, row_allreduce(): pl.pallas_call(functools.partial(_allreduce_kernel, groups), out_shape=ja...  92.5 us
    all_gather x1, waiting for transfers between devices, on_device(): lax.all_gather(panel_second, 'col', axis=1, tiled=True)  41.2 us
    dot_general x6, matrix products, local_dot(): jnp.dot(left, right, precision=lax.Precision.HIGHEST, preferred_element_t...  32.8 us
  transfers between devices with their start and end apart: 2, of which 1 were waited for; matrix products, arithmetic and copies ran while one was open for 10% of the time, Pallas kernels for 26%

profile of v2, /device:TPU:1, one launch (start us, length us, event | category | flops | bytes accessed | tf_op | source)
XLA Modules:
  0.0 186.1 jit_solution(3893587066614372632)
XLA Ops:
  6.5 0.0 copy-start
  6.5 0.0 all-gather.3.cloned.1.call-start
  6.5 0.7 all-gather.3.cloned.1.call-update
  7.3 0.0 all-gather.5.cloned.1.call-start
  7.3 0.7 all-gather.5.cloned.1.call-update
  8.0 0.0 copy-start.3
  8.0 41.2 %all-gather.3.cloned.1.call-done = f32[1024,512]{1,0:T(8,128)} async-done(((f32[1024,128]{1,0:T(8,128)}), f32[1024,512]{1,0:T(8,128)}) %all-gather.3.cloned.1.call-update) | async-done | bytes 2097168 | tf_op jit(solution)/shard_map/all_gather | solution.py:101
  49.2 6.7 %fusion.x_ref = f32[512,512]{1,0:T(8,128)} fusion(f32[1024,512]{1,0:T(8,128)} %all-gather.3.cloned.1.call-done, f32[1024,512]{1,0:T(8,128)} %param.5), kind=kOutput, calls=%fused_computation.3 | convolution fusion | flops 3221225472 | bytes 5242880 | tf_op jit(solution)/shard_map/dot_general | solution.py:12
  55.9 0.0 copy-done.3
  55.9 1.8 copy.6
  57.7 48.2 %shard_map.55 = f32[512,512]{1,0:T(8,128)} custom-call(f32[512,512]{1,0:T(8,128)} %fusion.x_ref), custom_call_target="tpu_custom_call" | custom-call | flops 262144 | bytes 4194304 | tf_op jit(solution)/shard_map/pallas_call | solution.py:77
  105.9 0.0 copy-done
  105.9 0.0 copy-start.2
  105.9 4.8 %fusion.1 = f32[512,512]{1,0:T(8,128)S(1)} fusion(f32[512,512]{1,0:T(8,128)} %shard_map.55, f32[512,512]{1,0:T(8,128)S(1)} %copy-done), kind=kOutput, calls=%fused_computation.4 | convolution fusion | flops 1610612736 | bytes 3145728 | tf_op jit(solution)/shard_map/dot_general | solution.py:12
  110.7 0.0 copy-done.2
  110.7 5.2 %bitcast_subtract_fusion.1 = f32[1024,512]{0,1:T(8,128)S(1)} fusion(f32[1024,512]{0,1:T(8,128)} %copy.6, f32[512,512]{1,0:T(8,128)S(1)} %fusion.1, f32[1024,512]{1,0:T(8,128)S(1)} %copy-done.2), kind=kOutput, calls=%fused_computation.1 | convolution fusion | flops 3221749760 | bytes 7340032 | tf_op jit(solution)/shard_map/dot_general | solution.py:12
  115.9 0.0 all-gather.5.cloned.1.call-done
  115.9 6.1 %convolution_bitcast_fusion.x_ref = f32[512,512]{1,0:T(8,128)} fusion(f32[1024,512]{0,1:T(8,128)S(1)} %bitcast_subtract_fusion.1, f32[1024,512]{1,0:T(8,128)} %all-gather.5.cloned.1.call-done), kind=kOutput, calls=%fused_computation.2 | convolution fusion | flops 3221225472 | bytes 5242880 | tf_op jit(solution)/shard_map/dot_general | solution.py:12
  122.0 44.3 %shard_map.56 = f32[512,512]{1,0:T(8,128)} custom-call(f32[512,512]{1,0:T(8,128)} %convolution_bitcast_fusion.x_ref), custom_call_target="tpu_custom_call" | custom-call | flops 262144 | bytes 4194304 | tf_op jit(solution)/shard_map/pallas_call | solution.py:77
  166.3 0.0 copy-start.1
  166.3 5.2 %fusion.2 = f32[512,512]{1,0:T(8,128)S(1)} fusion(f32[512,512]{1,0:T(8,128)} %shard_map.56, f32[512,512]{1,0:T(8,128)} %param.8), kind=kOutput, calls=%fused_computation.5 | convolution fusion | flops 1610612736 | bytes 3145728 | tf_op jit(solution)/shard_map/dot_general | solution.py:12
  171.5 0.0 copy-done.1
  171.5 4.9 %bitcast_subtract_fusion = f32[1024,512]{0,1:T(8,128)} fusion(f32[1024,512]{0,1:T(8,128)S(1)} %bitcast_subtract_fusion.1, f32[512,512]{1,0:T(8,128)S(1)} %fusion.2, f32[1024,512]{1,0:T(8,128)S(1)} %copy-done.1), kind=kOutput, calls=%fused_computation | convolution fusion | flops 3221749760 | bytes 7340032 | tf_op jit(solution)/shard_map/dot_general | solution.py:12
  176.4 2.9 %copy.7 = f32[1024,512]{1,0:T(8,128)} copy(f32[1024,512]{0,1:T(8,128)} %bitcast_subtract_fusion) | data formatting | bytes 4194304 | tf_op jit(solution)/shard_map/sub | solution.py:106
Async XLA Ops:
  6.5 99.3 %copy-start = (f32[512,512]{1,0:T(8,128)S(1)}, f32[512,512]{1,0:T(8,128)}, u32[]{:S(2)}) copy-start(f32[512,512]{1,0:T(8,128)} %param.9) | copy-start | bytes 3145732
  6.5 42.7 %all-gather.3.cloned.1.call-start = ((), (), s32[]{:S(2)}) async-start(), calls=%async_computation | async-start | bytes 2621440 | tf_op jit(solution)/shard_map/all_gather | solution.py:101
  7.3 108.7 %all-gather.5.cloned.1.call-start = ((), (), s32[]{:S(2)}) async-start(), calls=%async_computation.1 | async-start | bytes 2621440 | tf_op jit(solution)/shard_map/all_gather | solution.py:100
  8.0 47.9 %copy-start.3 = (f32[1024,512]{1,0:T(8,128)S(1)}, f32[1024,512]{1,0:T(8,128)}, u32[]{:S(2)}) copy-start(f32[1024,512]{1,0:T(8,128)} %param.5) | copy-start | bytes 6291460
  105.9 4.9 %copy-start.2 = (f32[1024,512]{1,0:T(8,128)S(1)}, f32[1024,512]{1,0:T(8,128)}, u32[]{:S(2)}) copy-start(f32[1024,512]{1,0:T(8,128)} %all-gather.3.cloned.1.call-done) | copy-start | bytes 6291460
  166.3 5.2 %copy-start.1 = (f32[1024,512]{1,0:T(8,128)S(1)}, f32[1024,512]{1,0:T(8,128)}, u32[]{:S(2)}) copy-start(f32[1024,512]{1,0:T(8,128)} %all-gather.5.cloned.1.call-done) | copy-start | bytes 6291460
Sparse Core Ops, SparseCore 0:
  9.2 39.9 all-gather.2
  51.0 38.0 all-gather.4

commit v3 on v2

--- a/solution.py
+++ b/solution.py
@@ -12,7 +12,7 @@
     return jnp.dot(left, right, precision=lax.Precision.HIGHEST, preferred_element_type=jnp.float32)
 
 
-def _allreduce_kernel(groups, x_ref, o_ref, buf1, buf2, recv1, recv2, recv3, send_sems, recv_sems):
+def _allreduce_kernel(groups, x_ref, t_ref, o_ref, buf1, buf2, recv1, recv2, recv3, send_sems, recv_sems):
     me = lax.axis_index("row")
     col = lax.axis_index("col")
     g1, g2, g3 = groups
@@ -56,7 +56,10 @@
     buf1[...] = reduce_stage(0, g1, s1, i1, x_ref, p1, recv1)
     buf2[...] = reduce_stage(1, g2, s2, i2, buf1, p2, recv2)
     base3 = i1 * p1 + i2 * p2
-    o_ref[pl.ds(pl.multiple_of(base3 + i3 * p3, p3), p3), :] = reduce_stage(2, g3, s3, i3, buf2, p3, recv3)
+    reduced = reduce_stage(2, g3, s3, i3, buf2, p3, recv3)
+    o_ref[pl.ds(pl.multiple_of(base3 + i3 * p3, p3), p3), :] = jnp.dot(
+        reduced, t_ref[...], precision=lax.Precision.HIGHEST, preferred_element_type=jnp.float32
+    )
 
     def gather_stage(stage, g, stride, mine, base, block):
         own = rows_of(o_ref, base + mine * block, block)
@@ -67,7 +70,7 @@
     gather_stage(5, g1, s1, i1, 0, p1)
 
 
-def row_allreduce(x, n):
+def row_allreduce_times(x, t_transposed, n):
     rows, cols = x.shape
     groups = (2, 4, n // 8)
     g1, g2, g3 = groups
@@ -77,7 +80,7 @@
     return pl.pallas_call(
         functools.partial(_allreduce_kernel, groups),
         out_shape=jax.ShapeDtypeStruct((rows, cols), x.dtype),
-        in_specs=[pl.BlockSpec(memory_space=pltpu.VMEM)],
+        in_specs=[pl.BlockSpec(memory_space=pltpu.VMEM)] * 2,
         out_specs=pl.BlockSpec(memory_space=pltpu.VMEM),
         scratch_shapes=[
             pltpu.VMEM((p1, cols), x.dtype),
@@ -92,7 +95,7 @@
         cost_estimate=pl.CostEstimate(
             flops=rows * cols, transcendentals=0, bytes_accessed=4 * rows * cols * 4
         ),
-    )(x)
+    )(x, t_transposed)
 
 
 def on_device(n_row, eigen_vectors, panel_first, panel_second, factor_first, factor_second):
@@ -102,8 +105,9 @@
     )
     updated = eigen_vectors
     for vectors, factor in ((vectors_second, factor_second), (vectors_first, factor_first)):
-        projected = row_allreduce(local_dot(vectors.T, updated), n_row)
-        updated = updated - local_dot(vectors, local_dot(factor, projected))
+        partial_t = lax.dot_general(updated, vectors, (((0,), (0,)), ((), ())), precision=lax.Precision.HIGHEST, preferred_element_type=jnp.float32)
+        applied_t = row_allreduce_times(partial_t, factor.T, n_row)
+        updated = updated - lax.dot_general(vectors, applied_t, (((1,), (1,)), ((), ())), precision=lax.Precision.HIGHEST, preferred_element_type=jnp.float32)
     return updated
 
 

time: 186 us -> 179 us (0.962)
  matrix products: 32.8 us -> 25.1 us
  waiting for transfers between devices: 42.6 us -> 36.9 us
  local copies, waits for them, and re-layouts: 4.7 us -> 8.57 us
    dot_general x6 -> x4, matrix products: 32.8 us -> 25.1 us  [the longest x2 12.9 us: on_device(): lax.dot_general(vectors, applied_t, (((1,), (1,)), ((), ())), precision=l...]
    all_gather x1, waiting for transfers between devices: 41.2 us -> 35.5 us  [on_device(): lax.all_gather(panel_second, 'col', axis=1, tiled=True)]
    unnamed x9 -> x7, local copies, waits for them, and re-layouts: 1.82 us -> 5.69 us
    pallas_call x2, Pallas kernels: 92.5 us -> 94.3 us  [row_allreduce_times(): pl.pallas_call(functools.partial(_allreduce_kernel, groups), out_shape=ja...]
  transfers between devices with their start and end apart: 2 -> 2, of which waited for: 1 -> 1; matrix products, arithmetic and copies ran while one was open for 10% -> 10% of each run, Pallas kernels for 26% -> 27%
where the time goes in v3:
time: 179 us; the launch traced here: 178 us
  Pallas kernels  94.3 us (53%)
  waiting for transfers between devices  36.9 us (21%)
  matrix products  25.1 us (14%)
  between operations  13.4 us (7%)
  local copies, waits for them, and re-layouts  8.57 us (5%)
    pallas_call x2, Pallas kernels, row_allreduce_times(): pl.pallas_call(functools.partial(_allreduce_kernel, groups), out_shape=ja...  94.3 us
    all_gather x1, waiting for transfers between devices, on_device(): lax.all_gather(panel_second, 'col', axis=1, tiled=True)  35.5 us
    dot_general x2, matrix products, on_device(): lax.dot_general(vectors, applied_t, (((1,), (1,)), ((), ())), precision=l...  12.9 us
    dot_general x2, matrix products, on_device(): lax.dot_general(updated, vectors, (((0,), (0,)), ((), ())), precision=lax...  12.2 us
    unnamed x7, local copies, waits for them, and re-layouts  5.69 us
  transfers between devices with their start and end apart: 2, of which 1 were waited for; matrix products, arithmetic and copies ran while one was open for 10% of the time, Pallas kernels for 27%

profile of v3, /device:TPU:1, one launch (start us, length us, event | category | flops | bytes accessed | tf_op | source)
XLA Modules:
  0.0 178.3 jit_solution(10751504557670293500)
XLA Ops:
  6.5 0.0 copy-start
  6.5 0.0 all-gather.3.cloned.1.call-start
  6.5 0.7 all-gather.3.cloned.1.call-update
  7.3 0.0 all-gather.5.cloned.1.call-start
  7.3 0.7 all-gather.5.cloned.1.call-update
  8.0 2.6 %copy.6 = f32[512,512]{0,1:T(8,128)} copy(f32[512,512]{1,0:T(8,128)} %param.9) | data formatting | bytes 2097152 | tf_op args[4]
  10.6 0.0 copy-done
  10.6 0.0 copy-start.1
  10.6 1.8 %copy.7 = f32[1024,512]{0,1:T(8,128)} copy(f32[1024,512]{1,0:T(8,128)S(1)} %copy-done) | data formatting | bytes 4194304 | tf_op args[0]
  12.4 0.0 copy-done.1
  12.4 1.3 copy.8
  13.7 35.5 %all-gather.3.cloned.1.call-done = f32[1024,512]{1,0:T(8,128)} async-done(((f32[1024,128]{1,0:T(8,128)}), f32[1024,512]{1,0:T(8,128)}) %all-gather.3.cloned.1.call-update) | async-done | bytes 2097168 | tf_op jit(solution)/shard_map/all_gather | solution.py:104
  49.2 6.1 %fusion.x_ref = f32[512,512]{1,0:T(8,128)} fusion(f32[1024,512]{1,0:T(8,128)S(1)} %copy-done, f32[1024,512]{1,0:T(8,128)} %all-gather.3.cloned.1.call-done), kind=kOutput, calls=%fused_computation.2 | convolution fusion | flops 3221225472 | bytes 5242880 | tf_op jit(solution)/shard_map/dot_general | solution.py:108
  55.3 49.0 %shard_map.55 = f32[512,512]{1,0:T(8,128)} custom-call(f32[512,512]{1,0:T(8,128)} %fusion.x_ref, f32[512,512]{1,0:T(8,128)} %bitcast.15), custom_call_target="tpu_custom_call" | custom-call | flops 262144 | bytes 4194304 | tf_op jit(solution)/shard_map/pallas_call | solution.py:80
  104.3 6.1 %bitcast_subtract_fusion.1 = f32[1024,512]{0,1:T(8,128)S(1)} fusion(f32[1024,512]{0,1:T(8,128)} %copy.7, f32[512,512]{1,0:T(8,128)} %shard_map.55, f32[1024,512]{1,0:T(8,128)} %all-gather.3.cloned.1.call-done), kind=kOutput, calls=%fused_computation.1 | convolution fusion | flops 3221749760 | bytes 7340032 | tf_op jit(solution)/shard_map/dot_general | solution.py:110
  110.4 0.0 all-gather.5.cloned.1.call-done
  110.4 6.1 %fusion.1.x_ref = f32[512,512]{1,0:T(8,128)} fusion(f32[1024,512]{0,1:T(8,128)S(1)} %bitcast_subtract_fusion.1, f32[1024,512]{1,0:T(8,128)} %all-gather.5.cloned.1.call-done), kind=kOutput, calls=%fused_computation.3 | convolution fusion | flops 3221225472 | bytes 5242880 | tf_op jit(solution)/shard_map/dot_general | solution.py:108
  116.5 45.3 %shard_map.56 = f32[512,512]{1,0:T(8,128)} custom-call(f32[512,512]{1,0:T(8,128)} %fusion.1.x_ref, f32[512,512]{1,0:T(8,128)} %bitcast.14), custom_call_target="tpu_custom_call" | custom-call | flops 262144 | bytes 4194304 | tf_op jit(solution)/shard_map/pallas_call | solution.py:80
  161.8 6.8 %bitcast_subtract_fusion = f32[1024,512]{0,1:T(8,128)} fusion(f32[1024,512]{0,1:T(8,128)S(1)} %bitcast_subtract_fusion.1, f32[512,512]{1,0:T(8,128)} %shard_map.56, f32[1024,512]{1,0:T(8,128)} %all-gather.5.cloned.1.call-done), kind=kOutput, calls=%fused_computation | convolution fusion | flops 3221749760 | bytes 7340032 | tf_op jit(solution)/shard_map/dot_general | solution.py:110
  168.6 2.9 %copy.9 = f32[1024,512]{1,0:T(8,128)} copy(f32[1024,512]{0,1:T(8,128)} %bitcast_subtract_fusion) | data formatting | bytes 4194304 | tf_op jit(solution)/shard_map/sub | solution.py:110
Async XLA Ops:
  6.5 4.0 %copy-start = (f32[1024,512]{1,0:T(8,128)S(1)}, f32[1024,512]{1,0:T(8,128)}, u32[]{:S(2)}) copy-start(f32[1024,512]{1,0:T(8,128)} %param.5) | copy-start | bytes 6291460
  6.5 42.7 %all-gather.3.cloned.1.call-start = ((), (), s32[]{:S(2)}) async-start(), calls=%async_computation | async-start | bytes 2621440 | tf_op jit(solution)/shard_map/all_gather | solution.py:104
  7.3 103.2 %all-gather.5.cloned.1.call-start = ((), (), s32[]{:S(2)}) async-start(), calls=%async_computation.1 | async-start | bytes 2621440 | tf_op jit(solution)/shard_map/all_gather | solution.py:103
  10.6 1.8 %copy-start.1 = (f32[512,512]{1,0:T(8,128)S(1)}, f32[512,512]{1,0:T(8,128)}, u32[]{:S(2)}) copy-start(f32[512,512]{1,0:T(8,128)} %param.8) | copy-start | bytes 3145732
Sparse Core Ops, SparseCore 0:
  9.2 39.9 all-gather.2
  51.0 38.0 all-gather.4

commit v4 on v3

--- a/solution.py
+++ b/solution.py
@@ -98,11 +98,50 @@
     )(x, t_transposed)
 
 
-def on_device(n_row, eigen_vectors, panel_first, panel_second, factor_first, factor_second):
-    vectors_first, vectors_second = (
-        lax.all_gather(panel_first, "col", axis=1, tiled=True),
-        lax.all_gather(panel_second, "col", axis=1, tiled=True),
-    )
+def _col_gather_kernel(n, v_ref, o_ref, send_sems, recv_sems):
+    me = lax.axis_index("col")
+    row = lax.axis_index("row")
+    w = v_ref.shape[1]
+    own = o_ref.at[:, pl.ds(pl.multiple_of(me * w, w), w)]
+
+    def copy(s):
+        return pltpu.make_async_remote_copy(
+            src_ref=v_ref,
+            dst_ref=own,
+            send_sem=send_sems.at[s],
+            recv_sem=recv_sems.at[s],
+            device_id=(row, lax.rem(me + s, n)),
+            device_id_type=pl.DeviceIdType.MESH,
+        )
+
+    @pl.loop(1, n)
+    def _(s):
+        copy(s).start()
+
+    own[...] = v_ref[...]
+
+    @pl.loop(1, n)
+    def _(s):
+        copy(s).wait()
+
+
+def col_gather(v, n):
+    rows, w = v.shape
+    return pl.pallas_call(
+        functools.partial(_col_gather_kernel, n),
+        out_shape=jax.ShapeDtypeStruct((rows, w * n), v.dtype),
+        in_specs=[pl.BlockSpec(memory_space=pltpu.VMEM)],
+        out_specs=pl.BlockSpec(memory_space=pltpu.VMEM),
+        scratch_shapes=[pltpu.SemaphoreType.DMA((n,)), pltpu.SemaphoreType.DMA((n,))],
+        compiler_params=pltpu.CompilerParams(has_side_effects=True),
+        cost_estimate=pl.CostEstimate(flops=0, transcendentals=0, bytes_accessed=2 * rows * w * n * 4),
+    )(v)
+
+
+def on_device(n_row, n_col, eigen_vectors, panel_first, panel_second, factor_first, factor_second):
+    vectors_second = col_gather(panel_second, n_col)
+    vectors_second, panel_first = lax.optimization_barrier((vectors_second, panel_first))
+    vectors_first = lax.all_gather(panel_first, "col", axis=1, tiled=True)
     updated = eigen_vectors
     for vectors, factor in ((vectors_second, factor_second), (vectors_first, factor_first)):
         partial_t = lax.dot_general(updated, vectors, (((0,), (0,)), ((), ())), precision=lax.Precision.HIGHEST, preferred_element_type=jnp.float32)
@@ -113,7 +152,7 @@
 
 def solution(mesh):
     return jax.shard_map(
-        functools.partial(on_device, mesh.shape["row"]),
+        functools.partial(on_device, mesh.shape["row"], mesh.shape["col"]),
         mesh=mesh,
         in_specs=(P("row", "col"), P("row", "col"), P("row", "col"), P(), P()),
         out_specs=P("row", "col"),

time: 179 us -> 177 us (0.989)
  Pallas kernels: 94.3 us -> 135 us
  waiting for transfers between devices: 36.9 us -> 0.04 us
  local copies, waits for them, and re-layouts: 8.57 us -> 3.25 us
    pallas_call x0 -> x1, Pallas kernels: none -> 42.3 us  [col_gather(): pl.pallas_call(functools.partial(_col_gather_kernel, n), out_shape=jax.Sh...]
    all_gather x2 -> x1, waiting for transfers between devices: 35.5 us -> 0.02 us  [on_device(): vectors_first = lax.all_gather(panel_first, 'col', axis=1, tiled=True)]
    sub x1 -> x0, local copies, waits for them, and re-layouts: 2.88 us -> none  [on_device(): updated - lax.dot_general(vectors, applied_t, (((1,), (1,)), ((), ())), p...]
    unnamed x7 -> x10, local copies, waits for them, and re-layouts: 5.69 us -> 3.25 us
  transfers between devices with their start and end apart: 2 -> 1, of which waited for: 1 -> 0; matrix products, arithmetic and copies ran while one was open for 10% -> 8% of each run, Pallas kernels for 27% -> 27%
where the time goes in v4:
time: 177 us; the launch traced here: 176 us
  Pallas kernels  135 us (76%)
  matrix products  24.5 us (14%)
  between operations  13.5 us (8%)
  local copies, waits for them, and re-layouts  3.25 us (2%)
    pallas_call x2, Pallas kernels, row_allreduce_times(): pl.pallas_call(functools.partial(_allreduce_kernel, groups), out_shape=ja...  92.8 us
    pallas_call x1, Pallas kernels, col_gather(): pl.pallas_call(functools.partial(_col_gather_kernel, n), out_shape=jax.Sh...  42.3 us
    dot_general x2, matrix products, on_device(): lax.dot_general(vectors, applied_t, (((1,), (1,)), ((), ())), precision=l...  12.3 us
    dot_general x2, matrix products, on_device(): lax.dot_general(updated, vectors, (((0,), (0,)), ((), ())), precision=lax...  12.1 us
  transfers between devices with their start and end apart: 1, of which 0 were waited for; matrix products, arithmetic and copies ran while one was open for 8% of the time, Pallas kernels for 27%

profile of v4, /device:TPU:1, one launch (start us, length us, event | category | flops | bytes accessed | tf_op | source)
XLA Modules:
  0.0 176.4 jit_solution(17128958866856844010)
XLA Ops:
  6.5 0.0 copy-start.2
  6.5 0.0 all-gather.2.cloned.1.call-start
  6.5 42.3 %shard_map.55 = f32[1024,512]{1,0:T(8,128)} custom-call(f32[1024,128]{1,0:T(8,128)} %v_ref.1), custom_call_target="tpu_custom_call" | custom-call | bytes 4194304 | tf_op jit(solution)/shard_map/pallas_call | solution.py:130
  48.9 0.0 copy-start
  48.9 0.0 all-gather.2.cloned.1.call-update
  48.9 0.0 copy-done.2
  48.9 1.3 copy.6
  50.2 0.6 copy-done
  50.9 6.1 %convolution_bitcast_fusion.x_ref = f32[512,512]{1,0:T(8,128)} fusion(f32[1024,512]{1,0:T(8,128)S(1)} %copy-done, f32[1024,512]{1,0:T(8,128)} %param.5), kind=kOutput, calls=%fused_computation.2 | convolution fusion | flops 3221225472 | bytes 5242880 | tf_op jit(solution)/shard_map/dot_general | solution.py:147
  56.9 0.0 copy-start.3
  56.9 47.6 %shard_map.56 = f32[512,512]{1,0:T(8,128)} custom-call(f32[512,512]{1,0:T(8,128)} %convolution_bitcast_fusion.x_ref, f32[512,512]{1,0:T(8,128)} %bitcast.13), custom_call_target="tpu_custom_call" | custom-call | flops 262144 | bytes 4194304 | tf_op jit(solution)/shard_map/pallas_call | solution.py:80
  104.6 0.0 copy-done.3
  104.6 0.0 copy-start.1
  104.6 1.3 copy.7
  105.9 0.0 copy-done.1
  105.9 5.7 %convolution_subtract_fusion.1 = f32[1024,512]{1,0:T(8,128)S(1)} fusion(f32[1024,512]{1,0:T(8,128)} %param.5, f32[1024,512]{1,0:T(8,128)} %shard_map.55, f32[512,512]{1,0:T(8,128)S(1)} %copy-done.1), kind=kOutput, calls=%fused_computation.1 | convolution fusion | flops 3221749760 | bytes 7340032 | tf_op jit(solution)/shard_map/dot_general | solution.py:149
  111.6 0.0 all-gather.2.cloned.1.call-done
  111.6 6.1 %fusion.x_ref = f32[512,512]{1,0:T(8,128)} fusion(f32[1024,512]{1,0:T(8,128)S(1)} %convolution_subtract_fusion.1, f32[1024,512]{1,0:T(8,128)} %all-gather.2.cloned.1.call-done), kind=kOutput, calls=%fused_computation.3 | convolution fusion | flops 3221225472 | bytes 5242880 | tf_op jit(solution)/shard_map/dot_general | solution.py:147
  117.7 45.2 %shard_map.57 = f32[512,512]{1,0:T(8,128)} custom-call(f32[512,512]{1,0:T(8,128)} %fusion.x_ref, f32[512,512]{1,0:T(8,128)} %bitcast.12), custom_call_target="tpu_custom_call" | custom-call | flops 262144 | bytes 4194304 | tf_op jit(solution)/shard_map/pallas_call | solution.py:80
  162.9 6.6 %convolution_subtract_fusion = f32[1024,512]{1,0:T(8,128)} fusion(f32[1024,512]{1,0:T(8,128)S(1)} %convolution_subtract_fusion.1, f32[1024,512]{1,0:T(8,128)} %all-gather.2.cloned.1.call-done, f32[512,512]{1,0:T(8,128)} %shard_map.57), kind=kOutput, calls=%fused_computation | convolution fusion | flops 3221749760 | bytes 7340032 | tf_op jit(solution)/shard_map/dot_general | solution.py:149
Async XLA Ops:
  6.5 42.4 %copy-start.2 = (f32[512,512]{1,0:T(8,128)S(1)}, f32[512,512]{1,0:T(8,128)}, u32[]{:S(2)}) copy-start(f32[512,512]{1,0:T(8,128)} %param.9) | copy-start | bytes 3145732
  6.5 105.1 %all-gather.2.cloned.1.call-start = ((), (), s32[]{:S(2)}) async-start(), calls=%async_computation | async-start | bytes 2621440 | tf_op jit(solution)/shard_map/all_gather | solution.py:144
  48.9 2.0 %copy-start = (f32[1024,512]{1,0:T(8,128)S(1)}, f32[1024,512]{1,0:T(8,128)}, u32[]{:S(2)}) copy-start(f32[1024,512]{1,0:T(8,128)} %shard_map.55) | copy-start | bytes 6291460
  56.9 47.6 %copy-start.3 = (f32[512,512]{1,0:T(8,128)S(1)}, f32[512,512]{1,0:T(8,128)}, u32[]{:S(2)}) copy-start(f32[512,512]{1,0:T(8,128)} %param.8) | copy-start | bytes 3145732
  104.6 1.3 copy-start.1
Sparse Core Ops, SparseCore 0:
  49.0 36.6 all-gather.1

commit v5 on v4

--- a/solution.py
+++ b/solution.py
@@ -57,8 +57,8 @@
     buf2[...] = reduce_stage(1, g2, s2, i2, buf1, p2, recv2)
     base3 = i1 * p1 + i2 * p2
     reduced = reduce_stage(2, g3, s3, i3, buf2, p3, recv3)
-    o_ref[pl.ds(pl.multiple_of(base3 + i3 * p3, p3), p3), :] = jnp.dot(
-        reduced, t_ref[...], precision=lax.Precision.HIGHEST, preferred_element_type=jnp.float32
+    o_ref[pl.ds(pl.multiple_of(base3 + i3 * p3, p3), p3), :] = lax.dot_general(
+        reduced, t_ref[...], (((1,), (1,)), ((), ())), precision=lax.Precision.HIGHEST, preferred_element_type=jnp.float32
     )
 
     def gather_stage(stage, g, stride, mine, base, block):
@@ -70,7 +70,7 @@
     gather_stage(5, g1, s1, i1, 0, p1)
 
 
-def row_allreduce_times(x, t_transposed, n):
+def row_allreduce_times(x, t, n):
     rows, cols = x.shape
     groups = (2, 4, n // 8)
     g1, g2, g3 = groups
@@ -95,7 +95,7 @@
         cost_estimate=pl.CostEstimate(
             flops=rows * cols, transcendentals=0, bytes_accessed=4 * rows * cols * 4
         ),
-    )(x, t_transposed)
+    )(x, t)
 
 
 def _col_gather_kernel(n, v_ref, o_ref, send_sems, recv_sems):
@@ -144,9 +144,9 @@
     vectors_first = lax.all_gather(panel_first, "col", axis=1, tiled=True)
     updated = eigen_vectors
     for vectors, factor in ((vectors_second, factor_second), (vectors_first, factor_first)):
-        partial_t = lax.dot_general(updated, vectors, (((0,), (0,)), ((), ())), precision=lax.Precision.HIGHEST, preferred_element_type=jnp.float32)
-        applied_t = row_allreduce_times(partial_t, factor.T, n_row)
-        updated = updated - lax.dot_general(vectors, applied_t, (((1,), (1,)), ((), ())), precision=lax.Precision.HIGHEST, preferred_element_type=jnp.float32)
+        partial_t = lax.dot_general(updated, vectors, (((0,), (0,)), ((), ())), precision=lax.Precision.HIGH, preferred_element_type=jnp.float32)
+        applied_t = row_allreduce_times(partial_t, factor, n_row)
+        updated = updated - lax.dot_general(vectors, applied_t, (((1,), (1,)), ((), ())), precision=lax.Precision.HIGH, preferred_element_type=jnp.float32)
     return updated
 
 

time: 177 us -> 168 us (0.949)
  matrix products: 24.5 us -> 18.2 us
  local copies, waits for them, and re-layouts: 3.25 us -> 0.01 us
    dot_general x2, matrix products: 12.1 us -> 8.8 us  [on_device(): lax.dot_general(updated, vectors, (((0,), (0,)), ((), ())), precision=lax...]
    unnamed x10 -> x2, local copies, waits for them, and re-layouts: 3.25 us -> 0.01 us
    dot_general x2, matrix products: 12.3 us -> 9.41 us  [on_device(): lax.dot_general(vectors, applied_t, (((1,), (1,)), ((), ())), precision=l...]
  transfers between devices with their start and end apart: 1 -> 1, of which waited for: 0 -> 0; matrix products, arithmetic and copies ran while one was open for 8% -> 5% of each run, Pallas kernels for 27% -> 28%
where the time goes in v5:
time: 168 us
  Pallas kernels  136 us (81%)
  matrix products  18.2 us (11%)
  between operations  13.4 us (8%)
    pallas_call x2, Pallas kernels, row_allreduce_times(): pl.pallas_call(functools.partial(_allreduce_kernel, groups), out_shape=ja...  93.5 us
    pallas_call x1, Pallas kernels, col_gather(): pl.pallas_call(functools.partial(_col_gather_kernel, n), out_shape=jax.Sh...  42.3 us
    dot_general x2, matrix products, on_device(): lax.dot_general(vectors, applied_t, (((1,), (1,)), ((), ())), precision=l...  9.41 us
    dot_general x2, matrix products, on_device(): lax.dot_general(updated, vectors, (((0,), (0,)), ((), ())), precision=lax...  8.8 us
  transfers between devices with their start and end apart: 1, of which 0 were waited for; matrix products, arithmetic and copies ran while one was open for 5% of the time, Pallas kernels for 28%

profile of v5, /device:TPU:1, one launch (start us, length us, event | category | flops | bytes accessed | tf_op | source)
XLA Modules:
  0.0 167.6 jit_solution(56603127739189323)
XLA Ops:
  6.5 0.0 copy-start
  6.5 0.0 all-gather.2.cloned.1.call-start
  6.5 42.3 %shard_map.55 = f32[1024,512]{1,0:T(8,128)} custom-call(f32[1024,128]{1,0:T(8,128)} %v_ref.1), custom_call_target="tpu_custom_call" | custom-call | bytes 4194304 | tf_op jit(solution)/shard_map/pallas_call | solution.py:130
  48.9 0.0 all-gather.2.cloned.1.call-update
  48.9 0.0 copy-done
  48.9 4.4 %convolution_bitcast_fusion.x_ref = f32[512,512]{1,0:T(8,128)} fusion(f32[1024,512]{1,0:T(8,128)} %shard_map.55, f32[1024,512]{1,0:T(8,128)S(1)} %copy-done), kind=kOutput, calls=%fused_computation.2 | convolution fusion | flops 1610612736 | bytes 5242880 | tf_op jit(solution)/shard_map/dot_general | solution.py:147
  53.3 47.7 %shard_map.56 = f32[512,512]{1,0:T(8,128)} custom-call(f32[512,512]{1,0:T(8,128)} %convolution_bitcast_fusion.x_ref, f32[512,512]{1,0:T(8,128)} %t_ref.2), custom_call_target="tpu_custom_call" | custom-call | flops 262144 | bytes 4194304 | tf_op jit(solution)/shard_map/pallas_call | solution.py:80
  101.0 4.4 %convolution_subtract_fusion.1 = f32[1024,512]{1,0:T(8,128)S(1)} fusion(f32[1024,512]{1,0:T(8,128)} %param.5, f32[1024,512]{1,0:T(8,128)} %shard_map.55, f32[512,512]{1,0:T(8,128)} %shard_map.56), kind=kOutput, calls=%fused_computation.1 | convolution fusion | flops 1611137024 | bytes 7340032 | tf_op jit(solution)/shard_map/dot_general | solution.py:149
  105.5 0.0 all-gather.2.cloned.1.call-done
  105.5 4.4 %fusion.x_ref = f32[512,512]{1,0:T(8,128)} fusion(f32[1024,512]{1,0:T(8,128)S(1)} %convolution_subtract_fusion.1, f32[1024,512]{1,0:T(8,128)} %all-gather.2.cloned.1.call-done), kind=kOutput, calls=%fused_computation.3 | convolution fusion | flops 1610612736 | bytes 5242880 | tf_op jit(solution)/shard_map/dot_general | solution.py:147
  109.9 45.8 %shard_map.57 = f32[512,512]{1,0:T(8,128)} custom-call(f32[512,512]{1,0:T(8,128)} %fusion.x_ref, f32[512,512]{1,0:T(8,128)} %t_ref.3), custom_call_target="tpu_custom_call" | custom-call | flops 262144 | bytes 4194304 | tf_op jit(solution)/shard_map/pallas_call | solution.py:80
  155.7 5.0 %convolution_subtract_fusion = f32[1024,512]{1,0:T(8,128)} fusion(f32[1024,512]{1,0:T(8,128)S(1)} %convolution_subtract_fusion.1, f32[1024,512]{1,0:T(8,128)} %all-gather.2.cloned.1.call-done, f32[512,512]{1,0:T(8,128)} %shard_map.57), kind=kOutput, calls=%fused_computation | convolution fusion | flops 1611137024 | bytes 7340032 | tf_op jit(solution)/shard_map/dot_general | solution.py:149
Async XLA Ops:
  6.5 42.4 %copy-start = (f32[1024,512]{1,0:T(8,128)S(1)}, f32[1024,512]{1,0:T(8,128)}, u32[]{:S(2)}) copy-start(f32[1024,512]{1,0:T(8,128)} %param.5) | copy-start | bytes 6291460
  6.5 98.9 %all-gather.2.cloned.1.call-start = ((), (), s32[]{:S(2)}) async-start(), calls=%async_computation | async-start | bytes 2621440 | tf_op jit(solution)/shard_map/all_gather | solution.py:144
Sparse Core Ops, SparseCore 0:
  49.0 36.6 all-gather.1

commit v6 on v5

--- a/solution.py
+++ b/solution.py
@@ -72,7 +72,7 @@
 
 def row_allreduce_times(x, t, n):
     rows, cols = x.shape
-    groups = (2, 4, n // 8)
+    groups = (2, min(4, n // 2), max(1, n // 8))
     g1, g2, g3 = groups
     p1 = rows // g1
     p2 = p1 // g2
@@ -101,31 +101,44 @@
 def _col_gather_kernel(n, v_ref, o_ref, send_sems, recv_sems):
     me = lax.axis_index("col")
     row = lax.axis_index("row")
-    w = v_ref.shape[1]
-    own = o_ref.at[:, pl.ds(pl.multiple_of(me * w, w), w)]
+    rows, w = v_ref.shape
+    half = rows // 2
+    left, right = lax.rem(me + n - 1, n), lax.rem(me + 1, n)
 
-    def copy(s):
+    def block(j):
+        return o_ref.at[:, pl.ds(pl.multiple_of(j * w, w), w)]
+
+    def send(src, dst, k, target):
         return pltpu.make_async_remote_copy(
-            src_ref=v_ref,
-            dst_ref=own,
-            send_sem=send_sems.at[s],
-            recv_sem=recv_sems.at[s],
-            device_id=(row, lax.rem(me + s, n)),
+            src_ref=src,
+            dst_ref=dst,
+            send_sem=send_sems.at[k],
+            recv_sem=recv_sems.at[k],
+            device_id=(row, target),
             device_id_type=pl.DeviceIdType.MESH,
         )
 
-    @pl.loop(1, n)
-    def _(s):
-        copy(s).start()
-
-    own[...] = v_ref[...]
-
-    @pl.loop(1, n)
-    def _(s):
-        copy(s).wait()
+    to_right = send(v_ref, block(me), 0, right)
+    to_left = send(v_ref, block(me), 1, left)
+    to_right.start()
+    to_left.start()
+    block(me)[...] = v_ref[...]
+    to_right.wait_recv()
+    from_left = block(left)
+    fwd_right = send(from_left.at[pl.ds(0, half), :], from_left.at[pl.ds(0, half), :], 2, right)
+    fwd_right.start()
+    to_left.wait_recv()
+    from_right = block(right)
+    fwd_left = send(from_right.at[pl.ds(half, half), :], from_right.at[pl.ds(half, half), :], 3, left)
+    fwd_left.start()
+    to_right.wait_send()
+    to_left.wait_send()
+    fwd_right.wait()
+    fwd_left.wait()
 
 
 def col_gather(v, n):
+    assert n == 4
     rows, w = v.shape
     return pl.pallas_call(
         functools.partial(_col_gather_kernel, n),

time: 168 us -> 164 us (0.976)
  Pallas kernels: 136 us -> 132 us
    pallas_call x1, Pallas kernels: 42.3 us -> 37.2 us  [col_gather(): pl.pallas_call(functools.partial(_col_gather_kernel, n), out_shape=jax.Sh...]
    pallas_call x2, Pallas kernels: 93.5 us -> 95.3 us  [row_allreduce_times(): pl.pallas_call(functools.partial(_allreduce_kernel, groups), out_shape=ja...]
  transfers between devices with their start and end apart: 1 -> 1, of which waited for: 0 -> 0; matrix products, arithmetic and copies ran while one was open for 5% -> 5% of each run, Pallas kernels for 28% -> 30%
where the time goes in v6:
time: 164 us
  Pallas kernels  132 us (80%)
  matrix products  18.2 us (11%)
  between operations  13.4 us (8%)
    pallas_call x2, Pallas kernels, row_allreduce_times(): pl.pallas_call(functools.partial(_allreduce_kernel, groups), out_shape=ja...  95.3 us
    pallas_call x1, Pallas kernels, col_gather(): pl.pallas_call(functools.partial(_col_gather_kernel, n), out_shape=jax.Sh...  37.2 us
    dot_general x2, matrix products, on_device(): lax.dot_general(vectors, applied_t, (((1,), (1,)), ((), ())), precision=l...  9.41 us
    dot_general x2, matrix products, on_device(): lax.dot_general(updated, vectors, (((0,), (0,)), ((), ())), precision=lax...  8.79 us
  transfers between devices with their start and end apart: 1, of which 0 were waited for; matrix products, arithmetic and copies ran while one was open for 5% of the time, Pallas kernels for 30%

profile of v6, /device:TPU:1, one launch (start us, length us, event | category | flops | bytes accessed | tf_op | source)
XLA Modules:
  0.0 164.2 jit_solution(10240889132245759753)
XLA Ops:
  6.5 0.0 copy-start
  6.5 0.0 all-gather.2.cloned.1.call-start
  6.5 37.2 %shard_map.55 = f32[1024,512]{1,0:T(8,128)} custom-call(f32[1024,128]{1,0:T(8,128)} %v_ref.1), custom_call_target="tpu_custom_call" | custom-call | bytes 4194304 | tf_op jit(solution)/shard_map/pallas_call | solution.py:143
  43.7 0.0 all-gather.2.cloned.1.call-update
  43.8 0.0 copy-done
  43.8 4.4 %convolution_bitcast_fusion.x_ref = f32[512,512]{1,0:T(8,128)} fusion(f32[1024,512]{1,0:T(8,128)} %shard_map.55, f32[1024,512]{1,0:T(8,128)S(1)} %copy-done), kind=kOutput, calls=%fused_computation.2 | convolution fusion | flops 1610612736 | bytes 5242880 | tf_op jit(solution)/shard_map/dot_general | solution.py:160
  48.2 49.5 %shard_map.56 = f32[512,512]{1,0:T(8,128)} custom-call(f32[512,512]{1,0:T(8,128)} %convolution_bitcast_fusion.x_ref, f32[512,512]{1,0:T(8,128)} %t_ref.2), custom_call_target="tpu_custom_call" | custom-call | flops 262144 | bytes 4194304 | tf_op jit(solution)/shard_map/pallas_call | solution.py:80
  97.6 4.4 %convolution_subtract_fusion.1 = f32[1024,512]{1,0:T(8,128)S(1)} fusion(f32[1024,512]{1,0:T(8,128)} %param.5, f32[1024,512]{1,0:T(8,128)} %shard_map.55, f32[512,512]{1,0:T(8,128)} %shard_map.56), kind=kOutput, calls=%fused_computation.1 | convolution fusion | flops 1611137024 | bytes 7340032 | tf_op jit(solution)/shard_map/dot_general | solution.py:162
  102.0 0.0 all-gather.2.cloned.1.call-done
  102.1 4.4 %fusion.x_ref = f32[512,512]{1,0:T(8,128)} fusion(f32[1024,512]{1,0:T(8,128)S(1)} %convolution_subtract_fusion.1, f32[1024,512]{1,0:T(8,128)} %all-gather.2.cloned.1.call-done), kind=kOutput, calls=%fused_computation.3 | convolution fusion | flops 1610612736 | bytes 5242880 | tf_op jit(solution)/shard_map/dot_general | solution.py:160
  106.5 45.8 %shard_map.57 = f32[512,512]{1,0:T(8,128)} custom-call(f32[512,512]{1,0:T(8,128)} %fusion.x_ref, f32[512,512]{1,0:T(8,128)} %t_ref.3), custom_call_target="tpu_custom_call" | custom-call | flops 262144 | bytes 4194304 | tf_op jit(solution)/shard_map/pallas_call | solution.py:80
  152.3 5.0 %convolution_subtract_fusion = f32[1024,512]{1,0:T(8,128)} fusion(f32[1024,512]{1,0:T(8,128)S(1)} %convolution_subtract_fusion.1, f32[1024,512]{1,0:T(8,128)} %all-gather.2.cloned.1.call-done, f32[512,512]{1,0:T(8,128)} %shard_map.57), kind=kOutput, calls=%fused_computation | convolution fusion | flops 1611137024 | bytes 7340032 | tf_op jit(solution)/shard_map/dot_general | solution.py:162
Async XLA Ops:
  6.5 37.2 %copy-start = (f32[1024,512]{1,0:T(8,128)S(1)}, f32[1024,512]{1,0:T(8,128)}, u32[]{:S(2)}) copy-start(f32[1024,512]{1,0:T(8,128)} %param.5) | copy-start | bytes 6291460
  6.5 95.5 %all-gather.2.cloned.1.call-start = ((), (), s32[]{:S(2)}) async-start(), calls=%async_computation | async-start | bytes 2621440 | tf_op jit(solution)/shard_map/all_gather | solution.py:157
Sparse Core Ops, SparseCore 0:
  43.9 38.4 all-gather.1

commit v7 on v6

--- a/solution.py
+++ b/solution.py
@@ -152,7 +152,10 @@
 
 
 def on_device(n_row, n_col, eigen_vectors, panel_first, panel_second, factor_first, factor_second):
-    vectors_second = col_gather(panel_second, n_col)
+    half = panel_second.shape[0] // 2
+    upper = lax.all_gather(panel_second[:half], "col", axis=1, tiled=True)
+    lower = col_gather(panel_second[half:], n_col)
+    vectors_second = jnp.concatenate([upper, lower], axis=0)
     vectors_second, panel_first = lax.optimization_barrier((vectors_second, panel_first))
     vectors_first = lax.all_gather(panel_first, "col", axis=1, tiled=True)
     updated = eigen_vectors

time: 164 us -> 168 us (1.024)
  waiting for transfers between devices: 0.04 us -> 4.25 us
  Pallas kernels: 132 us -> 128 us
  local copies, waits for them, and re-layouts: 0.01 us -> 1.85 us
  other arithmetic: 0 us -> 1.71 us
    all_gather x0 -> x1, waiting for transfers between devices: none -> 4.2 us  [on_device(): upper = lax.all_gather(panel_second[:half], 'col', axis=1, tiled=True)]
    pallas_call x1, Pallas kernels: 37.2 us -> 34.6 us  [col_gather(): pl.pallas_call(functools.partial(_col_gather_kernel, n), out_shape=jax.Sh...]
    pallas_call x2, Pallas kernels: 95.3 us -> 93.3 us  [row_allreduce_times(): pl.pallas_call(functools.partial(_allreduce_kernel, groups), out_shape=ja...]
    slice x0 -> x1, local copies, waits for them, and re-layouts: none -> 1.84 us  [on_device(): upper = lax.all_gather(panel_second[:half], 'col', axis=1, tiled=True)]
    concatenate x0 -> x1, other arithmetic: none -> 1.71 us  [on_device(): vectors_second = jnp.concatenate([upper, lower], axis=0)]
  transfers between devices with their start and end apart: 1 -> 2, of which waited for: 0 -> 1; matrix products, arithmetic and copies ran while one was open for 5% -> 6% of each run, Pallas kernels for 30% -> 49%
where the time goes in v7:
time: 168 us
  Pallas kernels  128 us (76%)
  matrix products  19 us (11%)
  between operations  13.5 us (8%)
  waiting for transfers between devices  4.25 us (3%)
  local copies, waits for them, and re-layouts  1.85 us (1%)
  other arithmetic  1.71 us (1%)
    pallas_call x2, Pallas kernels, row_allreduce_times(): pl.pallas_call(functools.partial(_allreduce_kernel, groups), out_shape=ja...  93.3 us
    pallas_call x1, Pallas kernels, col_gather(): pl.pallas_call(functools.partial(_col_gather_kernel, n), out_shape=jax.Sh...  34.6 us
    dot_general x2, matrix products, on_device(): lax.dot_general(updated, vectors, (((0,), (0,)), ((), ())), precision=lax...  9.57 us
    dot_general x2, matrix products, on_device(): lax.dot_general(vectors, applied_t, (((1,), (1,)), ((), ())), precision=l...  9.41 us
    all_gather x1, waiting for transfers between devices, on_device(): upper = lax.all_gather(panel_second[:half], 'col', axis=1, tiled=True)  4.2 us
  transfers between devices with their start and end apart: 2, of which 1 were waited for; matrix products, arithmetic and copies ran while one was open for 6% of the time, Pallas kernels for 49%

profile of v7, /device:TPU:1, one launch (start us, length us, event | category | flops | bytes accessed | tf_op | source)
XLA Modules:
  0.0 168.2 jit_solution(12111222448345665228)
XLA Ops:
  6.5 0.0 all-gather.3.cloned.1.call-start
  6.5 1.8 %fusion = (f32[512,128]{1,0:T(8,128)}, f32[512,128]{1,0:T(8,128)}) fusion(f32[1024,128]{1,0:T(8,128)} %param.7), kind=kLoop, calls=%fused_computation.4 | loop fusion | bytes 1048576 | tf_op jit(solution)/shard_map/slice | solution.py:156
  8.4 0.0 all-gather.3.cloned.1.call-update
  8.4 0.0 all-gather.5.cloned.1.call-start
  8.5 34.6 %shard_map.55 = f32[512,512]{1,0:T(8,128)} custom-call(f32[512,128]{1,0:T(8,128)} %get-tuple-element.10.v_ref), custom_call_target="tpu_custom_call" | custom-call | bytes 2097152 | tf_op jit(solution)/shard_map/pallas_call | solution.py:143
  43.1 4.2 %all-gather.3.cloned.1.call-done = f32[512,512]{1,0:T(8,128)} async-done(((f32[512,128]{1,0:T(8,128)}), f32[512,512]{1,0:T(8,128)}) %all-gather.3.cloned.1.call-update) | async-done | bytes 1048592 | tf_op jit(solution)/shard_map/all_gather | solution.py:156
  47.3 1.7 %pad_maximum_fusion = f32[1024,512]{1,0:T(8,128)S(1)} fusion(f32[512,512]{1,0:T(8,128)} %shard_map.55, f32[512,512]{1,0:T(8,128)} %all-gather.3.cloned.1.call-done), kind=kLoop, calls=%fused_computation | loop fusion | flops 524288 | bytes 4194304 | tf_op jit(solution)/shard_map/concatenate | solution.py:158
  49.0 0.0 copy-start
  49.0 0.0 all-gather.5.cloned.1.call-update
  49.0 5.2 %convolution_bitcast_fusion.x_ref = f32[512,512]{1,0:T(8,128)} fusion(f32[1024,512]{1,0:T(8,128)S(1)} %pad_maximum_fusion, f32[1024,512]{1,0:T(8,128)} %param.5), kind=kOutput, calls=%fused_computation.3 | convolution fusion | flops 1610612736 | bytes 5242880 | tf_op jit(solution)/shard_map/dot_general | solution.py:163
  54.2 0.0 copy-done
  54.2 47.5 %shard_map.56 = f32[512,512]{1,0:T(8,128)} custom-call(f32[512,512]{1,0:T(8,128)} %convolution_bitcast_fusion.x_ref, f32[512,512]{1,0:T(8,128)} %t_ref.2), custom_call_target="tpu_custom_call" | custom-call | flops 262144 | bytes 4194304 | tf_op jit(solution)/shard_map/pallas_call | solution.py:80
  101.7 4.4 %convolution_subtract_fusion.1 = f32[1024,512]{1,0:T(8,128)S(1)} fusion(f32[1024,512]{1,0:T(8,128)} %param.5, f32[1024,512]{1,0:T(8,128)} %copy-done, f32[512,512]{1,0:T(8,128)} %shard_map.56), kind=kOutput, calls=%fused_computation.2 | convolution fusion | flops 1611137024 | bytes 7340032 | tf_op jit(solution)/shard_map/dot_general | solution.py:165
  106.1 0.0 all-gather.5.cloned.1.call-done
  106.1 4.4 %fusion.1.x_ref = f32[512,512]{1,0:T(8,128)} fusion(f32[1024,512]{1,0:T(8,128)S(1)} %convolution_subtract_fusion.1, f32[1024,512]{1,0:T(8,128)} %all-gather.5.cloned.1.call-done), kind=kOutput, calls=%fused_computation.5 | convolution fusion | flops 1610612736 | bytes 5242880 | tf_op jit(solution)/shard_map/dot_general | solution.py:163
  110.5 45.8 %shard_map.57 = f32[512,512]{1,0:T(8,128)} custom-call(f32[512,512]{1,0:T(8,128)} %fusion.1.x_ref, f32[512,512]{1,0:T(8,128)} %t_ref.3), custom_call_target="tpu_custom_call" | custom-call | flops 262144 | bytes 4194304 | tf_op jit(solution)/shard_map/pallas_call | solution.py:80
  156.3 5.0 %convolution_subtract_fusion = f32[1024,512]{1,0:T(8,128)} fusion(f32[1024,512]{1,0:T(8,128)S(1)} %convolution_subtract_fusion.1, f32[1024,512]{1,0:T(8,128)} %all-gather.5.cloned.1.call-done, f32[512,512]{1,0:T(8,128)} %shard_map.57), kind=kOutput, calls=%fused_computation.1 | convolution fusion | flops 1611137024 | bytes 7340032 | tf_op jit(solution)/shard_map/dot_general | solution.py:165
Async XLA Ops:
  6.5 40.7 %all-gather.3.cloned.1.call-start = ((), (), s32[]{:S(2)}) async-start(), calls=%async_computation | async-start | bytes 1310720 | tf_op jit(solution)/shard_map/all_gather | solution.py:156
  8.4 97.7 %all-gather.5.cloned.1.call-start = ((), (), s32[]{:S(2)}) async-start(), calls=%async_computation.1 | async-start | bytes 2621440 | tf_op jit(solution)/shard_map/all_gather | solution.py:160
  49.0 5.2 %copy-start = (f32[1024,512]{1,0:T(8,128)}, f32[1024,512]{1,0:T(8,128)S(1)}, u32[]{:S(2)}) copy-start(f32[1024,512]{1,0:T(8,128)S(1)} %pad_maximum_fusion) | copy-start | bytes 6291460
Sparse Core Ops, SparseCore 0:
  9.2 38.0 all-gather.2
  49.1 36.4 all-gather.4

commit v8 on v6

--- a/solution.py
+++ b/solution.py
@@ -28,6 +28,16 @@
 
     def rows_of(ref, start, size):
         return ref.at[pl.ds(pl.multiple_of(start, size), size), :]
+
+    barrier = pltpu.get_barrier_semaphore()
+    for g, stride, mine in ((g1, s1, i1), (g2, s2, i2), (g3, s3, i3)):
+
+        @pl.loop(1, g)
+        def _(s):
+            j = lax.rem(mine + s, g)
+            pl.semaphore_signal(barrier, inc=1, device_id=(me + (j - mine) * stride, col), device_id_type=mesh_id)
+
+    pl.semaphore_wait(barrier, g1 + g2 + g3 - 3)
 
     def exchange(stage, g, stride, mine, src_of, dst_of):
         def copy(s):
@@ -70,7 +80,7 @@
     gather_stage(5, g1, s1, i1, 0, p1)
 
 
-def row_allreduce_times(x, t, n):
+def row_allreduce_times(x, t, n, collective_id):
     rows, cols = x.shape
     groups = (2, min(4, n // 2), max(1, n // 8))
     g1, g2, g3 = groups
@@ -91,7 +101,7 @@
             pltpu.SemaphoreType.DMA((6, max(groups))),
             pltpu.SemaphoreType.DMA((6, max(groups))),
         ],
-        compiler_params=pltpu.CompilerParams(has_side_effects=True),
+        compiler_params=pltpu.CompilerParams(has_side_effects=True, collective_id=collective_id),
         cost_estimate=pl.CostEstimate(
             flops=rows * cols, transcendentals=0, bytes_accessed=4 * rows * cols * 4
         ),
@@ -117,6 +127,11 @@
             device_id=(row, target),
             device_id_type=pl.DeviceIdType.MESH,
         )
+
+    barrier = pltpu.get_barrier_semaphore()
+    for target in (left, right):
+        pl.semaphore_signal(barrier, inc=1, device_id=(row, target), device_id_type=pl.DeviceIdType.MESH)
+    pl.semaphore_wait(barrier, 2)
 
     to_right = send(v_ref, block(me), 0, right)
     to_left = send(v_ref, block(me), 1, left)
@@ -146,7 +161,7 @@
         in_specs=[pl.BlockSpec(memory_space=pltpu.VMEM)],
         out_specs=pl.BlockSpec(memory_space=pltpu.VMEM),
         scratch_shapes=[pltpu.SemaphoreType.DMA((n,)), pltpu.SemaphoreType.DMA((n,))],
-        compiler_params=pltpu.CompilerParams(has_side_effects=True),
+        compiler_params=pltpu.CompilerParams(has_side_effects=True, collective_id=0),
         cost_estimate=pl.CostEstimate(flops=0, transcendentals=0, bytes_accessed=2 * rows * w * n * 4),
     )(v)
 
@@ -156,9 +171,9 @@
     vectors_second, panel_first = lax.optimization_barrier((vectors_second, panel_first))
     vectors_first = lax.all_gather(panel_first, "col", axis=1, tiled=True)
     updated = eigen_vectors
-    for vectors, factor in ((vectors_second, factor_second), (vectors_first, factor_first)):
+    for collective_id, vectors, factor in ((1, vectors_second, factor_second), (2, vectors_first, factor_first)):
         partial_t = lax.dot_general(updated, vectors, (((0,), (0,)), ((), ())), precision=lax.Precision.HIGH, preferred_element_type=jnp.float32)
-        applied_t = row_allreduce_times(partial_t, factor, n_row)
+        applied_t = row_allreduce_times(partial_t, factor, n_row, collective_id)
         updated = updated - lax.dot_general(vectors, applied_t, (((1,), (1,)), ((), ())), precision=lax.Precision.HIGH, preferred_element_type=jnp.float32)
     return updated
 

time: 164 us -> 136 us (0.83)
  Pallas kernels: 132 us -> 105 us
    pallas_call x2, Pallas kernels: 95.3 us -> 80.6 us  [row_allreduce_times(): pl.pallas_call(functools.partial(_allreduce_kernel, groups), out_shape=ja...]
    pallas_call x1, Pallas kernels: 37.2 us -> 23.9 us  [col_gather(): pl.pallas_call(functools.partial(_col_gather_kernel, n), out_shape=jax.Sh...]
  transfers between devices with their start and end apart: 1 -> 1, of which waited for: 0 -> 0; matrix products, arithmetic and copies ran while one was open for 5% -> 6% of each run, Pallas kernels for 30% -> 32%
where the time goes in v8:
time: 136 us
  Pallas kernels  105 us (77%)
  matrix products  18.2 us (13%)
  between operations  13.4 us (10%)
    pallas_call x2, Pallas kernels, row_allreduce_times(): pl.pallas_call(functools.partial(_allreduce_kernel, groups), out_shape=ja...  80.6 us
    pallas_call x1, Pallas kernels, col_gather(): pl.pallas_call(functools.partial(_col_gather_kernel, n), out_shape=jax.Sh...  23.9 us
    dot_general x2, matrix products, on_device(): lax.dot_general(vectors, applied_t, (((1,), (1,)), ((), ())), precision=l...  9.41 us
    dot_general x2, matrix products, on_device(): lax.dot_general(updated, vectors, (((0,), (0,)), ((), ())), precision=lax...  8.8 us
  transfers between devices with their start and end apart: 1, of which 0 were waited for; matrix products, arithmetic and copies ran while one was open for 6% of the time, Pallas kernels for 32%

profile of v8, /device:TPU:1, one launch (start us, length us, event | category | flops | bytes accessed | tf_op | source)
XLA Modules:
  0.0 136.3 jit_solution(2680138929856265914)
XLA Ops:
  6.5 0.0 copy-start
  6.5 0.0 all-gather.2.cloned.1.call-start
  6.5 23.9 %shard_map.55 = f32[1024,512]{1,0:T(8,128)} custom-call(f32[1024,128]{1,0:T(8,128)} %v_ref.1), custom_call_target="tpu_custom_call" | custom-call | bytes 4194304 | tf_op jit(solution)/shard_map/pallas_call | solution.py:158
  30.5 0.0 all-gather.2.cloned.1.call-update
  30.5 0.0 copy-done
  30.5 4.4 %convolution_bitcast_fusion.x_ref = f32[512,512]{1,0:T(8,128)} fusion(f32[1024,512]{1,0:T(8,128)} %shard_map.55, f32[1024,512]{1,0:T(8,128)S(1)} %copy-done), kind=kOutput, calls=%fused_computation.2 | convolution fusion | flops 1610612736 | bytes 5242880 | tf_op jit(solution)/shard_map/dot_general | solution.py:175
  34.9 44.1 %shard_map.56 = f32[512,512]{1,0:T(8,128)} custom-call(f32[512,512]{1,0:T(8,128)} %convolution_bitcast_fusion.x_ref, f32[512,512]{1,0:T(8,128)} %t_ref.2), custom_call_target="tpu_custom_call" | custom-call | flops 262144 | bytes 4194304 | tf_op jit(solution)/shard_map/pallas_call | solution.py:90
  79.0 4.4 %convolution_subtract_fusion.1 = f32[1024,512]{1,0:T(8,128)S(1)} fusion(f32[1024,512]{1,0:T(8,128)} %param.5, f32[1024,512]{1,0:T(8,128)} %shard_map.55, f32[512,512]{1,0:T(8,128)} %shard_map.56), kind=kOutput, calls=%fused_computation.1 | convolution fusion | flops 1611137024 | bytes 7340032 | tf_op jit(solution)/shard_map/dot_general | solution.py:177
  83.4 0.0 all-gather.2.cloned.1.call-done
  83.5 4.4 %fusion.x_ref = f32[512,512]{1,0:T(8,128)} fusion(f32[1024,512]{1,0:T(8,128)S(1)} %convolution_subtract_fusion.1, f32[1024,512]{1,0:T(8,128)} %all-gather.2.cloned.1.call-done), kind=kOutput, calls=%fused_computation.3 | convolution fusion | flops 1610612736 | bytes 5242880 | tf_op jit(solution)/shard_map/dot_general | solution.py:175
  87.9 36.5 %shard_map.57 = f32[512,512]{1,0:T(8,128)} custom-call(f32[512,512]{1,0:T(8,128)} %fusion.x_ref, f32[512,512]{1,0:T(8,128)} %t_ref.3), custom_call_target="tpu_custom_call" | custom-call | flops 262144 | bytes 4194304 | tf_op jit(solution)/shard_map/pallas_call | solution.py:90
  124.4 5.0 %convolution_subtract_fusion = f32[1024,512]{1,0:T(8,128)} fusion(f32[1024,512]{1,0:T(8,128)S(1)} %convolution_subtract_fusion.1, f32[1024,512]{1,0:T(8,128)} %all-gather.2.cloned.1.call-done, f32[512,512]{1,0:T(8,128)} %shard_map.57), kind=kOutput, calls=%fused_computation | convolution fusion | flops 1611137024 | bytes 7340032 | tf_op jit(solution)/shard_map/dot_general | solution.py:177
Async XLA Ops:
  6.5 24.0 %copy-start = (f32[1024,512]{1,0:T(8,128)S(1)}, f32[1024,512]{1,0:T(8,128)}, u32[]{:S(2)}) copy-start(f32[1024,512]{1,0:T(8,128)} %param.5) | copy-start | bytes 6291460
  6.5 76.9 %all-gather.2.cloned.1.call-start = ((), (), s32[]{:S(2)}) async-start(), calls=%async_computation | async-start | bytes 2621440 | tf_op jit(solution)/shard_map/all_gather | solution.py:172
Sparse Core Ops, SparseCore 0:
  30.6 40.1 all-gather.1

commit v9 on v8

--- a/solution.py
+++ b/solution.py
@@ -12,7 +12,7 @@
     return jnp.dot(left, right, precision=lax.Precision.HIGHEST, preferred_element_type=jnp.float32)
 
 
-def _allreduce_kernel(groups, x_ref, t_ref, o_ref, buf1, buf2, recv1, recv2, recv3, send_sems, recv_sems):
+def _allreduce_kernel(groups, nc, x_ref, t_ref, o_ref, buf1, buf2, red, recv1, recv2, recv3, send_sems, recv_sems):
     me = lax.axis_index("row")
     col = lax.axis_index("col")
     g1, g2, g3 = groups
@@ -20,14 +20,15 @@
     i1 = lax.rem(me, g1)
     i2 = lax.rem(me // s2, g2)
     i3 = me // s3
-    rows = x_ref.shape[0]
+    rows, cols = x_ref.shape
+    cw = cols // nc
     p1 = rows // g1
     p2 = p1 // g2
     p3 = p2 // g3
     mesh_id = pl.DeviceIdType.MESH
 
-    def rows_of(ref, start, size):
-        return ref.at[pl.ds(pl.multiple_of(start, size), size), :]
+    def part(ref, start, size, c):
+        return ref.at[pl.ds(pl.multiple_of(start, size), size), pl.ds(c * cw, cw)]
 
     barrier = pltpu.get_barrier_semaphore()
     for g, stride, mine in ((g1, s1, i1), (g2, s2, i2), (g3, s3, i3)):
@@ -39,48 +40,78 @@
 
     pl.semaphore_wait(barrier, g1 + g2 + g3 - 3)
 
-    def exchange(stage, g, stride, mine, src_of, dst_of):
+    def exchange(stage, c, g, stride, mine, src_of, dst_of):
         def copy(s):
             j = lax.rem(mine + s, g)
             return pltpu.make_async_remote_copy(
                 src_ref=src_of(j),
                 dst_ref=dst_of(j, s),
-                send_sem=send_sems.at[stage, s],
-                recv_sem=recv_sems.at[stage, s],
+                send_sem=send_sems.at[stage, c, s],
+                recv_sem=recv_sems.at[stage, c, s],
                 device_id=(me + (j - mine) * stride, col),
                 device_id_type=mesh_id,
             )
 
-        @pl.loop(1, g)
-        def _(s):
-            copy(s).start()
-
-        @pl.loop(1, g)
-        def _(s):
-            copy(s).wait()
-
-    def reduce_stage(stage, g, stride, mine, src, piece, recv):
-        exchange(stage, g, stride, mine, lambda j: rows_of(src, j * piece, piece), lambda j, s: recv.at[s])
-        return lax.fori_loop(1, g, lambda s, acc: acc + recv[s], src[pl.ds(pl.multiple_of(mine * piece, piece), piece), :])
-
-    buf1[...] = reduce_stage(0, g1, s1, i1, x_ref, p1, recv1)
-    buf2[...] = reduce_stage(1, g2, s2, i2, buf1, p2, recv2)
+        def start():
+            @pl.loop(1, g)
+            def _(s):
+                copy(s).start()
+
+        def finish():
+            @pl.loop(1, g)
+            def _(s):
+                copy(s).wait()
+
+        return start, finish
+
+    reduce_plan = (
+        (0, g1, s1, i1, x_ref, p1, recv1, buf1),
+        (1, g2, s2, i2, buf1, p2, recv2, buf2),
+        (2, g3, s3, i3, buf2, p3, recv3, red),
+    )
+
+    def reduce_stage(stage, g, stride, mine, src, piece, recv, dst, c):
+        start, finish = exchange(
+            stage, c, g, stride, mine,
+            lambda j: part(src, j * piece, piece, c),
+            lambda j, s: recv.at[s, :, pl.ds(c * cw, cw)],
+        )
+
+        def combine():
+            finish()
+            own = src[pl.ds(pl.multiple_of(mine * piece, piece), piece), pl.ds(c * cw, cw)]
+            dst[:, pl.ds(c * cw, cw)] = lax.fori_loop(1, g, lambda s, acc: acc + recv[s, :, pl.ds(c * cw, cw)], own)
+
+        return start, combine
+
+    def run(plan):
+        for c in range(nc):
+            plan[0](c)[0]()
+        for k in range(len(plan)):
+            for c in range(nc):
+                plan[k](c)[1]()
+                if k + 1 < len(plan):
+                    plan[k + 1](c)[0]()
+
+    run([functools.partial(reduce_stage, *p) for p in reduce_plan])
+
     base3 = i1 * p1 + i2 * p2
-    reduced = reduce_stage(2, g3, s3, i3, buf2, p3, recv3)
     o_ref[pl.ds(pl.multiple_of(base3 + i3 * p3, p3), p3), :] = lax.dot_general(
-        reduced, t_ref[...], (((1,), (1,)), ((), ())), precision=lax.Precision.HIGHEST, preferred_element_type=jnp.float32
+        red[...], t_ref[...], (((1,), (1,)), ((), ())), precision=lax.Precision.HIGHEST, preferred_element_type=jnp.float32
     )
 
-    def gather_stage(stage, g, stride, mine, base, block):
-        own = rows_of(o_ref, base + mine * block, block)
-        exchange(stage, g, stride, mine, lambda j: own, lambda j, s: own)
-
-    gather_stage(3, g3, s3, i3, base3, p3)
-    gather_stage(4, g2, s2, i2, i1 * p1, p2)
-    gather_stage(5, g1, s1, i1, 0, p1)
-
-
-def row_allreduce_times(x, t, n, collective_id):
+    def gather_stage(stage, g, stride, mine, base, block, c):
+        own = part(o_ref, base + mine * block, block, c)
+        return exchange(stage, c, g, stride, mine, lambda j: own, lambda j, s: own)
+
+    run([
+        functools.partial(gather_stage, 3, g3, s3, i3, base3, p3),
+        functools.partial(gather_stage, 4, g2, s2, i2, i1 * p1, p2),
+        functools.partial(gather_stage, 5, g1, s1, i1, 0, p1),
+    ])
+
+
+def row_allreduce_times(x, t, n, collective_id, nc=2):
     rows, cols = x.shape
     groups = (2, min(4, n // 2), max(1, n // 8))
     g1, g2, g3 = groups
@@ -88,18 +119,19 @@
     p2 = p1 // g2
     p3 = p2 // g3
     return pl.pallas_call(
-        functools.partial(_allreduce_kernel, groups),
+        functools.partial(_allreduce_kernel, groups, nc),
         out_shape=jax.ShapeDtypeStruct((rows, cols), x.dtype),
         in_specs=[pl.BlockSpec(memory_space=pltpu.VMEM)] * 2,
         out_specs=pl.BlockSpec(memory_space=pltpu.VMEM),
         scratch_shapes=[
             pltpu.VMEM((p1, cols), x.dtype),
             pltpu.VMEM((p2, cols), x.dtype),
+            pltpu.VMEM((p3, cols), x.dtype),
             pltpu.VMEM((g1, p1, cols), x.dtype),
             pltpu.VMEM((g2, p2, cols), x.dtype),
             pltpu.VMEM((g3, p3, cols), x.dtype),
-            pltpu.SemaphoreType.DMA((6, max(groups))),
-            pltpu.SemaphoreType.DMA((6, max(groups))),
+            pltpu.SemaphoreType.DMA((6, nc, max(groups))),
+            pltpu.SemaphoreType.DMA((6, nc, max(groups))),
         ],
         compiler_params=pltpu.CompilerParams(has_side_effects=True, collective_id=collective_id),
         cost_estimate=pl.CostEstimate(

time: 136 us -> 134 us (0.985)
  Pallas kernels: 105 us -> 102 us
    pallas_call x2, Pallas kernels: 80.6 us -> 77.9 us  [row_allreduce_times(): pl.pallas_call(functools.partial(_allreduce_kernel, groups, nc), out_shap...]
  transfers between devices with their start and end apart: 1 -> 1, of which waited for: 0 -> 0; matrix products, arithmetic and copies ran while one was open for 6% -> 7% of each run, Pallas kernels for 32% -> 32%
where the time goes in v9:
time: 134 us
  Pallas kernels  102 us (76%)
  matrix products  18.2 us (14%)
  between operations  13.4 us (10%)
    pallas_call x2, Pallas kernels, row_allreduce_times(): pl.pallas_call(functools.partial(_allreduce_kernel, groups, nc), out_shap...  77.9 us
    pallas_call x1, Pallas kernels, col_gather(): pl.pallas_call(functools.partial(_col_gather_kernel, n), out_shape=jax.Sh...  23.9 us
    dot_general x2, matrix products, on_device(): lax.dot_general(vectors, applied_t, (((1,), (1,)), ((), ())), precision=l...  9.41 us
    dot_general x2, matrix products, on_device(): lax.dot_general(updated, vectors, (((0,), (0,)), ((), ())), precision=lax...  8.8 us
  transfers between devices with their start and end apart: 1, of which 0 were waited for; matrix products, arithmetic and copies ran while one was open for 7% of the time, Pallas kernels for 32%

profile of v9, /device:TPU:1, one launch (start us, length us, event | category | flops | bytes accessed | tf_op | source)
XLA Modules:
  0.0 133.5 jit_solution(3684063679813916149)
XLA Ops:
  6.5 0.0 copy-start
  6.5 0.0 all-gather.2.cloned.1.call-start
  6.5 23.9 %shard_map.55 = f32[1024,512]{1,0:T(8,128)} custom-call(f32[1024,128]{1,0:T(8,128)} %v_ref.1), custom_call_target="tpu_custom_call" | custom-call | bytes 4194304 | tf_op jit(solution)/shard_map/pallas_call | solution.py:190
  30.5 0.0 all-gather.2.cloned.1.call-update
  30.5 0.0 copy-done
  30.5 4.4 %convolution_bitcast_fusion.x_ref = f32[512,512]{1,0:T(8,128)} fusion(f32[1024,512]{1,0:T(8,128)} %shard_map.55, f32[1024,512]{1,0:T(8,128)S(1)} %copy-done), kind=kOutput, calls=%fused_computation.2 | convolution fusion | flops 1610612736 | bytes 5242880 | tf_op jit(solution)/shard_map/dot_general | solution.py:207
  34.9 42.8 %shard_map.56 = f32[512,512]{1,0:T(8,128)} custom-call(f32[512,512]{1,0:T(8,128)} %convolution_bitcast_fusion.x_ref, f32[512,512]{1,0:T(8,128)} %t_ref.2), custom_call_target="tpu_custom_call" | custom-call | flops 262144 | bytes 4194304 | tf_op jit(solution)/shard_map/pallas_call | solution.py:121
  77.8 4.4 %convolution_subtract_fusion.1 = f32[1024,512]{1,0:T(8,128)S(1)} fusion(f32[1024,512]{1,0:T(8,128)} %param.5, f32[1024,512]{1,0:T(8,128)} %shard_map.55, f32[512,512]{1,0:T(8,128)} %shard_map.56), kind=kOutput, calls=%fused_computation.1 | convolution fusion | flops 1611137024 | bytes 7340032 | tf_op jit(solution)/shard_map/dot_general | solution.py:209
  82.2 0.0 all-gather.2.cloned.1.call-done
  82.2 4.4 %fusion.x_ref = f32[512,512]{1,0:T(8,128)} fusion(f32[1024,512]{1,0:T(8,128)S(1)} %convolution_subtract_fusion.1, f32[1024,512]{1,0:T(8,128)} %all-gather.2.cloned.1.call-done), kind=kOutput, calls=%fused_computation.3 | convolution fusion | flops 1610612736 | bytes 5242880 | tf_op jit(solution)/shard_map/dot_general | solution.py:207
  86.6 35.1 %shard_map.57 = f32[512,512]{1,0:T(8,128)} custom-call(f32[512,512]{1,0:T(8,128)} %fusion.x_ref, f32[512,512]{1,0:T(8,128)} %t_ref.3), custom_call_target="tpu_custom_call" | custom-call | flops 262144 | bytes 4194304 | tf_op jit(solution)/shard_map/pallas_call | solution.py:121
  121.7 5.0 %convolution_subtract_fusion = f32[1024,512]{1,0:T(8,128)} fusion(f32[1024,512]{1,0:T(8,128)S(1)} %convolution_subtract_fusion.1, f32[1024,512]{1,0:T(8,128)} %all-gather.2.cloned.1.call-done, f32[512,512]{1,0:T(8,128)} %shard_map.57), kind=kOutput, calls=%fused_computation | convolution fusion | flops 1611137024 | bytes 7340032 | tf_op jit(solution)/shard_map/dot_general | solution.py:209
Async XLA Ops:
  6.5 24.0 %copy-start = (f32[1024,512]{1,0:T(8,128)S(1)}, f32[1024,512]{1,0:T(8,128)}, u32[]{:S(2)}) copy-start(f32[1024,512]{1,0:T(8,128)} %param.5) | copy-start | bytes 6291460
  6.5 75.7 %all-gather.2.cloned.1.call-start = ((), (), s32[]{:S(2)}) async-start(), calls=%async_computation | async-start | bytes 2621440 | tf_op jit(solution)/shard_map/all_gather | solution.py:204
Sparse Core Ops, SparseCore 0:
  30.6 40.1 all-gather.1

commit v10 on v9

--- a/solution.py
+++ b/solution.py
@@ -200,7 +200,6 @@
 
 def on_device(n_row, n_col, eigen_vectors, panel_first, panel_second, factor_first, factor_second):
     vectors_second = col_gather(panel_second, n_col)
-    vectors_second, panel_first = lax.optimization_barrier((vectors_second, panel_first))
     vectors_first = lax.all_gather(panel_first, "col", axis=1, tiled=True)
     updated = eigen_vectors
     for collective_id, vectors, factor in ((1, vectors_second, factor_second), (2, vectors_first, factor_first)):

time: 134 us -> 145 us (1.082)
  Pallas kernels: 102 us -> 107 us
  local copies, waits for them, and re-layouts: 0.01 us -> 4.7 us
    pallas_call x2, Pallas kernels: 77.9 us -> 83.2 us  [row_allreduce_times(): pl.pallas_call(functools.partial(_allreduce_kernel, groups, nc), out_shap...]
    sub x0 -> x1, local copies, waits for them, and re-layouts: none -> 2.88 us  [on_device(): updated - lax.dot_general(vectors, applied_t, (((1,), (1,)), ((), ())), p...]
    unnamed x2 -> x5, local copies, waits for them, and re-layouts: 0.01 us -> 1.82 us
  transfers between devices with their start and end apart: 1 -> 1, of which waited for: 0 -> 0; matrix products, arithmetic and copies ran while one was open for 7% -> 7% of each run, Pallas kernels for 32% -> 50%
where the time goes in v10:
time: 145 us; the launch traced here: 144 us
  Pallas kernels  107 us (74%)
  matrix products  17.9 us (12%)
  between operations  13.4 us (9%)
  local copies, waits for them, and re-layouts  4.7 us (3%)
    pallas_call x2, Pallas kernels, row_allreduce_times(): pl.pallas_call(functools.partial(_allreduce_kernel, groups, nc), out_shap...  83.2 us
    pallas_call x1, Pallas kernels, col_gather(): pl.pallas_call(functools.partial(_col_gather_kernel, n), out_shape=jax.Sh...  24.3 us
    dot_general x2, matrix products, on_device(): lax.dot_general(vectors, applied_t, (((1,), (1,)), ((), ())), precision=l...  9.15 us
    dot_general x2, matrix products, on_device(): lax.dot_general(updated, vectors, (((0,), (0,)), ((), ())), precision=lax...  8.8 us
  transfers between devices with their start and end apart: 1, of which 0 were waited for; matrix products, arithmetic and copies ran while one was open for 7% of the time, Pallas kernels for 50%

profile of v10, /device:TPU:1, one launch (start us, length us, event | category | flops | bytes accessed | tf_op | source)
XLA Modules:
  0.0 144.3 jit_solution(8321137233300259210)
XLA Ops:
  6.5 0.0 copy-start
  6.5 0.0 all-gather.2.cloned.1.call-start
  6.5 0.7 all-gather.2.cloned.1.call-update
  7.3 24.3 %shard_map.55 = f32[1024,512]{1,0:T(8,128)} custom-call(f32[1024,128]{1,0:T(8,128)} %v_ref.1), custom_call_target="tpu_custom_call" | custom-call | bytes 4194304 | tf_op jit(solution)/shard_map/pallas_call | solution.py:190
  31.5 0.0 copy-done
  31.6 4.4 %fusion.x_ref = f32[512,512]{1,0:T(8,128)} fusion(f32[1024,512]{1,0:T(8,128)S(1)} %copy-done, f32[1024,512]{1,0:T(8,128)} %shard_map.55), kind=kOutput, calls=%fused_computation.2 | convolution fusion | flops 1610612736 | bytes 5242880 | tf_op jit(solution)/shard_map/dot_general | solution.py:206
  36.0 48.1 %shard_map.56 = f32[512,512]{1,0:T(8,128)} custom-call(f32[512,512]{1,0:T(8,128)} %fusion.x_ref, f32[512,512]{1,0:T(8,128)} %t_ref.2), custom_call_target="tpu_custom_call" | custom-call | flops 262144 | bytes 4194304 | tf_op jit(solution)/shard_map/pallas_call | solution.py:121
  84.0 0.0 copy-start.1
  84.0 1.8 %copy.6 = f32[1024,512]{0,1:T(8,128)} copy(f32[1024,512]{1,0:T(8,128)S(1)} %copy-done) | data formatting | bytes 4194304 | tf_op args[0]
  85.9 0.0 copy-done.1
  85.9 4.1 %bitcast_subtract_fusion.1 = f32[1024,512]{0,1:T(8,128)S(1)} fusion(f32[1024,512]{0,1:T(8,128)} %copy.6, f32[512,512]{1,0:T(8,128)S(1)} %copy-done.1, f32[1024,512]{1,0:T(8,128)} %shard_map.55), kind=kOutput, calls=%fused_computation.1 | convolution fusion | flops 1611137024 | bytes 7340032 | tf_op jit(solution)/shard_map/dot_general | solution.py:208
  89.9 0.0 all-gather.2.cloned.1.call-done
  90.0 4.4 %fusion.1.x_ref = f32[512,512]{1,0:T(8,128)} fusion(f32[1024,512]{0,1:T(8,128)S(1)} %bitcast_subtract_fusion.1, f32[1024,512]{1,0:T(8,128)} %all-gather.2.cloned.1.call-done), kind=kOutput, calls=%fused_computation.3 | convolution fusion | flops 1610612736 | bytes 5242880 | tf_op jit(solution)/shard_map/dot_general | solution.py:206
  94.4 35.1 %shard_map.57 = f32[512,512]{1,0:T(8,128)} custom-call(f32[512,512]{1,0:T(8,128)} %fusion.1.x_ref, f32[512,512]{1,0:T(8,128)} %t_ref.3), custom_call_target="tpu_custom_call" | custom-call | flops 262144 | bytes 4194304 | tf_op jit(solution)/shard_map/pallas_call | solution.py:121
  129.5 5.1 %bitcast_subtract_fusion = f32[1024,512]{0,1:T(8,128)} fusion(f32[1024,512]{0,1:T(8,128)S(1)} %bitcast_subtract_fusion.1, f32[512,512]{1,0:T(8,128)} %shard_map.57, f32[1024,512]{1,0:T(8,128)} %all-gather.2.cloned.1.call-done), kind=kOutput, calls=%fused_computation | convolution fusion | flops 1611137024 | bytes 7340032 | tf_op jit(solution)/shard_map/dot_general | solution.py:208
  134.6 2.9 %copy.7 = f32[1024,512]{1,0:T(8,128)} copy(f32[1024,512]{0,1:T(8,128)} %bitcast_subtract_fusion) | data formatting | bytes 4194304 | tf_op jit(solution)/shard_map/sub | solution.py:208
Async XLA Ops:
  6.5 25.0 %copy-start = (f32[1024,512]{1,0:T(8,128)S(1)}, f32[1024,512]{1,0:T(8,128)}, u32[]{:S(2)}) copy-start(f32[1024,512]{1,0:T(8,128)} %param.5) | copy-start | bytes 6291460
  6.5 83.4 %all-gather.2.cloned.1.call-start = ((), (), s32[]{:S(2)}) async-start(), calls=%async_computation | async-start | bytes 2621440 | tf_op jit(solution)/shard_map/all_gather | solution.py:203
  84.0 1.8 %copy-start.1 = (f32[512,512]{1,0:T(8,128)S(1)}, f32[512,512]{1,0:T(8,128)}, u32[]{:S(2)}) copy-start(f32[512,512]{1,0:T(8,128)} %shard_map.56) | copy-start | bytes 3145732
Sparse Core Ops, SparseCore 0:
  9.2 43.6 all-gather.1

commit v11 on v9

--- a/solution.py
+++ b/solution.py
@@ -12,7 +12,7 @@
     return jnp.dot(left, right, precision=lax.Precision.HIGHEST, preferred_element_type=jnp.float32)
 
 
-def _allreduce_kernel(groups, nc, x_ref, t_ref, o_ref, buf1, buf2, red, recv1, recv2, recv3, send_sems, recv_sems):
+def _allreduce_kernel(groups, nc, x_ref, t_ref, o_ref, buf1, buf2, red, relay, recv1, recv2, recv3, send_sems, recv_sems):
     me = lax.axis_index("row")
     col = lax.axis_index("col")
     g1, g2, g3 = groups
@@ -84,6 +84,48 @@
 
         return start, combine
 
+    def ring_reduce_stage(stage, g, stride, mine, src, piece, recv, dst, c):
+        half = piece // 2
+        right_i, left_i = lax.rem(mine + 1, g), lax.rem(mine + g - 1, g)
+        right, left = me + (right_i - mine) * stride, me + (left_i - mine) * stride
+        far = lax.rem(mine + 2, g)
+
+        def send(src_ref, dst_ref, k, target):
+            return pltpu.make_async_remote_copy(
+                src_ref=src_ref, dst_ref=dst_ref,
+                send_sem=send_sems.at[stage, c, k], recv_sem=recv_sems.at[stage, c, k],
+                device_id=(target, col), device_id_type=mesh_id,
+            )
+
+        cols_c = pl.ds(c * cw, cw)
+        first = [
+            send(part(src, far * piece, half, c), recv.at[0, pl.ds(0, half), cols_c], 0, right),
+            send(part(src, far * piece + half, half, c), recv.at[1, pl.ds(0, half), cols_c], 1, left),
+        ]
+        second = [
+            send(relay.at[0, :, cols_c], recv.at[2, :, cols_c], 2, right),
+            send(relay.at[1, :, cols_c], recv.at[3, :, cols_c], 3, left),
+        ]
+
+        def start():
+            for cp in first:
+                cp.start()
+
+        def combine():
+            for cp in first:
+                cp.wait()
+            for k, (j, lo) in enumerate(((right_i, 0), (left_i, half))):
+                relay[k, :, cols_c] = src[pl.ds(pl.multiple_of(j * piece, piece), piece), cols_c]
+                relay[k, pl.ds(lo, half), cols_c] += recv[k, pl.ds(0, half), cols_c]
+            for cp in second:
+                cp.start()
+            for cp in second:
+                cp.wait()
+            own = src[pl.ds(pl.multiple_of(mine * piece, piece), piece), cols_c]
+            dst[:, cols_c] = own + recv[2, :, cols_c] + recv[3, :, cols_c]
+
+        return start, combine
+
     def run(plan):
         for c in range(nc):
             plan[0](c)[0]()
@@ -93,7 +135,7 @@
                 if k + 1 < len(plan):
                     plan[k + 1](c)[0]()
 
-    run([functools.partial(reduce_stage, *p) for p in reduce_plan])
+    run([functools.partial(ring_reduce_stage if p[1] == 4 else reduce_stage, *p) for p in reduce_plan])
 
     base3 = i1 * p1 + i2 * p2
     o_ref[pl.ds(pl.multiple_of(base3 + i3 * p3, p3), p3), :] = lax.dot_general(
@@ -104,9 +146,44 @@
         own = part(o_ref, base + mine * block, block, c)
         return exchange(stage, c, g, stride, mine, lambda j: own, lambda j, s: own)
 
+    def ring_gather_stage(stage, g, stride, mine, base, block, c):
+        half = block // 2
+        right_i, left_i = lax.rem(mine + 1, g), lax.rem(mine + g - 1, g)
+        right, left = me + (right_i - mine) * stride, me + (left_i - mine) * stride
+
+        def send(view, k, target):
+            return pltpu.make_async_remote_copy(
+                src_ref=view, dst_ref=view,
+                send_sem=send_sems.at[stage, c, k], recv_sem=recv_sems.at[stage, c, k],
+                device_id=(target, col), device_id_type=mesh_id,
+            )
+
+        own = part(o_ref, base + mine * block, block, c)
+        first = [send(own, 0, right), send(own, 1, left)]
+        second = [
+            send(part(o_ref, base + left_i * block, half, c), 2, right),
+            send(part(o_ref, base + right_i * block + half, half, c), 3, left),
+        ]
+
+        def start():
+            for cp in first:
+                cp.start()
+
+        def finish():
+            first[0].wait_recv()
+            second[0].start()
+            first[1].wait_recv()
+            second[1].start()
+            for cp in first:
+                cp.wait_send()
+            for cp in second:
+                cp.wait()
+
+        return start, finish
+
     run([
         functools.partial(gather_stage, 3, g3, s3, i3, base3, p3),
-        functools.partial(gather_stage, 4, g2, s2, i2, i1 * p1, p2),
+        functools.partial(ring_gather_stage if g2 == 4 else gather_stage, 4, g2, s2, i2, i1 * p1, p2),
         functools.partial(gather_stage, 5, g1, s1, i1, 0, p1),
     ])
 
@@ -127,6 +204,7 @@
             pltpu.VMEM((p1, cols), x.dtype),
             pltpu.VMEM((p2, cols), x.dtype),
             pltpu.VMEM((p3, cols), x.dtype),
+            pltpu.VMEM((2, p2, cols), x.dtype),
             pltpu.VMEM((g1, p1, cols), x.dtype),
             pltpu.VMEM((g2, p2, cols), x.dtype),
             pltpu.VMEM((g3, p3, cols), x.dtype),

time: 134 us -> 148 us (1.10)
  Pallas kernels: 102 us -> 116 us
    pallas_call x2, Pallas kernels: 77.9 us -> 92.4 us  [row_allreduce_times(): pl.pallas_call(functools.partial(_allreduce_kernel, groups, nc), out_shap...]
  transfers between devices with their start and end apart: 1 -> 1, of which waited for: 0 -> 0; matrix products, arithmetic and copies ran while one was open for 7% -> 6% of each run, Pallas kernels for 32% -> 33%
where the time goes in v11:
time: 148 us
  Pallas kernels  116 us (78%)
  matrix products  18.2 us (12%)
  between operations  13.4 us (9%)
    pallas_call x2, Pallas kernels, row_allreduce_times(): pl.pallas_call(functools.partial(_allreduce_kernel, groups, nc), out_shap...  92.4 us
    pallas_call x1, Pallas kernels, col_gather(): pl.pallas_call(functools.partial(_col_gather_kernel, n), out_shape=jax.Sh...  23.9 us
    dot_general x2, matrix products, on_device(): lax.dot_general(vectors, applied_t, (((1,), (1,)), ((), ())), precision=l...  9.41 us
    dot_general x2, matrix products, on_device(): lax.dot_general(updated, vectors, (((0,), (0,)), ((), ())), precision=lax...  8.8 us
  transfers between devices with their start and end apart: 1, of which 0 were waited for; matrix products, arithmetic and copies ran while one was open for 6% of the time, Pallas kernels for 33%

profile of v11, /device:TPU:1, one launch (start us, length us, event | category | flops | bytes accessed | tf_op | source)
XLA Modules:
  0.0 148.0 jit_solution(8221636423779483123)
XLA Ops:
  6.5 0.0 copy-start
  6.5 0.0 all-gather.2.cloned.1.call-start
  6.5 23.9 %shard_map.55 = f32[1024,512]{1,0:T(8,128)} custom-call(f32[1024,128]{1,0:T(8,128)} %v_ref.1), custom_call_target="tpu_custom_call" | custom-call | bytes 4194304 | tf_op jit(solution)/shard_map/pallas_call | solution.py:268
  30.5 0.0 all-gather.2.cloned.1.call-update
  30.5 0.0 copy-done
  30.5 4.4 %convolution_bitcast_fusion.x_ref = f32[512,512]{1,0:T(8,128)} fusion(f32[1024,512]{1,0:T(8,128)} %shard_map.55, f32[1024,512]{1,0:T(8,128)S(1)} %copy-done), kind=kOutput, calls=%fused_computation.2 | convolution fusion | flops 1610612736 | bytes 5242880 | tf_op jit(solution)/shard_map/dot_general | solution.py:285
  34.9 49.5 %shard_map.56 = f32[512,512]{1,0:T(8,128)} custom-call(f32[512,512]{1,0:T(8,128)} %convolution_bitcast_fusion.x_ref, f32[512,512]{1,0:T(8,128)} %t_ref.2), custom_call_target="tpu_custom_call" | custom-call | flops 262144 | bytes 4194304 | tf_op jit(solution)/shard_map/pallas_call | solution.py:198
  84.5 4.4 %convolution_subtract_fusion.1 = f32[1024,512]{1,0:T(8,128)S(1)} fusion(f32[1024,512]{1,0:T(8,128)} %param.5, f32[1024,512]{1,0:T(8,128)} %shard_map.55, f32[512,512]{1,0:T(8,128)} %shard_map.56), kind=kOutput, calls=%fused_computation.1 | convolution fusion | flops 1611137024 | bytes 7340032 | tf_op jit(solution)/shard_map/dot_general | solution.py:287
  88.9 0.0 all-gather.2.cloned.1.call-done
  88.9 4.4 %fusion.x_ref = f32[512,512]{1,0:T(8,128)} fusion(f32[1024,512]{1,0:T(8,128)S(1)} %convolution_subtract_fusion.1, f32[1024,512]{1,0:T(8,128)} %all-gather.2.cloned.1.call-done), kind=kOutput, calls=%fused_computation.3 | convolution fusion | flops 1610612736 | bytes 5242880 | tf_op jit(solution)/shard_map/dot_general | solution.py:285
  93.3 42.8 %shard_map.57 = f32[512,512]{1,0:T(8,128)} custom-call(f32[512,512]{1,0:T(8,128)} %fusion.x_ref, f32[512,512]{1,0:T(8,128)} %t_ref.3), custom_call_target="tpu_custom_call" | custom-call | flops 262144 | bytes 4194304 | tf_op jit(solution)/shard_map/pallas_call | solution.py:198
  136.1 5.0 %convolution_subtract_fusion = f32[1024,512]{1,0:T(8,128)} fusion(f32[1024,512]{1,0:T(8,128)S(1)} %convolution_subtract_fusion.1, f32[1024,512]{1,0:T(8,128)} %all-gather.2.cloned.1.call-done, f32[512,512]{1,0:T(8,128)} %shard_map.57), kind=kOutput, calls=%fused_computation | convolution fusion | flops 1611137024 | bytes 7340032 | tf_op jit(solution)/shard_map/dot_general | solution.py:287
Async XLA Ops:
  6.5 24.0 %copy-start = (f32[1024,512]{1,0:T(8,128)S(1)}, f32[1024,512]{1,0:T(8,128)}, u32[]{:S(2)}) copy-start(f32[1024,512]{1,0:T(8,128)} %param.5) | copy-start | bytes 6291460
  6.5 82.3 %all-gather.2.cloned.1.call-start = ((), (), s32[]{:S(2)}) async-start(), calls=%async_computation | async-start | bytes 2621440 | tf_op jit(solution)/shard_map/all_gather | solution.py:282
Sparse Core Ops, SparseCore 0:
  30.6 40.1 all-gather.1

commit v12 on v9

--- a/solution.py
+++ b/solution.py
@@ -165,21 +165,25 @@
         pl.semaphore_signal(barrier, inc=1, device_id=(row, target), device_id_type=pl.DeviceIdType.MESH)
     pl.semaphore_wait(barrier, 2)
 
-    to_right = send(v_ref, block(me), 0, right)
-    to_left = send(v_ref, block(me), 1, left)
-    to_right.start()
-    to_left.start()
+    def rows(view, lo):
+        return view.at[pl.ds(lo, half), :]
+
+    to_right = [send(rows(v_ref, lo), rows(block(me), lo), k, right) for k, lo in ((0, 0), (1, half))]
+    to_left = [send(rows(v_ref, lo), rows(block(me), lo), k, left) for k, lo in ((2, half), (3, 0))]
+    for a, b in zip(to_right, to_left):
+        a.start()
+        b.start()
     block(me)[...] = v_ref[...]
-    to_right.wait_recv()
-    from_left = block(left)
-    fwd_right = send(from_left.at[pl.ds(0, half), :], from_left.at[pl.ds(0, half), :], 2, right)
+    to_right[0].wait_recv()
+    fwd_right = send(rows(block(left), 0), rows(block(left), 0), 4, right)
     fwd_right.start()
-    to_left.wait_recv()
-    from_right = block(right)
-    fwd_left = send(from_right.at[pl.ds(half, half), :], from_right.at[pl.ds(half, half), :], 3, left)
+    to_left[0].wait_recv()
+    fwd_left = send(rows(block(right), half), rows(block(right), half), 5, left)
     fwd_left.start()
-    to_right.wait_send()
-    to_left.wait_send()
+    for cp in to_right + to_left:
+        cp.wait_send()
+    to_right[1].wait_recv()
+    to_left[1].wait_recv()
     fwd_right.wait()
     fwd_left.wait()
 
@@ -192,7 +196,7 @@
         out_shape=jax.ShapeDtypeStruct((rows, w * n), v.dtype),
         in_specs=[pl.BlockSpec(memory_space=pltpu.VMEM)],
         out_specs=pl.BlockSpec(memory_space=pltpu.VMEM),
-        scratch_shapes=[pltpu.SemaphoreType.DMA((n,)), pltpu.SemaphoreType.DMA((n,))],
+        scratch_shapes=[pltpu.SemaphoreType.DMA((6,)), pltpu.SemaphoreType.DMA((6,))],
         compiler_params=pltpu.CompilerParams(has_side_effects=True, collective_id=0),
         cost_estimate=pl.CostEstimate(flops=0, transcendentals=0, bytes_accessed=2 * rows * w * n * 4),
     )(v)

time: 134 us -> 133 us (level)
    pallas_call x1, Pallas kernels: 23.9 us -> 22.4 us  [col_gather(): pl.pallas_call(functools.partial(_col_gather_kernel, n), out_shape=jax.Sh...]
  transfers between devices with their start and end apart: 1 -> 1, of which waited for: 0 -> 0; matrix products, arithmetic and copies ran while one was open for 7% -> 7% of each run, Pallas kernels for 32% -> 33%
where the time goes in v12:
time: 133 us; the launch traced here: 132 us
  Pallas kernels  101 us (76%)
  matrix products  18.2 us (14%)
  between operations  13.4 us (10%)
    pallas_call x2, Pallas kernels, row_allreduce_times(): pl.pallas_call(functools.partial(_allreduce_kernel, groups, nc), out_shap...  78.4 us
    pallas_call x1, Pallas kernels, col_gather(): pl.pallas_call(functools.partial(_col_gather_kernel, n), out_shape=jax.Sh...  22.4 us
    dot_general x2, matrix products, on_device(): lax.dot_general(vectors, applied_t, (((1,), (1,)), ((), ())), precision=l...  9.41 us
    dot_general x2, matrix products, on_device(): lax.dot_general(updated, vectors, (((0,), (0,)), ((), ())), precision=lax...  8.8 us
  transfers between devices with their start and end apart: 1, of which 0 were waited for; matrix products, arithmetic and copies ran while one was open for 7% of the time, Pallas kernels for 33%

profile of v12, /device:TPU:1, one launch (start us, length us, event | category | flops | bytes accessed | tf_op | source)
XLA Modules:
  0.0 132.5 jit_solution(16104933236726829911)
XLA Ops:
  6.5 0.0 copy-start
  6.5 0.0 all-gather.2.cloned.1.call-start
  6.5 22.4 %shard_map.55 = f32[1024,512]{1,0:T(8,128)} custom-call(f32[1024,128]{1,0:T(8,128)} %v_ref.1), custom_call_target="tpu_custom_call" | custom-call | bytes 4194304 | tf_op jit(solution)/shard_map/pallas_call | solution.py:194
  28.9 0.0 all-gather.2.cloned.1.call-update
  29.0 0.0 copy-done
  29.0 4.4 %convolution_bitcast_fusion.x_ref = f32[512,512]{1,0:T(8,128)} fusion(f32[1024,512]{1,0:T(8,128)} %shard_map.55, f32[1024,512]{1,0:T(8,128)S(1)} %copy-done), kind=kOutput, calls=%fused_computation.2 | convolution fusion | flops 1610612736 | bytes 5242880 | tf_op jit(solution)/shard_map/dot_general | solution.py:211
  33.4 43.3 %shard_map.56 = f32[512,512]{1,0:T(8,128)} custom-call(f32[512,512]{1,0:T(8,128)} %convolution_bitcast_fusion.x_ref, f32[512,512]{1,0:T(8,128)} %t_ref.2), custom_call_target="tpu_custom_call" | custom-call | flops 262144 | bytes 4194304 | tf_op jit(solution)/shard_map/pallas_call | solution.py:121
  76.7 4.4 %convolution_subtract_fusion.1 = f32[1024,512]{1,0:T(8,128)S(1)} fusion(f32[1024,512]{1,0:T(8,128)} %param.5, f32[1024,512]{1,0:T(8,128)} %shard_map.55, f32[512,512]{1,0:T(8,128)} %shard_map.56), kind=kOutput, calls=%fused_computation.1 | convolution fusion | flops 1611137024 | bytes 7340032 | tf_op jit(solution)/shard_map/dot_general | solution.py:213
  81.1 0.0 all-gather.2.cloned.1.call-done
  81.2 4.4 %fusion.x_ref = f32[512,512]{1,0:T(8,128)} fusion(f32[1024,512]{1,0:T(8,128)S(1)} %convolution_subtract_fusion.1, f32[1024,512]{1,0:T(8,128)} %all-gather.2.cloned.1.call-done), kind=kOutput, calls=%fused_computation.3 | convolution fusion | flops 1610612736 | bytes 5242880 | tf_op jit(solution)/shard_map/dot_general | solution.py:211
  85.6 35.1 %shard_map.57 = f32[512,512]{1,0:T(8,128)} custom-call(f32[512,512]{1,0:T(8,128)} %fusion.x_ref, f32[512,512]{1,0:T(8,128)} %t_ref.3), custom_call_target="tpu_custom_call" | custom-call | flops 262144 | bytes 4194304 | tf_op jit(solution)/shard_map/pallas_call | solution.py:121
  120.6 5.0 %convolution_subtract_fusion = f32[1024,512]{1,0:T(8,128)} fusion(f32[1024,512]{1,0:T(8,128)S(1)} %convolution_subtract_fusion.1, f32[1024,512]{1,0:T(8,128)} %all-gather.2.cloned.1.call-done, f32[512,512]{1,0:T(8,128)} %shard_map.57), kind=kOutput, calls=%fused_computation | convolution fusion | flops 1611137024 | bytes 7340032 | tf_op jit(solution)/shard_map/dot_general | solution.py:213
Async XLA Ops:
  6.5 22.4 %copy-start = (f32[1024,512]{1,0:T(8,128)S(1)}, f32[1024,512]{1,0:T(8,128)}, u32[]{:S(2)}) copy-start(f32[1024,512]{1,0:T(8,128)} %param.5) | copy-start | bytes 6291460
  6.5 74.6 %all-gather.2.cloned.1.call-start = ((), (), s32[]{:S(2)}) async-start(), calls=%async_computation | async-start | bytes 2621440 | tf_op jit(solution)/shard_map/all_gather | solution.py:208
Sparse Core Ops, SparseCore 0:
  29.1 40.5 all-gather.1

commit v13 on v12

--- a/solution.py
+++ b/solution.py
@@ -111,7 +111,7 @@
     ])
 
 
-def row_allreduce_times(x, t, n, collective_id, nc=2):
+def row_allreduce_times(x, t, n, collective_id, nc=4):
     rows, cols = x.shape
     groups = (2, min(4, n // 2), max(1, n // 8))
     g1, g2, g3 = groups

time: 133 us -> 134 us (level)
    pallas_call x2, Pallas kernels: 78.4 us -> 79.9 us  [row_allreduce_times(): pl.pallas_call(functools.partial(_allreduce_kernel, groups, nc), out_shap...]
where the time goes in v13:
time: 134 us
  Pallas kernels  102 us (76%)
  matrix products  18.2 us (14%)
  between operations  13.4 us (10%)
    pallas_call x2, Pallas kernels, row_allreduce_times(): pl.pallas_call(functools.partial(_allreduce_kernel, groups, nc), out_shap...  79.9 us
    pallas_call x1, Pallas kernels, col_gather(): pl.pallas_call(functools.partial(_col_gather_kernel, n), out_shape=jax.Sh...  22.4 us
    dot_general x2, matrix products, on_device(): lax.dot_general(vectors, applied_t, (((1,), (1,)), ((), ())), precision=l...  9.41 us
    dot_general x2, matrix products, on_device(): lax.dot_general(updated, vectors, (((0,), (0,)), ((), ())), precision=lax...  8.8 us
  transfers between devices with their start and end apart: 1, of which 0 were waited for; matrix products, arithmetic and copies ran while one was open for 7% of the time, Pallas kernels for 33%

profile of v13, /device:TPU:1, one launch (start us, length us, event | category | flops | bytes accessed | tf_op | source)
XLA Modules:
  0.0 134.0 jit_solution(1780176083249481381)
XLA Ops:
  6.5 0.0 copy-start
  6.5 0.0 all-gather.2.cloned.1.call-start
  6.5 22.4 %shard_map.55 = f32[1024,512]{1,0:T(8,128)} custom-call(f32[1024,128]{1,0:T(8,128)} %v_ref.1), custom_call_target="tpu_custom_call" | custom-call | bytes 4194304 | tf_op jit(solution)/shard_map/pallas_call | solution.py:194
  28.9 0.0 all-gather.2.cloned.1.call-update
  29.0 0.0 copy-done
  29.0 4.4 %convolution_bitcast_fusion.x_ref = f32[512,512]{1,0:T(8,128)} fusion(f32[1024,512]{1,0:T(8,128)} %shard_map.55, f32[1024,512]{1,0:T(8,128)S(1)} %copy-done), kind=kOutput, calls=%fused_computation.2 | convolution fusion | flops 1610612736 | bytes 5242880 | tf_op jit(solution)/shard_map/dot_general | solution.py:211
  33.4 43.8 %shard_map.56 = f32[512,512]{1,0:T(8,128)} custom-call(f32[512,512]{1,0:T(8,128)} %convolution_bitcast_fusion.x_ref, f32[512,512]{1,0:T(8,128)} %t_ref.2), custom_call_target="tpu_custom_call" | custom-call | flops 262144 | bytes 4194304 | tf_op jit(solution)/shard_map/pallas_call | solution.py:121
  77.2 4.4 %convolution_subtract_fusion.1 = f32[1024,512]{1,0:T(8,128)S(1)} fusion(f32[1024,512]{1,0:T(8,128)} %param.5, f32[1024,512]{1,0:T(8,128)} %shard_map.55, f32[512,512]{1,0:T(8,128)} %shard_map.56), kind=kOutput, calls=%fused_computation.1 | convolution fusion | flops 1611137024 | bytes 7340032 | tf_op jit(solution)/shard_map/dot_general | solution.py:213
  81.6 0.0 all-gather.2.cloned.1.call-done
  81.6 4.4 %fusion.x_ref = f32[512,512]{1,0:T(8,128)} fusion(f32[1024,512]{1,0:T(8,128)S(1)} %convolution_subtract_fusion.1, f32[1024,512]{1,0:T(8,128)} %all-gather.2.cloned.1.call-done), kind=kOutput, calls=%fused_computation.3 | convolution fusion | flops 1610612736 | bytes 5242880 | tf_op jit(solution)/shard_map/dot_general | solution.py:211
  86.0 36.1 %shard_map.57 = f32[512,512]{1,0:T(8,128)} custom-call(f32[512,512]{1,0:T(8,128)} %fusion.x_ref, f32[512,512]{1,0:T(8,128)} %t_ref.3), custom_call_target="tpu_custom_call" | custom-call | flops 262144 | bytes 4194304 | tf_op jit(solution)/shard_map/pallas_call | solution.py:121
  122.1 5.0 %convolution_subtract_fusion = f32[1024,512]{1,0:T(8,128)} fusion(f32[1024,512]{1,0:T(8,128)S(1)} %convolution_subtract_fusion.1, f32[1024,512]{1,0:T(8,128)} %all-gather.2.cloned.1.call-done, f32[512,512]{1,0:T(8,128)} %shard_map.57), kind=kOutput, calls=%fused_computation | convolution fusion | flops 1611137024 | bytes 7340032 | tf_op jit(solution)/shard_map/dot_general | solution.py:213
Async XLA Ops:
  6.5 22.4 %copy-start = (f32[1024,512]{1,0:T(8,128)S(1)}, f32[1024,512]{1,0:T(8,128)}, u32[]{:S(2)}) copy-start(f32[1024,512]{1,0:T(8,128)} %param.5) | copy-start | bytes 6291460
  6.5 75.1 %all-gather.2.cloned.1.call-start = ((), (), s32[]{:S(2)}) async-start(), calls=%async_computation | async-start | bytes 2621440 | tf_op jit(solution)/shard_map/all_gather | solution.py:208
Sparse Core Ops, SparseCore 0:
  29.1 40.5 all-gather.1

commit v14 on v12

--- a/solution.py
+++ b/solution.py
@@ -97,8 +97,8 @@
 
     base3 = i1 * p1 + i2 * p2
     o_ref[pl.ds(pl.multiple_of(base3 + i3 * p3, p3), p3), :] = lax.dot_general(
-        red[...], t_ref[...], (((1,), (1,)), ((), ())), precision=lax.Precision.HIGHEST, preferred_element_type=jnp.float32
-    )
+        t_ref[...], red[...], (((1,), (1,)), ((), ())), precision=lax.Precision.HIGHEST, preferred_element_type=jnp.float32
+    ).T
 
     def gather_stage(stage, g, stride, mine, base, block, c):
         own = part(o_ref, base + mine * block, block, c)

time: 133 us -> 133 us (level)
  no operation moved by 1% of the time
where the time goes in v14:
time: 133 us
  Pallas kernels  101 us (76%)
  matrix products  18.2 us (14%)
  between operations  13.4 us (10%)
    pallas_call x2, Pallas kernels, row_allreduce_times(): pl.pallas_call(functools.partial(_allreduce_kernel, groups, nc), out_shap...  78.6 us
    pallas_call x1, Pallas kernels, col_gather(): pl.pallas_call(functools.partial(_col_gather_kernel, n), out_shape=jax.Sh...  22.4 us
    dot_general x2, matrix products, on_device(): lax.dot_general(vectors, applied_t, (((1,), (1,)), ((), ())), precision=l...  9.41 us
    dot_general x2, matrix products, on_device(): lax.dot_general(updated, vectors, (((0,), (0,)), ((), ())), precision=lax...  8.8 us
  transfers between devices with their start and end apart: 1, of which 0 were waited for; matrix products, arithmetic and copies ran while one was open for 7% of the time, Pallas kernels for 33%

profile of v14, /device:TPU:1, one launch (start us, length us, event | category | flops | bytes accessed | tf_op | source)
XLA Modules:
  0.0 132.7 jit_solution(5748935979551225646)
XLA Ops:
  6.5 0.0 copy-start
  6.5 0.0 all-gather.2.cloned.1.call-start
  6.5 22.4 %shard_map.55 = f32[1024,512]{1,0:T(8,128)} custom-call(f32[1024,128]{1,0:T(8,128)} %v_ref.1), custom_call_target="tpu_custom_call" | custom-call | bytes 4194304 | tf_op jit(solution)/shard_map/pallas_call | solution.py:194
  28.9 0.0 all-gather.2.cloned.1.call-update
  29.0 0.0 copy-done
  29.0 4.4 %convolution_bitcast_fusion.x_ref = f32[512,512]{1,0:T(8,128)} fusion(f32[1024,512]{1,0:T(8,128)} %shard_map.55, f32[1024,512]{1,0:T(8,128)S(1)} %copy-done), kind=kOutput, calls=%fused_computation.2 | convolution fusion | flops 1610612736 | bytes 5242880 | tf_op jit(solution)/shard_map/dot_general | solution.py:211
  33.4 43.4 %shard_map.56 = f32[512,512]{1,0:T(8,128)} custom-call(f32[512,512]{1,0:T(8,128)} %convolution_bitcast_fusion.x_ref, f32[512,512]{1,0:T(8,128)} %t_ref.2), custom_call_target="tpu_custom_call" | custom-call | flops 262144 | bytes 4194304 | tf_op jit(solution)/shard_map/pallas_call | solution.py:121
  76.8 4.4 %convolution_subtract_fusion.1 = f32[1024,512]{1,0:T(8,128)S(1)} fusion(f32[1024,512]{1,0:T(8,128)} %param.5, f32[1024,512]{1,0:T(8,128)} %shard_map.55, f32[512,512]{1,0:T(8,128)} %shard_map.56), kind=kOutput, calls=%fused_computation.1 | convolution fusion | flops 1611137024 | bytes 7340032 | tf_op jit(solution)/shard_map/dot_general | solution.py:213
  81.2 0.0 all-gather.2.cloned.1.call-done
  81.2 4.4 %fusion.x_ref = f32[512,512]{1,0:T(8,128)} fusion(f32[1024,512]{1,0:T(8,128)S(1)} %convolution_subtract_fusion.1, f32[1024,512]{1,0:T(8,128)} %all-gather.2.cloned.1.call-done), kind=kOutput, calls=%fused_computation.3 | convolution fusion | flops 1610612736 | bytes 5242880 | tf_op jit(solution)/shard_map/dot_general | solution.py:211
  85.6 35.1 %shard_map.57 = f32[512,512]{1,0:T(8,128)} custom-call(f32[512,512]{1,0:T(8,128)} %fusion.x_ref, f32[512,512]{1,0:T(8,128)} %t_ref.3), custom_call_target="tpu_custom_call" | custom-call | flops 262144 | bytes 4194304 | tf_op jit(solution)/shard_map/pallas_call | solution.py:121
  120.8 5.0 %convolution_subtract_fusion = f32[1024,512]{1,0:T(8,128)} fusion(f32[1024,512]{1,0:T(8,128)S(1)} %convolution_subtract_fusion.1, f32[1024,512]{1,0:T(8,128)} %all-gather.2.cloned.1.call-done, f32[512,512]{1,0:T(8,128)} %shard_map.57), kind=kOutput, calls=%fused_computation | convolution fusion | flops 1611137024 | bytes 7340032 | tf_op jit(solution)/shard_map/dot_general | solution.py:213
Async XLA Ops:
  6.5 22.4 %copy-start = (f32[1024,512]{1,0:T(8,128)S(1)}, f32[1024,512]{1,0:T(8,128)}, u32[]{:S(2)}) copy-start(f32[1024,512]{1,0:T(8,128)} %param.5) | copy-start | bytes 6291460
  6.5 74.7 %all-gather.2.cloned.1.call-start = ((), (), s32[]{:S(2)}) async-start(), calls=%async_computation | async-start | bytes 2621440 | tf_op jit(solution)/shard_map/all_gather | solution.py:208
Sparse Core Ops, SparseCore 0:
  29.1 40.5 all-gather.1

commit v15 on v14

--- a/solution.py
+++ b/solution.py
@@ -28,7 +28,10 @@
     mesh_id = pl.DeviceIdType.MESH
 
     def part(ref, start, size, c):
-        return ref.at[pl.ds(pl.multiple_of(start, size), size), pl.ds(c * cw, cw)]
+        return ref.at[pl.ds(pl.multiple_of(start, size), size), cols_of(c)]
+
+    def cols_of(c):
+        return pl.ds(0, cols) if c is None else pl.ds(c * cw, cw)
 
     barrier = pltpu.get_barrier_semaphore()
     for g, stride, mine in ((g1, s1, i1), (g2, s2, i2), (g3, s3, i3)):
@@ -46,8 +49,8 @@
             return pltpu.make_async_remote_copy(
                 src_ref=src_of(j),
                 dst_ref=dst_of(j, s),
-                send_sem=send_sems.at[stage, c, s],
-                recv_sem=recv_sems.at[stage, c, s],
+                send_sem=send_sems.at[stage, 0 if c is None else c, s],
+                recv_sem=recv_sems.at[stage, 0 if c is None else c, s],
                 device_id=(me + (j - mine) * stride, col),
                 device_id_type=mesh_id,
             )
@@ -74,26 +77,33 @@
         start, finish = exchange(
             stage, c, g, stride, mine,
             lambda j: part(src, j * piece, piece, c),
-            lambda j, s: recv.at[s, :, pl.ds(c * cw, cw)],
+            lambda j, s: recv.at[s, :, cols_of(c)],
         )
 
         def combine():
             finish()
-            own = src[pl.ds(pl.multiple_of(mine * piece, piece), piece), pl.ds(c * cw, cw)]
-            dst[:, pl.ds(c * cw, cw)] = lax.fori_loop(1, g, lambda s, acc: acc + recv[s, :, pl.ds(c * cw, cw)], own)
+            own = src[pl.ds(pl.multiple_of(mine * piece, piece), piece), cols_of(c)]
+            dst[:, cols_of(c)] = lax.fori_loop(1, g, lambda s, acc: acc + recv[s, :, cols_of(c)], own)
 
         return start, combine
 
-    def run(plan):
-        for c in range(nc):
+    def run(plan, whole):
+        chunks = [[None] if k in whole else list(range(nc)) for k in range(len(plan))]
+        for c in chunks[0]:
             plan[0](c)[0]()
         for k in range(len(plan)):
-            for c in range(nc):
+            if k + 1 < len(plan) and chunks[k + 1] != chunks[k]:
+                for c in chunks[k]:
+                    plan[k](c)[1]()
+                for c in chunks[k + 1]:
+                    plan[k + 1](c)[0]()
+                continue
+            for c in chunks[k]:
                 plan[k](c)[1]()
                 if k + 1 < len(plan):
                     plan[k + 1](c)[0]()
 
-    run([functools.partial(reduce_stage, *p) for p in reduce_plan])
+    run([functools.partial(reduce_stage, *p) for p in reduce_plan], whole=(2,))
 
     base3 = i1 * p1 + i2 * p2
     o_ref[pl.ds(pl.multiple_of(base3 + i3 * p3, p3), p3), :] = lax.dot_general(
@@ -108,7 +118,7 @@
         functools.partial(gather_stage, 3, g3, s3, i3, base3, p3),
         functools.partial(gather_stage, 4, g2, s2, i2, i1 * p1, p2),
         functools.partial(gather_stage, 5, g1, s1, i1, 0, p1),
-    ])
+    ], whole=(0,))
 
 
 def row_allreduce_times(x, t, n, collective_id, nc=2):

time: 133 us -> 136 us (1.023)
  Pallas kernels: 101 us -> 104 us
    pallas_call x2, Pallas kernels: 78.6 us -> 81.8 us  [row_allreduce_times(): pl.pallas_call(functools.partial(_allreduce_kernel, groups, nc), out_shap...]
  transfers between devices with their start and end apart: 1 -> 1, of which waited for: 0 -> 0; matrix products, arithmetic and copies ran while one was open for 7% -> 6% of each run, Pallas kernels for 33% -> 33%
where the time goes in v15:
time: 136 us
  Pallas kernels  104 us (76%)
  matrix products  18.2 us (13%)
  between operations  13.4 us (10%)
    pallas_call x2, Pallas kernels, row_allreduce_times(): pl.pallas_call(functools.partial(_allreduce_kernel, groups, nc), out_shap...  81.8 us
    pallas_call x1, Pallas kernels, col_gather(): pl.pallas_call(functools.partial(_col_gather_kernel, n), out_shape=jax.Sh...  22.4 us
    dot_general x2, matrix products, on_device(): lax.dot_general(vectors, applied_t, (((1,), (1,)), ((), ())), precision=l...  9.41 us
    dot_general x2, matrix products, on_device(): lax.dot_general(updated, vectors, (((0,), (0,)), ((), ())), precision=lax...  8.8 us
  transfers between devices with their start and end apart: 1, of which 0 were waited for; matrix products, arithmetic and copies ran while one was open for 6% of the time, Pallas kernels for 33%

profile of v15, /device:TPU:1, one launch (start us, length us, event | category | flops | bytes accessed | tf_op | source)
XLA Modules:
  0.0 135.9 jit_solution(10922017585378192286)
XLA Ops:
  6.5 0.0 copy-start
  6.5 0.0 all-gather.2.cloned.1.call-start
  6.5 22.4 %shard_map.55 = f32[1024,512]{1,0:T(8,128)} custom-call(f32[1024,128]{1,0:T(8,128)} %v_ref.1), custom_call_target="tpu_custom_call" | custom-call | bytes 4194304 | tf_op jit(solution)/shard_map/pallas_call | solution.py:204
  28.9 0.0 all-gather.2.cloned.1.call-update
  29.0 0.0 copy-done
  29.0 4.4 %convolution_bitcast_fusion.x_ref = f32[512,512]{1,0:T(8,128)} fusion(f32[1024,512]{1,0:T(8,128)} %shard_map.55, f32[1024,512]{1,0:T(8,128)S(1)} %copy-done), kind=kOutput, calls=%fused_computation.2 | convolution fusion | flops 1610612736 | bytes 5242880 | tf_op jit(solution)/shard_map/dot_general | solution.py:221
  33.4 44.8 %shard_map.56 = f32[512,512]{1,0:T(8,128)} custom-call(f32[512,512]{1,0:T(8,128)} %convolution_bitcast_fusion.x_ref, f32[512,512]{1,0:T(8,128)} %t_ref.2), custom_call_target="tpu_custom_call" | custom-call | flops 262144 | bytes 4194304 | tf_op jit(solution)/shard_map/pallas_call | solution.py:131
  78.1 4.4 %convolution_subtract_fusion.1 = f32[1024,512]{1,0:T(8,128)S(1)} fusion(f32[1024,512]{1,0:T(8,128)} %param.5, f32[1024,512]{1,0:T(8,128)} %shard_map.55, f32[512,512]{1,0:T(8,128)} %shard_map.56), kind=kOutput, calls=%fused_computation.1 | convolution fusion | flops 1611137024 | bytes 7340032 | tf_op jit(solution)/shard_map/dot_general | solution.py:223
  82.5 0.0 all-gather.2.cloned.1.call-done
  82.6 4.4 %fusion.x_ref = f32[512,512]{1,0:T(8,128)} fusion(f32[1024,512]{1,0:T(8,128)S(1)} %convolution_subtract_fusion.1, f32[1024,512]{1,0:T(8,128)} %all-gather.2.cloned.1.call-done), kind=kOutput, calls=%fused_computation.3 | convolution fusion | flops 1610612736 | bytes 5242880 | tf_op jit(solution)/shard_map/dot_general | solution.py:221
  87.0 37.0 %shard_map.57 = f32[512,512]{1,0:T(8,128)} custom-call(f32[512,512]{1,0:T(8,128)} %fusion.x_ref, f32[512,512]{1,0:T(8,128)} %t_ref.3), custom_call_target="tpu_custom_call" | custom-call | flops 262144 | bytes 4194304 | tf_op jit(solution)/shard_map/pallas_call | solution.py:131
  124.0 5.0 %convolution_subtract_fusion = f32[1024,512]{1,0:T(8,128)} fusion(f32[1024,512]{1,0:T(8,128)S(1)} %convolution_subtract_fusion.1, f32[1024,512]{1,0:T(8,128)} %all-gather.2.cloned.1.call-done, f32[512,512]{1,0:T(8,128)} %shard_map.57), kind=kOutput, calls=%fused_computation | convolution fusion | flops 1611137024 | bytes 7340032 | tf_op jit(solution)/shard_map/dot_general | solution.py:223
Async XLA Ops:
  6.5 22.4 %copy-start = (f32[1024,512]{1,0:T(8,128)S(1)}, f32[1024,512]{1,0:T(8,128)}, u32[]{:S(2)}) copy-start(f32[1024,512]{1,0:T(8,128)} %param.5) | copy-start | bytes 6291460
  6.5 76.0 %all-gather.2.cloned.1.call-start = ((), (), s32[]{:S(2)}) async-start(), calls=%async_computation | async-start | bytes 2621440 | tf_op jit(solution)/shard_map/all_gather | solution.py:218
Sparse Core Ops, SparseCore 0:
  29.1 40.5 all-gather.1

commit v16 on v14

--- a/solution.py
+++ b/solution.py
@@ -140,7 +140,7 @@
     )(x, t)
 
 
-def _col_gather_kernel(n, v_ref, o_ref, send_sems, recv_sems):
+def _col_gather_kernel(n, v_ref, e_ref, o_ref, s_ref, send_sems, recv_sems):
     me = lax.axis_index("col")
     row = lax.axis_index("row")
     rows, w = v_ref.shape
@@ -174,6 +174,13 @@
         a.start()
         b.start()
     block(me)[...] = v_ref[...]
+
+    def project(j):
+        s_ref[:, pl.ds(pl.multiple_of(j * w, w), w)] = lax.dot_general(
+            e_ref[...], block(j)[...], (((0,), (0,)), ((), ())), precision=lax.Precision.HIGH, preferred_element_type=jnp.float32
+        )
+
+    project(me)
     to_right[0].wait_recv()
     fwd_right = send(rows(block(left), 0), rows(block(left), 0), 4, right)
     fwd_right.start()
@@ -183,32 +190,40 @@
     for cp in to_right + to_left:
         cp.wait_send()
     to_right[1].wait_recv()
+    project(left)
     to_left[1].wait_recv()
+    project(right)
     fwd_right.wait()
     fwd_left.wait()
-
-
-def col_gather(v, n):
+    project(lax.rem(me + 2, n))
+
+
+def col_gather(v, e, n):
     assert n == 4
     rows, w = v.shape
     return pl.pallas_call(
         functools.partial(_col_gather_kernel, n),
-        out_shape=jax.ShapeDtypeStruct((rows, w * n), v.dtype),
-        in_specs=[pl.BlockSpec(memory_space=pltpu.VMEM)],
-        out_specs=pl.BlockSpec(memory_space=pltpu.VMEM),
+        out_shape=(
+            jax.ShapeDtypeStruct((rows, w * n), v.dtype),
+            jax.ShapeDtypeStruct((e.shape[1], w * n), jnp.float32),
+        ),
+        in_specs=[pl.BlockSpec(memory_space=pltpu.VMEM)] * 2,
+        out_specs=(pl.BlockSpec(memory_space=pltpu.VMEM), pl.BlockSpec(memory_space=pltpu.VMEM)),
         scratch_shapes=[pltpu.SemaphoreType.DMA((6,)), pltpu.SemaphoreType.DMA((6,))],
         compiler_params=pltpu.CompilerParams(has_side_effects=True, collective_id=0),
-        cost_estimate=pl.CostEstimate(flops=0, transcendentals=0, bytes_accessed=2 * rows * w * n * 4),
-    )(v)
+        cost_estimate=pl.CostEstimate(
+            flops=2 * rows * e.shape[1] * w * n, transcendentals=0, bytes_accessed=2 * rows * w * n * 4 + rows * e.shape[1] * 4
+        ),
+    )(v, e)
 
 
 def on_device(n_row, n_col, eigen_vectors, panel_first, panel_second, factor_first, factor_second):
-    vectors_second = col_gather(panel_second, n_col)
+    vectors_second, partial_second = col_gather(panel_second, eigen_vectors, n_col)
     vectors_second, panel_first = lax.optimization_barrier((vectors_second, panel_first))
     vectors_first = lax.all_gather(panel_first, "col", axis=1, tiled=True)
     updated = eigen_vectors
     for collective_id, vectors, factor in ((1, vectors_second, factor_second), (2, vectors_first, factor_first)):
-        partial_t = lax.dot_general(updated, vectors, (((0,), (0,)), ((), ())), precision=lax.Precision.HIGH, preferred_element_type=jnp.float32)
+        partial_t = partial_second if collective_id == 1 else lax.dot_general(updated, vectors, (((0,), (0,)), ((), ())), precision=lax.Precision.HIGH, preferred_element_type=jnp.float32)
         applied_t = row_allreduce_times(partial_t, factor, n_row, collective_id)
         updated = updated - lax.dot_general(vectors, applied_t, (((1,), (1,)), ((), ())), precision=lax.Precision.HIGH, preferred_element_type=jnp.float32)
     return updated

time: 133 us -> 131 us (0.985)
  matrix products: 18.2 us -> 13.8 us
  Pallas kernels: 101 us -> 103 us
    dot_general x2 -> x1, matrix products: 8.8 us -> 4.4 us  [on_device(): lax.dot_general(updated, vectors, (((0,), (0,)), ((), ())), precision=lax...]
    pallas_call x1, Pallas kernels: 22.4 us -> 24.4 us  [col_gather(): pl.pallas_call(functools.partial(_col_gather_kernel, n), out_shape=(jax.S...]
  transfers between devices with their start and end apart: 1 -> 1, of which waited for: 0 -> 0; matrix products, arithmetic and copies ran while one was open for 7% -> 3% of each run, Pallas kernels for 33% -> 33%
where the time goes in v16:
time: 131 us; the launch traced here: 130 us
  Pallas kernels  103 us (79%)
  matrix products  13.8 us (11%)
  between operations  13.4 us (10%)
    pallas_call x2, Pallas kernels, row_allreduce_times(): pl.pallas_call(functools.partial(_allreduce_kernel, groups, nc), out_shap...  78.7 us
    pallas_call x1, Pallas kernels, col_gather(): pl.pallas_call(functools.partial(_col_gather_kernel, n), out_shape=(jax.S...  24.4 us
    dot_general x2, matrix products, on_device(): lax.dot_general(vectors, applied_t, (((1,), (1,)), ((), ())), precision=l...  9.41 us
    dot_general x1, matrix products, on_device(): lax.dot_general(updated, vectors, (((0,), (0,)), ((), ())), precision=lax...  4.4 us
  transfers between devices with their start and end apart: 1, of which 0 were waited for; matrix products, arithmetic and copies ran while one was open for 3% of the time, Pallas kernels for 33%

profile of v16, /device:TPU:1, one launch (start us, length us, event | category | flops | bytes accessed | tf_op | source)
XLA Modules:
  0.0 130.4 jit_solution(17248276992731903209)
XLA Ops:
  6.5 0.0 all-gather.2.cloned.1.call-start
  6.5 24.4 %shard_map.55 = (f32[1024,512]{1,0:T(8,128)}, f32[512,512]{1,0:T(8,128)}) custom-call(f32[1024,128]{1,0:T(8,128)} %v_ref.1, f32[1024,512]{1,0:T(8,128)} %e_ref.1), custom_call_target="tpu_custom_call" | custom-call | flops 536870912 | bytes 6291456 | tf_op jit(solution)/shard_map/pallas_call | solution.py:204
  31.0 0.0 all-gather.2.cloned.1.call-update
  31.0 43.5 %shard_map.56 = f32[512,512]{1,0:T(8,128)} custom-call(f32[512,512]{1,0:T(8,128)} %get-tuple-element.11.x_ref, f32[512,512]{1,0:T(8,128)} %t_ref.2), custom_call_target="tpu_custom_call" | custom-call | flops 262144 | bytes 4194304 | tf_op jit(solution)/shard_map/pallas_call | solution.py:121
  74.5 4.4 %convolution_subtract_fusion.1 = f32[1024,512]{1,0:T(8,128)S(1)} fusion(f32[1024,512]{1,0:T(8,128)} %e_ref.1, f32[1024,512]{1,0:T(8,128)} %get-tuple-element.10, f32[512,512]{1,0:T(8,128)} %shard_map.56), kind=kOutput, calls=%fused_computation.1 | convolution fusion | flops 1611137024 | bytes 7340032 | tf_op jit(solution)/shard_map/dot_general | solution.py:228
  78.9 0.0 all-gather.2.cloned.1.call-done
  78.9 4.4 %fusion.x_ref = f32[512,512]{1,0:T(8,128)} fusion(f32[1024,512]{1,0:T(8,128)S(1)} %convolution_subtract_fusion.1, f32[1024,512]{1,0:T(8,128)} %all-gather.2.cloned.1.call-done), kind=kOutput, calls=%fused_computation.2 | convolution fusion | flops 1610612736 | bytes 5242880 | tf_op jit(solution)/shard_map/dot_general | solution.py:226
  83.3 35.2 %shard_map.57 = f32[512,512]{1,0:T(8,128)} custom-call(f32[512,512]{1,0:T(8,128)} %fusion.x_ref, f32[512,512]{1,0:T(8,128)} %t_ref.3), custom_call_target="tpu_custom_call" | custom-call | flops 262144 | bytes 4194304 | tf_op jit(solution)/shard_map/pallas_call | solution.py:121
  118.6 5.0 %convolution_subtract_fusion = f32[1024,512]{1,0:T(8,128)} fusion(f32[1024,512]{1,0:T(8,128)S(1)} %convolution_subtract_fusion.1, f32[1024,512]{1,0:T(8,128)} %all-gather.2.cloned.1.call-done, f32[512,512]{1,0:T(8,128)} %shard_map.57), kind=kOutput, calls=%fused_computation | convolution fusion | flops 1611137024 | bytes 7340032 | tf_op jit(solution)/shard_map/dot_general | solution.py:228
Async XLA Ops:
  6.5 72.4 %all-gather.2.cloned.1.call-start = ((), (), s32[]{:S(2)}) async-start(), calls=%async_computation | async-start | bytes 2621440 | tf_op jit(solution)/shard_map/all_gather | solution.py:223
Sparse Core Ops, SparseCore 0:
  31.1 40.5 all-gather.1

commit v17 on v16

--- a/solution.py
+++ b/solution.py
@@ -165,37 +165,47 @@
         pl.semaphore_signal(barrier, inc=1, device_id=(row, target), device_id_type=pl.DeviceIdType.MESH)
     pl.semaphore_wait(barrier, 2)
 
-    def rows(view, lo):
+    def rows_of(view, lo):
         return view.at[pl.ds(lo, half), :]
 
-    to_right = [send(rows(v_ref, lo), rows(block(me), lo), k, right) for k, lo in ((0, 0), (1, half))]
-    to_left = [send(rows(v_ref, lo), rows(block(me), lo), k, left) for k, lo in ((2, half), (3, 0))]
+    to_right = [send(rows_of(v_ref, lo), rows_of(block(me), lo), k, right) for k, lo in ((0, 0), (1, half))]
+    to_left = [send(rows_of(v_ref, lo), rows_of(block(me), lo), k, left) for k, lo in ((2, half), (3, 0))]
     for a, b in zip(to_right, to_left):
         a.start()
         b.start()
     block(me)[...] = v_ref[...]
 
-    def project(j):
-        s_ref[:, pl.ds(pl.multiple_of(j * w, w), w)] = lax.dot_general(
-            e_ref[...], block(j)[...], (((0,), (0,)), ((), ())), precision=lax.Precision.HIGH, preferred_element_type=jnp.float32
+    def project(j, lo, size, add):
+        cols = pl.ds(pl.multiple_of(j * w, w), w)
+        part = lax.dot_general(
+            e_ref[pl.ds(lo, size), :], block(j)[pl.ds(lo, size), :], (((0,), (0,)), ((), ())),
+            precision=lax.Precision.HIGH, preferred_element_type=jnp.float32,
         )
-
-    project(me)
+        if add:
+            s_ref[:, cols] += part
+        else:
+            s_ref[:, cols] = part
+
+    project(me, 0, rows, False)
     to_right[0].wait_recv()
-    fwd_right = send(rows(block(left), 0), rows(block(left), 0), 4, right)
+    fwd_right = send(rows_of(block(left), 0), rows_of(block(left), 0), 4, right)
     fwd_right.start()
     to_left[0].wait_recv()
-    fwd_left = send(rows(block(right), half), rows(block(right), half), 5, left)
+    fwd_left = send(rows_of(block(right), half), rows_of(block(right), half), 5, left)
     fwd_left.start()
-    for cp in to_right + to_left:
+    project(left, 0, half, False)
+    project(right, half, half, False)
+    to_right[1].wait_recv()
+    project(left, half, half, True)
+    to_left[1].wait_recv()
+    project(right, 0, half, True)
+    far = lax.rem(me + 2, n)
+    fwd_right.wait_recv()
+    project(far, 0, half, False)
+    fwd_left.wait_recv()
+    project(far, half, half, True)
+    for cp in to_right + to_left + [fwd_right, fwd_left]:
         cp.wait_send()
-    to_right[1].wait_recv()
-    project(left)
-    to_left[1].wait_recv()
-    project(right)
-    fwd_right.wait()
-    fwd_left.wait()
-    project(lax.rem(me + 2, n))
 
 
 def col_gather(v, e, n):

time: 131 us -> 131 us (level)
  no operation moved by 1% of the time
where the time goes in v17:
time: 131 us
  Pallas kernels  104 us (79%)
  matrix products  13.8 us (11%)
  between operations  13.4 us (10%)
    pallas_call x2, Pallas kernels, row_allreduce_times(): pl.pallas_call(functools.partial(_allreduce_kernel, groups, nc), out_shap...  78.8 us
    pallas_call x1, Pallas kernels, col_gather(): pl.pallas_call(functools.partial(_col_gather_kernel, n), out_shape=(jax.S...  25.1 us
    dot_general x2, matrix products, on_device(): lax.dot_general(vectors, applied_t, (((1,), (1,)), ((), ())), precision=l...  9.41 us
    dot_general x1, matrix products, on_device(): lax.dot_general(updated, vectors, (((0,), (0,)), ((), ())), precision=lax...  4.4 us
  transfers between devices with their start and end apart: 1, of which 0 were waited for; matrix products, arithmetic and copies ran while one was open for 3% of the time, Pallas kernels for 33%

profile of v17, /device:TPU:1, one launch (start us, length us, event | category | flops | bytes accessed | tf_op | source)
XLA Modules:
  0.0 131.3 jit_solution(7177805281823426484)
XLA Ops:
  6.5 0.0 all-gather.2.cloned.1.call-start
  6.5 25.1 %shard_map.55 = (f32[1024,512]{1,0:T(8,128)}, f32[512,512]{1,0:T(8,128)}) custom-call(f32[1024,128]{1,0:T(8,128)} %v_ref.1, f32[1024,512]{1,0:T(8,128)} %e_ref.1), custom_call_target="tpu_custom_call" | custom-call | flops 536870912 | bytes 6291456 | tf_op jit(solution)/shard_map/pallas_call | solution.py:214
  31.7 0.0 all-gather.2.cloned.1.call-update
  31.7 43.6 %shard_map.56 = f32[512,512]{1,0:T(8,128)} custom-call(f32[512,512]{1,0:T(8,128)} %get-tuple-element.11.x_ref, f32[512,512]{1,0:T(8,128)} %t_ref.2), custom_call_target="tpu_custom_call" | custom-call | flops 262144 | bytes 4194304 | tf_op jit(solution)/shard_map/pallas_call | solution.py:121
  75.3 4.4 %convolution_subtract_fusion.1 = f32[1024,512]{1,0:T(8,128)S(1)} fusion(f32[1024,512]{1,0:T(8,128)} %e_ref.1, f32[1024,512]{1,0:T(8,128)} %get-tuple-element.10, f32[512,512]{1,0:T(8,128)} %shard_map.56), kind=kOutput, calls=%fused_computation.1 | convolution fusion | flops 1611137024 | bytes 7340032 | tf_op jit(solution)/shard_map/dot_general | solution.py:238
  79.7 0.0 all-gather.2.cloned.1.call-done
  79.8 4.4 %fusion.x_ref = f32[512,512]{1,0:T(8,128)} fusion(f32[1024,512]{1,0:T(8,128)S(1)} %convolution_subtract_fusion.1, f32[1024,512]{1,0:T(8,128)} %all-gather.2.cloned.1.call-done), kind=kOutput, calls=%fused_computation.2 | convolution fusion | flops 1610612736 | bytes 5242880 | tf_op jit(solution)/shard_map/dot_general | solution.py:236
  84.2 35.2 %shard_map.57 = f32[512,512]{1,0:T(8,128)} custom-call(f32[512,512]{1,0:T(8,128)} %fusion.x_ref, f32[512,512]{1,0:T(8,128)} %t_ref.3), custom_call_target="tpu_custom_call" | custom-call | flops 262144 | bytes 4194304 | tf_op jit(solution)/shard_map/pallas_call | solution.py:121
  119.4 5.0 %convolution_subtract_fusion = f32[1024,512]{1,0:T(8,128)} fusion(f32[1024,512]{1,0:T(8,128)S(1)} %convolution_subtract_fusion.1, f32[1024,512]{1,0:T(8,128)} %all-gather.2.cloned.1.call-done, f32[512,512]{1,0:T(8,128)} %shard_map.57), kind=kOutput, calls=%fused_computation | convolution fusion | flops 1611137024 | bytes 7340032 | tf_op jit(solution)/shard_map/dot_general | solution.py:238
Async XLA Ops:
  6.5 73.2 %all-gather.2.cloned.1.call-start = ((), (), s32[]{:S(2)}) async-start(), calls=%async_computation | async-start | bytes 2621440 | tf_op jit(solution)/shard_map/all_gather | solution.py:233
Sparse Core Ops, SparseCore 0:
  31.8 39.7 all-gather.1

commit v18 on v16

--- a/solution.py
+++ b/solution.py
@@ -12,7 +12,11 @@
     return jnp.dot(left, right, precision=lax.Precision.HIGHEST, preferred_element_type=jnp.float32)
 
 
-def _allreduce_kernel(groups, nc, x_ref, t_ref, o_ref, buf1, buf2, red, recv1, recv2, recv3, send_sems, recv_sems):
+def _allreduce_kernel(groups, nc, fused, *refs):
+    if fused:
+        a_ref, v_ref, t_ref, o_ref, x_ref, buf1, buf2, red, recv1, recv2, recv3, send_sems, recv_sems = refs
+    else:
+        x_ref, t_ref, o_ref, buf1, buf2, red, recv1, recv2, recv3, send_sems, recv_sems = refs
     me = lax.axis_index("row")
     col = lax.axis_index("col")
     g1, g2, g3 = groups
@@ -38,6 +42,14 @@
             j = lax.rem(mine + s, g)
             pl.semaphore_signal(barrier, inc=1, device_id=(me + (j - mine) * stride, col), device_id_type=mesh_id)
 
+    def project(c):
+        if fused:
+            x_ref[:, pl.ds(c * cw, cw)] = lax.dot_general(
+                a_ref[...], v_ref[:, pl.ds(c * cw, cw)], (((0,), (0,)), ((), ())),
+                precision=lax.Precision.HIGH, preferred_element_type=jnp.float32,
+            )
+
+    project(0)
     pl.semaphore_wait(barrier, g1 + g2 + g3 - 3)
 
     def exchange(stage, c, g, stride, mine, src_of, dst_of):
@@ -84,8 +96,9 @@
 
         return start, combine
 
-    def run(plan):
+    def run(plan, before=lambda c: None):
         for c in range(nc):
+            before(c)
             plan[0](c)[0]()
         for k in range(len(plan)):
             for c in range(nc):
@@ -93,7 +106,7 @@
                 if k + 1 < len(plan):
                     plan[k + 1](c)[0]()
 
-    run([functools.partial(reduce_stage, *p) for p in reduce_plan])
+    run([functools.partial(reduce_stage, *p) for p in reduce_plan], before=lambda c: project(c) if c > 0 else None)
 
     base3 = i1 * p1 + i2 * p2
     o_ref[pl.ds(pl.multiple_of(base3 + i3 * p3, p3), p3), :] = lax.dot_general(
@@ -111,33 +124,41 @@
     ])
 
 
-def row_allreduce_times(x, t, n, collective_id, nc=2):
-    rows, cols = x.shape
+def row_allreduce_times(x, t, n, collective_id, nc=2, factors=None):
+    fused = factors is not None
+    if fused:
+        a, v = factors
+        rows, cols, dtype = a.shape[1], v.shape[1], jnp.float32
+        operands = (a, v, t)
+    else:
+        rows, cols = x.shape
+        dtype = x.dtype
+        operands = (x, t)
     groups = (2, min(4, n // 2), max(1, n // 8))
     g1, g2, g3 = groups
     p1 = rows // g1
     p2 = p1 // g2
     p3 = p2 // g3
     return pl.pallas_call(
-        functools.partial(_allreduce_kernel, groups, nc),
-        out_shape=jax.ShapeDtypeStruct((rows, cols), x.dtype),
-        in_specs=[pl.BlockSpec(memory_space=pltpu.VMEM)] * 2,
+        functools.partial(_allreduce_kernel, groups, nc, fused),
+        out_shape=jax.ShapeDtypeStruct((rows, cols), dtype),
+        in_specs=[pl.BlockSpec(memory_space=pltpu.VMEM)] * len(operands),
         out_specs=pl.BlockSpec(memory_space=pltpu.VMEM),
-        scratch_shapes=[
-            pltpu.VMEM((p1, cols), x.dtype),
-            pltpu.VMEM((p2, cols), x.dtype),
-            pltpu.VMEM((p3, cols), x.dtype),
-            pltpu.VMEM((g1, p1, cols), x.dtype),
-            pltpu.VMEM((g2, p2, cols), x.dtype),
-            pltpu.VMEM((g3, p3, cols), x.dtype),
+        scratch_shapes=([pltpu.VMEM((rows, cols), dtype)] if fused else []) + [
+            pltpu.VMEM((p1, cols), dtype),
+            pltpu.VMEM((p2, cols), dtype),
+            pltpu.VMEM((p3, cols), dtype),
+            pltpu.VMEM((g1, p1, cols), dtype),
+            pltpu.VMEM((g2, p2, cols), dtype),
+            pltpu.VMEM((g3, p3, cols), dtype),
             pltpu.SemaphoreType.DMA((6, nc, max(groups))),
             pltpu.SemaphoreType.DMA((6, nc, max(groups))),
         ],
         compiler_params=pltpu.CompilerParams(has_side_effects=True, collective_id=collective_id),
         cost_estimate=pl.CostEstimate(
-            flops=rows * cols, transcendentals=0, bytes_accessed=4 * rows * cols * 4
+            flops=rows * cols * (1 + (2 * a.shape[0] if fused else 0)), transcendentals=0, bytes_accessed=4 * rows * cols * 4
         ),
-    )(x, t)
+    )(*operands)
 
 
 def _col_gather_kernel(n, v_ref, e_ref, o_ref, s_ref, send_sems, recv_sems):
@@ -223,8 +244,10 @@
     vectors_first = lax.all_gather(panel_first, "col", axis=1, tiled=True)
     updated = eigen_vectors
     for collective_id, vectors, factor in ((1, vectors_second, factor_second), (2, vectors_first, factor_first)):
-        partial_t = partial_second if collective_id == 1 else lax.dot_general(updated, vectors, (((0,), (0,)), ((), ())), precision=lax.Precision.HIGH, preferred_element_type=jnp.float32)
-        applied_t = row_allreduce_times(partial_t, factor, n_row, collective_id)
+        if collective_id == 1:
+            applied_t = row_allreduce_times(partial_second, factor, n_row, collective_id)
+        else:
+            applied_t = row_allreduce_times(None, factor, n_row, collective_id, factors=(updated, vectors))
         updated = updated - lax.dot_general(vectors, applied_t, (((1,), (1,)), ((), ())), precision=lax.Precision.HIGH, preferred_element_type=jnp.float32)
     return updated
 

time: 131 us -> 129 us (0.985)
  matrix products: 13.8 us -> 10 us
  Pallas kernels: 103 us -> 105 us
    dot_general x1 -> x0, matrix products: 4.4 us -> none  [on_device(): lax.dot_general(updated, vectors, (((0,), (0,)), ((), ())), precision=lax...]
    pallas_call x2, Pallas kernels: 78.7 us -> 80.9 us  [row_allreduce_times(): pl.pallas_call(functools.partial(_allreduce_kernel, groups, nc, fused), o...]
  transfers between devices with their start and end apart: 1 -> 1, of which waited for: 0 -> 0; matrix products, arithmetic and copies ran while one was open for 3% -> 4% of each run, Pallas kernels for 33% -> 34%
where the time goes in v18:
time: 129 us
  Pallas kernels  105 us (81%)
  between operations  13.4 us (10%)
  matrix products  10 us (8%)
    pallas_call x2, Pallas kernels, row_allreduce_times(): pl.pallas_call(functools.partial(_allreduce_kernel, groups, nc, fused), o...  80.9 us
    pallas_call x1, Pallas kernels, col_gather(): pl.pallas_call(functools.partial(_col_gather_kernel, n), out_shape=(jax.S...  24.4 us
    dot_general x2, matrix products, on_device(): lax.dot_general(vectors, applied_t, (((1,), (1,)), ((), ())), precision=l...  10 us
  transfers between devices with their start and end apart: 1, of which 0 were waited for; matrix products, arithmetic and copies ran while one was open for 4% of the time, Pallas kernels for 34%

profile of v18, /device:TPU:1, one launch (start us, length us, event | category | flops | bytes accessed | tf_op | source)
XLA Modules:
  0.0 128.8 jit_solution(11799318751717377007)
XLA Ops:
  6.5 0.0 all-gather.2.cloned.1.call-start
  6.5 24.4 %shard_map.55 = (f32[1024,512]{1,0:T(8,128)}, f32[512,512]{1,0:T(8,128)}) custom-call(f32[1024,128]{1,0:T(8,128)} %v_ref.1, f32[1024,512]{1,0:T(8,128)} %e_ref.1), custom_call_target="tpu_custom_call" | custom-call | flops 536870912 | bytes 6291456 | tf_op jit(solution)/shard_map/pallas_call | solution.py:225
  31.0 0.0 copy-start.1
  31.0 0.0 all-gather.2.cloned.1.call-update
  31.0 43.6 %shard_map.56 = f32[512,512]{1,0:T(8,128)} custom-call(f32[512,512]{1,0:T(8,128)} %get-tuple-element.11.refs_0_, f32[512,512]{1,0:T(8,128)} %refs_1_.1), custom_call_target="tpu_custom_call" | custom-call | flops 262144 | bytes 4194304 | tf_op jit(solution)/shard_map/pallas_call | solution.py:142
  74.7 0.0 copy-done.1
  74.7 5.0 %convolution_subtract_fusion.1.refs_0_ = f32[1024,512]{1,0:T(8,128)} fusion(f32[1024,512]{1,0:T(8,128)S(1)} %copy-done.1, f32[1024,512]{1,0:T(8,128)} %get-tuple-element.10, f32[512,512]{1,0:T(8,128)} %shard_map.56), kind=kOutput, calls=%fused_computation.1 | convolution fusion | flops 1611137024 | bytes 7340032 | tf_op jit(solution)/shard_map/dot_general | solution.py:251
  79.7 0.0 copy-start
  79.7 0.0 all-gather.2.cloned.1.call-done.refs_1_
  79.7 37.2 %shard_map.57 = f32[512,512]{1,0:T(8,128)} custom-call(f32[1024,512]{1,0:T(8,128)} %convolution_subtract_fusion.1.refs_0_, f32[1024,512]{1,0:T(8,128)} %all-gather.2.cloned.1.call-done.refs_1_, f32[512,512]{1,0:T(8,128)} %refs_2_.1), custom_call_target="tpu_custom_call" | custom-call | flops 537133056 | bytes 4194304 | tf_op jit(solution)/shard_map/pallas_call | solution.py:142
  116.9 0.0 copy-done
  116.9 5.0 %convolution_subtract_fusion = f32[1024,512]{1,0:T(8,128)} fusion(f32[1024,512]{1,0:T(8,128)S(1)} %copy-done, f32[1024,512]{1,0:T(8,128)} %all-gather.2.cloned.1.call-done.refs_1_, f32[512,512]{1,0:T(8,128)} %shard_map.57), kind=kOutput, calls=%fused_computation | convolution fusion | flops 1611137024 | bytes 7340032 | tf_op jit(solution)/shard_map/dot_general | solution.py:251
Async XLA Ops:
  6.5 73.1 %all-gather.2.cloned.1.call-start = ((), (), s32[]{:S(2)}) async-start(), calls=%async_computation | async-start | bytes 2621440 | tf_op jit(solution)/shard_map/all_gather | solution.py:244
  31.0 43.7 %copy-start.1 = (f32[1024,512]{1,0:T(8,128)S(1)}, f32[1024,512]{1,0:T(8,128)}, u32[]{:S(2)}) copy-start(f32[1024,512]{1,0:T(8,128)} %e_ref.1) | copy-start | bytes 6291460
  79.7 37.2 %copy-start = (f32[1024,512]{1,0:T(8,128)S(1)}, f32[1024,512]{1,0:T(8,128)}, u32[]{:S(2)}) copy-start(f32[1024,512]{1,0:T(8,128)} %convolution_subtract_fusion.1.refs_0_) | copy-start | bytes 6291460
Sparse Core Ops, SparseCore 0:
  31.1 40.5 all-gather.1

commit v19 on v18

--- a/solution.py
+++ b/solution.py
@@ -14,7 +14,7 @@
 
 def _allreduce_kernel(groups, nc, fused, *refs):
     if fused:
-        a_ref, v_ref, t_ref, o_ref, x_ref, buf1, buf2, red, recv1, recv2, recv3, send_sems, recv_sems = refs
+        e_ref, u_ref, w_ref, v_ref, t_ref, o_ref, a_ref, x_ref, buf1, buf2, red, recv1, recv2, recv3, send_sems, recv_sems = refs
     else:
         x_ref, t_ref, o_ref, buf1, buf2, red, recv1, recv2, recv3, send_sems, recv_sems = refs
     me = lax.axis_index("row")
@@ -49,6 +49,10 @@
                 precision=lax.Precision.HIGH, preferred_element_type=jnp.float32,
             )
 
+    if fused:
+        a_ref[...] = e_ref[...] - lax.dot_general(
+            u_ref[...], w_ref[...], (((1,), (1,)), ((), ())), precision=lax.Precision.HIGH, preferred_element_type=jnp.float32
+        )
     project(0)
     pl.semaphore_wait(barrier, g1 + g2 + g3 - 3)
 
@@ -127,9 +131,10 @@
 def row_allreduce_times(x, t, n, collective_id, nc=2, factors=None):
     fused = factors is not None
     if fused:
-        a, v = factors
-        rows, cols, dtype = a.shape[1], v.shape[1], jnp.float32
-        operands = (a, v, t)
+        e, u, w, v = factors
+        a = e
+        rows, cols, dtype = e.shape[1], v.shape[1], jnp.float32
+        operands = (e, u, w, v, t)
     else:
         rows, cols = x.shape
         dtype = x.dtype
@@ -141,9 +146,9 @@
     p3 = p2 // g3
     return pl.pallas_call(
         functools.partial(_allreduce_kernel, groups, nc, fused),
-        out_shape=jax.ShapeDtypeStruct((rows, cols), dtype),
+        out_shape=(jax.ShapeDtypeStruct((rows, cols), dtype), jax.ShapeDtypeStruct(e.shape, dtype)) if fused else jax.ShapeDtypeStruct((rows, cols), dtype),
         in_specs=[pl.BlockSpec(memory_space=pltpu.VMEM)] * len(operands),
-        out_specs=pl.BlockSpec(memory_space=pltpu.VMEM),
+        out_specs=(pl.BlockSpec(memory_space=pltpu.VMEM),) * 2 if fused else pl.BlockSpec(memory_space=pltpu.VMEM),
         scratch_shapes=([pltpu.VMEM((rows, cols), dtype)] if fused else []) + [
             pltpu.VMEM((p1, cols), dtype),
             pltpu.VMEM((p2, cols), dtype),
@@ -242,13 +247,11 @@
     vectors_second, partial_second = col_gather(panel_second, eigen_vectors, n_col)
     vectors_second, panel_first = lax.optimization_barrier((vectors_second, panel_first))
     vectors_first = lax.all_gather(panel_first, "col", axis=1, tiled=True)
-    updated = eigen_vectors
-    for collective_id, vectors, factor in ((1, vectors_second, factor_second), (2, vectors_first, factor_first)):
-        if collective_id == 1:
-            applied_t = row_allreduce_times(partial_second, factor, n_row, collective_id)
-        else:
-            applied_t = row_allreduce_times(None, factor, n_row, collective_id, factors=(updated, vectors))
-        updated = updated - lax.dot_general(vectors, applied_t, (((1,), (1,)), ((), ())), precision=lax.Precision.HIGH, preferred_element_type=jnp.float32)
+    applied_second = row_allreduce_times(partial_second, factor_second, n_row, 1)
+    applied_first, updated = row_allreduce_times(
+        None, factor_first, n_row, 2, factors=(eigen_vectors, vectors_second, applied_second, vectors_first)
+    )
+    updated = updated - lax.dot_general(vectors_first, applied_first, (((1,), (1,)), ((), ())), precision=lax.Precision.HIGH, preferred_element_type=jnp.float32)
     return updated
 
 

time: 129 us -> 128 us (level)
  matrix products: 10 us -> 5.07 us
  Pallas kernels: 105 us -> 109 us
    dot_general x2 -> x1, matrix products: 10 us -> 5.07 us  [on_device(): lax.dot_general(vectors_first, applied_first, (((1,), (1,)), ((), ())), p...]
    pallas_call x2, Pallas kernels: 80.9 us -> 84.4 us  [row_allreduce_times(): pl.pallas_call(functools.partial(_allreduce_kernel, groups, nc, fused), o...]
  transfers between devices with their start and end apart: 1 -> 1, of which waited for: 0 -> 0; matrix products, arithmetic and copies ran while one was open for 4% -> 0% of each run, Pallas kernels for 34% -> 34%
where the time goes in v19:
time: 128 us; the launch traced here: 127 us
  Pallas kernels  109 us (85%)
  between operations  13.4 us (10%)
  matrix products  5.07 us (4%)
    pallas_call x2, Pallas kernels, row_allreduce_times(): pl.pallas_call(functools.partial(_allreduce_kernel, groups, nc, fused), o...  84.4 us
    pallas_call x1, Pallas kernels, col_gather(): pl.pallas_call(functools.partial(_col_gather_kernel, n), out_shape=(jax.S...  24.4 us
    dot_general x1, matrix products, on_device(): lax.dot_general(vectors_first, applied_first, (((1,), (1,)), ((), ())), p...  5.07 us
  transfers between devices with their start and end apart: 1, of which 0 were waited for; matrix products, arithmetic and copies ran while one was open for 0% of the time, Pallas kernels for 34%

profile of v19, /device:TPU:1, one launch (start us, length us, event | category | flops | bytes accessed | tf_op | source)
XLA Modules:
  0.0 127.4 jit_solution(7453328623143953719)
XLA Ops:
  6.5 0.0 all-gather.2.cloned.1.call-start
  6.5 24.4 %shard_map.55 = (f32[1024,512]{1,0:T(8,128)}, f32[512,512]{1,0:T(8,128)}) custom-call(f32[1024,128]{1,0:T(8,128)} %v_ref.1, f32[1024,512]{1,0:T(8,128)} %refs_0_.1), custom_call_target="tpu_custom_call" | custom-call | flops 536870912 | bytes 6291456 | tf_op jit(solution)/shard_map/pallas_call | solution.py:230
  31.0 0.0 all-gather.2.cloned.1.call-update
  31.0 43.5 %shard_map.56.refs_2_ = f32[512,512]{1,0:T(8,128)} custom-call(f32[512,512]{1,0:T(8,128)} %get-tuple-element.13.refs_0_, f32[512,512]{1,0:T(8,128)} %refs_1_.1), custom_call_target="tpu_custom_call" | custom-call | flops 262144 | bytes 4194304 | tf_op jit(solution)/shard_map/pallas_call | solution.py:147
  74.5 0.0 all-gather.2.cloned.1.call-done.refs_3_
  74.5 0.0 copy-start
  74.5 40.9 %shard_map.57 = (f32[512,512]{1,0:T(8,128)}, f32[1024,512]{1,0:T(8,128)}) custom-call(f32[1024,512]{1,0:T(8,128)} %refs_0_.1, f32[1024,512]{1,0:T(8,128)} %get-tuple-element.12.refs_1_, f32[512,512]{1,0:T(8,128)} %shard_map.56.refs_2_, f32[1024,512]{1,0:T(8,128)} %all-gather.2.cloned.1.call-done.refs_3_, f32[512,512]{1,0:T(8,128)} %refs_4_.1), custom_call_target="tpu_custom_call" | custom-call | flops 537133056 | bytes 4194304 | tf_op jit(solution)/shard_map/pallas_call | solution.py:147
  115.4 0.0 copy-done
  115.4 5.1 %convolution_subtract_fusion = f32[1024,512]{1,0:T(8,128)} fusion(f32[1024,512]{1,0:T(8,128)} %get-tuple-element.15, f32[1024,512]{1,0:T(8,128)S(1)} %copy-done, f32[512,512]{1,0:T(8,128)} %get-tuple-element.16), kind=kOutput, calls=%fused_computation | convolution fusion | flops 1611137024 | bytes 7340032 | tf_op jit(solution)/shard_map/dot_general | solution.py:254
Async XLA Ops:
  6.5 68.0 %all-gather.2.cloned.1.call-start = ((), (), s32[]{:S(2)}) async-start(), calls=%async_computation | async-start | bytes 2621440 | tf_op jit(solution)/shard_map/all_gather | solution.py:249
  74.5 40.9 %copy-start = (f32[1024,512]{1,0:T(8,128)S(1)}, f32[1024,512]{1,0:T(8,128)}, u32[]{:S(2)}) copy-start(f32[1024,512]{1,0:T(8,128)} %all-gather.2.cloned.1.call-done.refs_3_) | copy-start | bytes 6291460
Sparse Core Ops, SparseCore 0:
  31.1 40.5 all-gather.1

commit v20 on v19

--- a/solution.py
+++ b/solution.py
@@ -14,7 +14,7 @@
 
 def _allreduce_kernel(groups, nc, fused, *refs):
     if fused:
-        e_ref, u_ref, w_ref, v_ref, t_ref, o_ref, a_ref, x_ref, buf1, buf2, red, recv1, recv2, recv3, send_sems, recv_sems = refs
+        e_ref, u_ref, w_ref, v_ref, t_ref, out_ref, o_ref, a_ref, x_ref, buf1, buf2, red, recv1, recv2, recv3, send_sems, recv_sems = refs
     else:
         x_ref, t_ref, o_ref, buf1, buf2, red, recv1, recv2, recv3, send_sems, recv_sems = refs
     me = lax.axis_index("row")
@@ -100,11 +100,13 @@
 
         return start, combine
 
-    def run(plan, before=lambda c: None):
+    def run(plan, before=lambda c: None, last=lambda: None):
         for c in range(nc):
             before(c)
             plan[0](c)[0]()
         for k in range(len(plan)):
+            if k == len(plan) - 1:
+                last()
             for c in range(nc):
                 plan[k](c)[1]()
                 if k + 1 < len(plan):
@@ -121,11 +123,20 @@
         own = part(o_ref, base + mine * block, block, c)
         return exchange(stage, c, g, stride, mine, lambda j: own, lambda j, s: own)
 
+    def update(half):
+        if fused:
+            out_ref[:, pl.ds(pl.multiple_of(half * p1, p1), p1)] = a_ref[:, pl.ds(pl.multiple_of(half * p1, p1), p1)] - lax.dot_general(
+                v_ref[...], o_ref[pl.ds(pl.multiple_of(half * p1, p1), p1), :], (((1,), (1,)), ((), ())),
+                precision=lax.Precision.HIGH, preferred_element_type=jnp.float32,
+            )
+
     run([
         functools.partial(gather_stage, 3, g3, s3, i3, base3, p3),
         functools.partial(gather_stage, 4, g2, s2, i2, i1 * p1, p2),
         functools.partial(gather_stage, 5, g1, s1, i1, 0, p1),
-    ])
+    ], last=lambda: update(i1))
+    if g1 == 2:
+        update(1 - i1)
 
 
 def row_allreduce_times(x, t, n, collective_id, nc=2, factors=None):
@@ -146,10 +157,10 @@
     p3 = p2 // g3
     return pl.pallas_call(
         functools.partial(_allreduce_kernel, groups, nc, fused),
-        out_shape=(jax.ShapeDtypeStruct((rows, cols), dtype), jax.ShapeDtypeStruct(e.shape, dtype)) if fused else jax.ShapeDtypeStruct((rows, cols), dtype),
+        out_shape=jax.ShapeDtypeStruct(e.shape, dtype) if fused else jax.ShapeDtypeStruct((rows, cols), dtype),
         in_specs=[pl.BlockSpec(memory_space=pltpu.VMEM)] * len(operands),
-        out_specs=(pl.BlockSpec(memory_space=pltpu.VMEM),) * 2 if fused else pl.BlockSpec(memory_space=pltpu.VMEM),
-        scratch_shapes=([pltpu.VMEM((rows, cols), dtype)] if fused else []) + [
+        out_specs=pl.BlockSpec(memory_space=pltpu.VMEM),
+        scratch_shapes=([pltpu.VMEM((rows, cols), dtype), pltpu.VMEM(e.shape, dtype), pltpu.VMEM((rows, cols), dtype)] if fused else []) + [
             pltpu.VMEM((p1, cols), dtype),
             pltpu.VMEM((p2, cols), dtype),
             pltpu.VMEM((p3, cols), dtype),
@@ -248,10 +259,9 @@
     vectors_second, panel_first = lax.optimization_barrier((vectors_second, panel_first))
     vectors_first = lax.all_gather(panel_first, "col", axis=1, tiled=True)
     applied_second = row_allreduce_times(partial_second, factor_second, n_row, 1)
-    applied_first, updated = row_allreduce_times(
+    updated = row_allreduce_times(
         None, factor_first, n_row, 2, factors=(eigen_vectors, vectors_second, applied_second, vectors_first)
     )
-    updated = updated - lax.dot_general(vectors_first, applied_first, (((1,), (1,)), ((), ())), precision=lax.Precision.HIGH, preferred_element_type=jnp.float32)
     return updated
 
 

time: 128 us -> 127 us (level)
  matrix products: 5.07 us -> 0 us
  local copies, waits for them, and re-layouts: 0.01 us -> 3.08 us
    dot_general x1 -> x0, matrix products: 5.07 us -> none  [on_device(): lax.dot_general(vectors_first, applied_first, (((1,), (1,)), ((), ())), p...]
    unnamed x2 -> x1, local copies, waits for them, and re-layouts: 0.01 us -> 3.08 us
    pallas_call x2, Pallas kernels: 84.4 us -> 85.6 us  [row_allreduce_times(): pl.pallas_call(functools.partial(_allreduce_kernel, groups, nc, fused), o...]
where the time goes in v20:
time: 127 us
  Pallas kernels  110 us (87%)
  between operations  13.4 us (11%)
  local copies, waits for them, and re-layouts  3.08 us (2%)
    pallas_call x2, Pallas kernels, row_allreduce_times(): pl.pallas_call(functools.partial(_allreduce_kernel, groups, nc, fused), o...  85.6 us
    pallas_call x1, Pallas kernels, col_gather(): pl.pallas_call(functools.partial(_col_gather_kernel, n), out_shape=(jax.S...  24.4 us
    unnamed x1, local copies, waits for them, and re-layouts  3.08 us
  transfers between devices with their start and end apart: 1, of which 0 were waited for; matrix products, arithmetic and copies ran while one was open for 0% of the time, Pallas kernels for 34%

profile of v20, /device:TPU:1, one launch (start us, length us, event | category | flops | bytes accessed | tf_op | source)
XLA Modules:
  0.0 126.6 jit_solution(4044667154172578933)
XLA Ops:
  6.5 0.0 all-gather.2.cloned.1.call-start
  6.5 24.4 %shard_map.55 = (f32[1024,512]{1,0:T(8,128)}, f32[512,512]{1,0:T(8,128)}) custom-call(f32[1024,128]{1,0:T(8,128)} %v_ref.1, f32[1024,512]{1,0:T(8,128)} %refs_0_.1), custom_call_target="tpu_custom_call" | custom-call | flops 536870912 | bytes 6291456 | tf_op jit(solution)/shard_map/pallas_call | solution.py:241
  31.0 0.0 all-gather.2.cloned.1.call-update
  31.0 43.5 %shard_map.56.refs_2_ = f32[512,512]{1,0:T(8,128)} custom-call(f32[512,512]{1,0:T(8,128)} %get-tuple-element.11.refs_0_, f32[512,512]{1,0:T(8,128)} %refs_1_.1), custom_call_target="tpu_custom_call" | custom-call | flops 262144 | bytes 4194304 | tf_op jit(solution)/shard_map/pallas_call | solution.py:158
  74.5 0.0 all-gather.2.cloned.1.call-done.refs_3_
  74.5 42.1 %shard_map.57 = f32[1024,512]{1,0:T(8,128)} custom-call(f32[1024,512]{1,0:T(8,128)} %refs_0_.1, f32[1024,512]{1,0:T(8,128)} %get-tuple-element.10.refs_1_, f32[512,512]{1,0:T(8,128)} %shard_map.56.refs_2_, f32[1024,512]{1,0:T(8,128)} %all-gather.2.cloned.1.call-done.refs_3_, f32[512,512]{1,0:T(8,128)} %refs_4_.1), custom_call_target="tpu_custom_call" | custom-call | flops 537133056 | bytes 4194304 | tf_op jit(solution)/shard_map/pallas_call | solution.py:158
  116.7 3.1 %copy.7 = f32[1024,512]{1,0:T(8,128)} copy(f32[1024,512]{1,0:T(8,128)} %shard_map.57) | data formatting | bytes 4194304
Async XLA Ops:
  6.5 68.0 %all-gather.2.cloned.1.call-start = ((), (), s32[]{:S(2)}) async-start(), calls=%async_computation | async-start | bytes 2621440 | tf_op jit(solution)/shard_map/all_gather | solution.py:260
Sparse Core Ops, SparseCore 0:
  31.1 40.5 all-gather.1

commit v21 on v20

--- a/solution.py
+++ b/solution.py
@@ -100,7 +100,7 @@
 
         return start, combine
 
-    def run(plan, before=lambda c: None, last=lambda: None):
+    def run(plan, before=lambda c: None, last=lambda: None, after=lambda c: None):
         for c in range(nc):
             before(c)
             plan[0](c)[0]()
@@ -111,6 +111,8 @@
                 plan[k](c)[1]()
                 if k + 1 < len(plan):
                     plan[k + 1](c)[0]()
+                else:
+                    after(c)
 
     run([functools.partial(reduce_stage, *p) for p in reduce_plan], before=lambda c: project(c) if c > 0 else None)
 
@@ -130,13 +132,23 @@
                 precision=lax.Precision.HIGH, preferred_element_type=jnp.float32,
             )
 
+    def update_chunk(half, c):
+        if fused and g1 == 2:
+            cols_half = pl.ds(pl.multiple_of(half * p1, p1), p1)
+            term = lax.dot_general(
+                v_ref[:, pl.ds(c * cw, cw)], o_ref[cols_half, pl.ds(c * cw, cw)], (((1,), (1,)), ((), ())),
+                precision=lax.Precision.HIGH, preferred_element_type=jnp.float32,
+            )
+            if c == 0:
+                out_ref[:, cols_half] = a_ref[:, cols_half] - term
+            else:
+                out_ref[:, cols_half] -= term
+
     run([
         functools.partial(gather_stage, 3, g3, s3, i3, base3, p3),
         functools.partial(gather_stage, 4, g2, s2, i2, i1 * p1, p2),
         functools.partial(gather_stage, 5, g1, s1, i1, 0, p1),
-    ], last=lambda: update(i1))
-    if g1 == 2:
-        update(1 - i1)
+    ], last=lambda: update(i1), after=lambda c: update_chunk(1 - i1, c))
 
 
 def row_allreduce_times(x, t, n, collective_id, nc=2, factors=None):

time: 127 us -> 126 us (level)
  transfers between devices with their start and end apart: 1 -> 1, of which waited for: 0 -> 0; matrix products, arithmetic and copies ran while one was open for 0% -> 0% of each run, Pallas kernels for 34% -> 35%
where the time goes in v21:
time: 126 us
  Pallas kernels  109 us (87%)
  between operations  13.4 us (11%)
  local copies, waits for them, and re-layouts  3.08 us (2%)
    pallas_call x2, Pallas kernels, row_allreduce_times(): pl.pallas_call(functools.partial(_allreduce_kernel, groups, nc, fused), o...  84.7 us
    pallas_call x1, Pallas kernels, col_gather(): pl.pallas_call(functools.partial(_col_gather_kernel, n), out_shape=(jax.S...  24.4 us
    unnamed x1, local copies, waits for them, and re-layouts  3.08 us
  transfers between devices with their start and end apart: 1, of which 0 were waited for; matrix products, arithmetic and copies ran while one was open for 0% of the time, Pallas kernels for 35%

profile of v21, /device:TPU:1, one launch (start us, length us, event | category | flops | bytes accessed | tf_op | source)
XLA Modules:
  0.0 125.7 jit_solution(8840047565689397377)
XLA Ops:
  6.5 0.0 all-gather.2.cloned.1.call-start
  6.5 24.4 %shard_map.55 = (f32[1024,512]{1,0:T(8,128)}, f32[512,512]{1,0:T(8,128)}) custom-call(f32[1024,128]{1,0:T(8,128)} %v_ref.1, f32[1024,512]{1,0:T(8,128)} %refs_0_.1), custom_call_target="tpu_custom_call" | custom-call | flops 536870912 | bytes 6291456 | tf_op jit(solution)/shard_map/pallas_call | solution.py:253
  31.0 0.0 all-gather.2.cloned.1.call-update
  31.0 43.5 %shard_map.56.refs_2_ = f32[512,512]{1,0:T(8,128)} custom-call(f32[512,512]{1,0:T(8,128)} %get-tuple-element.11.refs_0_, f32[512,512]{1,0:T(8,128)} %refs_1_.1), custom_call_target="tpu_custom_call" | custom-call | flops 262144 | bytes 4194304 | tf_op jit(solution)/shard_map/pallas_call | solution.py:170
  74.5 0.0 all-gather.2.cloned.1.call-done.refs_3_
  74.5 41.2 %shard_map.57 = f32[1024,512]{1,0:T(8,128)} custom-call(f32[1024,512]{1,0:T(8,128)} %refs_0_.1, f32[1024,512]{1,0:T(8,128)} %get-tuple-element.10.refs_1_, f32[512,512]{1,0:T(8,128)} %shard_map.56.refs_2_, f32[1024,512]{1,0:T(8,128)} %all-gather.2.cloned.1.call-done.refs_3_, f32[512,512]{1,0:T(8,128)} %refs_4_.1), custom_call_target="tpu_custom_call" | custom-call | flops 537133056 | bytes 4194304 | tf_op jit(solution)/shard_map/pallas_call | solution.py:170
  115.7 3.1 %copy.7 = f32[1024,512]{1,0:T(8,128)} copy(f32[1024,512]{1,0:T(8,128)} %shard_map.57) | data formatting | bytes 4194304
Async XLA Ops:
  6.5 68.0 %all-gather.2.cloned.1.call-start = ((), (), s32[]{:S(2)}) async-start(), calls=%async_computation | async-start | bytes 2621440 | tf_op jit(solution)/shard_map/all_gather | solution.py:272
Sparse Core Ops, SparseCore 0:
  31.1 40.5 all-gather.1
